TPU v7x, 32 devices: a whole 2x2x4 slice. The times are simulated.
32 devices in a mesh: ray: 16 (over z, x, core), vox: 2 (over y).
Axes of the slice: x: 2, y: 2, z: 4, core: 2. Of those that a mesh axis runs over, the one named last changes fastest.
Arguments:
- tiles: bfloat16 [16, 2, 32, 128, 128], P('ray', 'vox'), may hold values from -0.1875 to 0.1875
- tile_scale: float32 [16, 2, 32], P('ray', 'vox'), may hold values from 0.25 to 4
- tile_row: int32 [16, 2, 32], P('ray', 'vox'), may hold values from 0 to 7
- tile_col: int32 [16, 2, 32], P('ray', 'vox'), may hold values from 0 to 1023
- tile_count: int32 [16, 2], P('ray', 'vox'), may hold values from 16 to 32, as said below
- delays: float32 [16384], P('ray'), may hold values from -6 to 6
- ray_receiver: int32 [16384], P('ray'), may hold values from 0 to 95
- receiver_weight: float32 [1536], P('ray'), may hold values from 0.5 to 2
- smooth_scale: float32 [64], replicated, may hold values from 0.05 to 0.5
Outputs:
- density: float32 [64, 2, 16, 128], P('ray', None, 'vox')
- rays_vec: float32 [16384], P('ray')
Inputs may be any that keep to these rules, and one draw needn't show every extreme that they name: `tile_count`: each ray group and voxel slab has between 16 and 32 live tile slots, and some has all 32 in every draw.
All inputs are finite; a program needn't handle non-finite values.
Results may differ from a plain program's by a relative error of at most 0.013.
Values sent between devices are 32-bit elements; how exact they have to be, the bound alone decides.
No kernel may reach another device: no remote copies, remote signals or barrier semaphores. Data moves between devices by JAX's collectives and lax.ppermute only.
A program may use at most 64 MiB of HBM per device.

v0:
```python
import jax
import jax.numpy as jnp
from jax import lax
from jax.sharding import PartitionSpec as P

ALT = 64
EPOCHS = 2
LAT = 128
LON_DEV = 8
RAY_TILE = 128
RT = 8
ITERS = 2


LATERAL = 1.0
VERTICAL = 4.0
TEMPORAL = 0.5


def with_halo(block, sides, width):
    for axis, dim in sides:
        count = lax.axis_size(axis)
        forward = [(i, i + 1) for i in range(count - 1)]
        backward = [(target, source) for source, target in forward]
        low = lax.ppermute(
            lax.slice_in_dim(block, block.shape[dim] - width, None, axis=dim), axis, forward
        )
        high = lax.ppermute(lax.slice_in_dim(block, 0, width, axis=dim), axis, backward)
        block = jnp.concatenate([low, block, high], axis=dim)
    return block


def stencil(padded, field):
    lateral = padded[1:-1, 1:-1, 2:, 1:-1] + padded[1:-1, 1:-1, :-2, 1:-1]
    lateral = lateral + padded[1:-1, 1:-1, 1:-1, 2:] + padded[1:-1, 1:-1, 1:-1, :-2]
    vertical = padded[2:, 1:-1, 1:-1, 1:-1] + padded[:-2, 1:-1, 1:-1, 1:-1]
    temporal = padded[1:-1, 2:, 1:-1, 1:-1] + padded[1:-1, :-2, 1:-1, 1:-1]
    centre = 2.0 * (2.0 * LATERAL + VERTICAL + TEMPORAL)
    return centre * field - LATERAL * lateral - VERTICAL * vertical - TEMPORAL * temporal


def laplace_local(field):
    padded = with_halo(field, (("vox", 2),), 1)
    padded = jnp.pad(padded, ((1, 1), (1, 1), (0, 0), (1, 1)))
    return stencil(padded, field)


def on_device(
    tiles,
    tile_scale,
    tile_row,
    tile_col,
    tile_count,
    delays,
    ray_receiver,
    receiver_weight,
    smooth_scale,
):
    block = tiles[0, 0]
    row_index = tile_row[0, 0]
    col_index = tile_col[0, 0]
    slots = block.shape[0]
    live = (jnp.arange(slots) < tile_count[0, 0]).astype(jnp.float32)
    effective = tile_scale[0, 0] * live
    table_size = receiver_weight.shape[0]
    matches = ray_receiver[:, None] == jnp.arange(table_size)[None, :]
    ray_weight = jnp.sum(jnp.where(matches, receiver_weight[None, :], 0.0), axis=1)
    damping = smooth_scale[:, None, None, None]
    lines_total = ALT * EPOCHS * LON_DEV
    share_rows = ALT // lax.axis_size("ray")
    offset = lax.axis_index("ray") * share_rows
    ray_onehot = (row_index[None, :] == jnp.arange(RT)[:, None]).astype(jnp.float32)

    def ray_total(values):
        return lax.psum(jnp.sum(values * values), "ray")

    def slab_total(values):
        return lax.psum(jnp.sum(values * values), "vox")

    def adjoint_lines(weighted):
        picked = jnp.take(weighted.reshape(RT, RAY_TILE), row_index, axis=0)
        return (
            jnp.einsum("ktl,kt->kl", block, picked, preferred_element_type=jnp.float32)
            * effective[:, None]
        )

    def pull_back(weighted):
        contrib = adjoint_lines(weighted)
        onehot = (col_index[None, :] == jnp.arange(lines_total)[:, None]).astype(jnp.float32)
        summed = jnp.dot(onehot, contrib, precision=lax.Precision.HIGHEST).reshape(
            ALT, EPOCHS, LON_DEV, LAT
        )
        return lax.psum(summed, "ray")

    def right_norm_of(values):
        return jnp.sqrt(slab_total(values))

    rays_vec = ray_weight * delays
    left_norm = jnp.sqrt(ray_total(rays_vec))
    rays_vec = rays_vec / left_norm
    smooth_vec = jnp.zeros((ALT, EPOCHS, LON_DEV, LAT), jnp.float32)
    right = pull_back((ray_weight * rays_vec).astype(jnp.bfloat16))
    right_norm = right_norm_of(right)
    right = right / right_norm
    search = right
    density = jnp.zeros_like(right)
    resid_bar = left_norm
    diag_bar = right_norm
    for iteration in range(ITERS):
        current = right
        smooth_vec = damping * laplace_local(current) - right_norm * smooth_vec
        lines = current.reshape(lines_total, LAT).astype(jnp.bfloat16)
        forward_picked = jnp.take(lines, col_index, axis=0)
        rays = (
            jnp.einsum("ktl,kl->kt", block, forward_picked, preferred_element_type=jnp.float32)
            * effective[:, None]
        )
        partial_value = jnp.dot(ray_onehot, rays, precision=lax.Precision.HIGHEST).reshape(-1)
        ray_sums = lax.psum(partial_value, "vox")
        smooth_sq = slab_total(smooth_vec)
        rays_vec = ray_weight * ray_sums - right_norm * rays_vec
        left_norm = jnp.sqrt(ray_total(rays_vec) + smooth_sq)
        rays_vec = rays_vec / left_norm
        smooth_vec = smooth_vec / left_norm
        smoothing = laplace_local(damping * smooth_vec)
        right = (
            pull_back((ray_weight * rays_vec).astype(jnp.bfloat16)) + smoothing - left_norm * right
        )
        right_norm = right_norm_of(right)
        right = right / right_norm
        diag_new = jnp.sqrt(diag_bar * diag_bar + left_norm * left_norm)
        cosine = diag_bar / diag_new
        sine_value = left_norm / diag_new
        coupling = sine_value * right_norm
        diag_bar = -cosine * right_norm
        step_size = cosine * resid_bar
        resid_bar = sine_value * resid_bar
        density = density + step_size / diag_new * search
        search = right - coupling / diag_new * search
    density_out = lax.dynamic_slice_in_dim(density, offset, share_rows, 0)
    return (density_out, rays_vec)


def solution(mesh):
    in_specs = (
        P("ray", "vox", None, None, None),
        P("ray", "vox", None),
        P("ray", "vox", None),
        P("ray", "vox", None),
        P("ray", "vox"),
        P("ray"),
        P("ray"),
        P("ray"),
        P(),
    )
    out_specs = (P("ray", None, "vox", None), P("ray"))
    return jax.shard_map(
        on_device, mesh=mesh, in_specs=in_specs, out_specs=out_specs, check_vma=False
    )
```

profile of v0, /device:TPU:0, one launch (start us, length us, event | category | flops | bytes accessed | tf_op | source)
XLA Modules:
  0.0 363.2 jit_solution(5082143402132900104)
XLA Ops:
  7.2 0.7 compare_select_fusion.1
  8.0 0.7 compare_and_fusion.1
  8.6 0.8 select_reduce_fusion
  9.5 1.3 multiply_reduce_fusion.5
  10.8 35.5 %psum.77 = f32[]{:T(128)} all-reduce(f32[]{:T(128)} %get-tuple-element.20), channel_id=1, replica_groups=mesh['ray'=16,'vox'=2] {'ray'}, use_global_device_ids=true, to_apply=%region_2.3 | all-reduce | flops 1 | bytes 8 | tf_op jit(solution)/shard_map/psum | solution.py:75
  47.6 0.6 gather_fusion
  48.3 0.4 fusion.11
  48.7 0.7 compare_select_fusion.2
  49.4 1.9 fusion.40
  51.3 0.7 compare_select_fusion
  52.0 0.7 compare_and_fusion
  52.7 86.1 %all-reduce.8.cloned.1.call-done = f32[64,2,8,128]{3,2,1,0:T(8,128)} async-done(((f32[64,2,8,128]{3,2,1,0:T(8,128)}), f32[64,2,8,128]{3,2,1,0:T(8,128)}) %all-reduce.8.cloned.1.call-update) | async-done | bytes 524304 | tf_op jit(solution)/shard_map/psum | solution.py:93
  138.7 1.8 multiply_reduce_fusion.2
  140.5 5.5 %psum.79 = f32[]{:T(128)} all-reduce(f32[]{:T(128)} %multiply_reduce_fusion.2), channel_id=1, replica_groups=mesh['ray'=16,'vox'=2] {'vox'}, use_global_device_ids=true, to_apply=%region_5.7 | all-reduce | flops 1 | bytes 8 | tf_op jit(solution)/shard_map/psum | solution.py:78
  146.7 1.1 fusion.64
  148.0 1.3 collective-permute-start
  149.3 4.5 %collective-permute-start.1 = (f32[64,2,1,128]{3,2,1,0:T(1,128)S(1)}, f32[64,2,1,128]{3,2,1,0:T(1,128)S(1)}, u32[]{:S(2)}, u32[]{:S(2)}) collective-permute-start(f32[64,2,1,128]{3,2,1,0:T(1,128)S(1)} %get-tuple-element.26), channel_id=1, source_target_pairs={{0,1},{2,3},{4,5},{6,7},{8,9},{10,11},{12,13},{14,15},{16,17},{18,... | collective-permute-start | bytes 196616 | tf_op jit(solution)/shard_map/ppermute | solution.py:25
  153.8 0.6 gather_fusion.1
  154.5 0.6 fusion.9
  155.1 0.2 convolution_bitcast_fusion.1
  155.3 0.4 collective-permute-done.1
  155.7 2.4 select_maximum_fusion.4
  158.1 1.5 multiply_reduce_fusion.1
  159.6 5.9 %all-reduce.4 = (f32[1024]{0:T(1024)S(1)}, f32[]{:T(128)}) all-reduce(f32[1024]{0:T(1024)S(1)} %convolution_bitcast_fusion.1, f32[]{:T(128)} %get-tuple-element.16), channel_id=1, replica_groups=mesh['ray'=16,'vox'=2] {'vox'}, use_global_device_ids=true, to_apply=%region_6.9 | all-reduce | flops 1025 | bytes 8200 | tf_op jit(solution)/shard_map/psum | solution.py:119
  165.6 0.6 multiply_reduce_fusion.4
  166.2 30.1 %psum.81 = f32[]{:T(128)} all-reduce(f32[]{:T(128)} %get-tuple-element.14), channel_id=1, replica_groups=mesh['ray'=16,'vox'=2] {'ray'}, use_global_device_ids=true, to_apply=%region_8.11 | all-reduce | flops 1 | bytes 8 | tf_op jit(solution)/shard_map/psum | solution.py:75
  197.8 1.3 collective-permute-start.2
  199.1 4.5 %collective-permute-start.3 = (f32[64,2,1,128]{3,2,1,0:T(1,128)S(1)}, f32[64,2,1,128]{3,2,1,0:T(1,128)S(1)}, u32[]{:S(2)}, u32[]{:S(2)}) collective-permute-start(f32[64,2,1,128]{3,2,1,0:T(1,128)S(1)} %get-tuple-element.24), channel_id=1, source_target_pairs={{0,1},{2,3},{4,5},{6,7},{8,9},{10,11},{12,13},{14,15},{16,17},{18,... | collective-permute-start | bytes 196616 | tf_op jit(solution)/shard_map/ppermute | solution.py:25
  203.7 0.6 gather_fusion.2
  204.4 0.4 fusion.7
  204.8 1.2 fusion.39
  206.2 3.7 %select_maximum_fusion.2 = f32[66,4,10,130]{3,2,1,0:T(8,128)} fusion(f32[64,2,1,128]{3,2,1,0:T(1,128)S(1)} %collective-permute-done.2, f32[64,2,8,128]{3,2,1,0:T(8,128)S(1)} %broadcast_multiply_fusion, f32[64,2,1,128]{3,2,1,0:T(1,128)S(1)} %collective-permute-done.3), kind=kLoop, calls=%fused_computation.12 | loop fusion | flops 7550400 | bytes 2028160 | tf_op jit(solution)/shard_map/concatenate | solution.py:29
  210.0 82.2 %all-reduce.10.cloned.1.call-done = f32[64,2,8,128]{3,2,1,0:T(8,128)} async-done(((f32[64,2,8,128]{3,2,1,0:T(8,128)}), f32[64,2,8,128]{3,2,1,0:T(8,128)}) %all-reduce.10.cloned.1.call-update) | async-done | bytes 524304 | tf_op jit(solution)/shard_map/psum | solution.py:93
  292.2 6.6 %multiply_reduce_fusion = (f32[]{:T(128)}, f32[64,2,8,128]{3,2,1,0:T(8,128)S(1)}) fusion(f32[64,2,8,128]{3,2,1,0:T(8,128)S(1)} %get-tuple-element.19, f32[]{:T(128)S(6)} %sqrt.23, f32[64,2,8,128]{3,2,1,0:T(8,128)} %all-reduce.10.cloned.1.call-done, f32[66,4,10,130]{3,2,1,0:T(8,128)} %select_maximum_fusion.2, ...), kind=kLoop, calls=%fused_computation.75 | loop fusion | flops 2359295 | bytes 5373960 | tf_op jit(solution)/shard_map/reduce_sum | solution.py:78
  298.9 5.5 %psum.84 = f32[]{:T(128)} all-reduce(f32[]{:T(128)} %get-tuple-element.12), channel_id=1, replica_groups=mesh['ray'=16,'vox'=2] {'vox'}, use_global_device_ids=true, to_apply=%region_13.16 | all-reduce | flops 1 | bytes 8 | tf_op jit(solution)/shard_map/psum | solution.py:78
  305.3 1.3 collective-permute-start.4
  306.6 4.5 %collective-permute-start.5 = (f32[64,2,1,128]{3,2,1,0:T(1,128)S(1)}, f32[64,2,1,128]{3,2,1,0:T(1,128)S(1)}, u32[]{:S(2)}, u32[]{:S(2)}) collective-permute-start(f32[64,2,1,128]{3,2,1,0:T(1,128)S(1)} %get-tuple-element.22), channel_id=1, source_target_pairs={{0,1},{2,3},{4,5},{6,7},{8,9},{10,11},{12,13},{14,15},{16,17},{18,... | collective-permute-start | bytes 196616 | tf_op jit(solution)/shard_map/ppermute | solution.py:25
  311.1 0.6 gather_fusion.3
  311.8 0.6 fusion.5
  312.5 0.2 convolution_bitcast_fusion
  312.7 0.3 collective-permute-done.5
  313.0 2.4 select_maximum_fusion
  315.4 1.6 fusion.18
  317.0 5.9 %all-reduce.3 = (f32[1024]{0:T(1024)S(1)}, f32[]{:T(128)}) all-reduce(f32[1024]{0:T(1024)S(1)} %convolution_bitcast_fusion, f32[]{:T(128)} %fusion.18), channel_id=1, replica_groups=mesh['ray'=16,'vox'=2] {'vox'}, use_global_device_ids=true, to_apply=%region_14.17 | all-reduce | flops 1025 | bytes 8200 | tf_op jit(solution)/shard_map/psum | solution.py:119
  322.9 0.6 multiply_reduce_fusion.3
  323.5 30.1 %psum.86 = f32[]{:T(128)} all-reduce(f32[]{:T(128)} %get-tuple-element.8), channel_id=1, replica_groups=mesh['ray'=16,'vox'=2] {'ray'}, use_global_device_ids=true, to_apply=%region_16.19 | all-reduce | flops 1 | bytes 8 | tf_op jit(solution)/shard_map/psum | solution.py:75
  355.0 0.6 broadcast_divide_fusion.3
  355.7 0.6 fusion.44
  (29 shorter events, 0.9 us)
Async XLA Ops:
  7.2 41.1 %copy-start = (bf16[1,1,32,128,128]{4,3,2,1,0:T(8,128)(2,1)S(1)}, bf16[1,1,32,128,128]{4,3,2,1,0:T(8,128)(2,1)}, u32[]{:S(2)}) copy-start(bf16[1,1,32,128,128]{4,3,2,1,0:T(8,128)(2,1)} %param.13) | copy-start | bytes 3145732
  7.2 148.0 %copy-start.3 = (s32[1,1,32]{2,1,0:T(1,128)S(1)}, s32[1,1,32]{2,1,0:T(1,128)}, u32[]{:S(2)}) copy-start(s32[1,1,32]{2,1,0:T(1,128)} %param.15) | copy-start | bytes 388
  7.2 131.5 %all-reduce.8.cloned.1.call-start = ((), (), s32[]{:S(2)}) async-start(), calls=%async_computation | async-start | bytes 1048576 | tf_op jit(solution)/shard_map/psum | solution.py:93
  51.3 106.8 %copy-start.1 = (f32[64]{0:T(128)S(1)}, f32[64]{0:T(128)}, u32[]{:S(2)}) copy-start(f32[64]{0:T(128)} %param.21) | copy-start | bytes 772
  51.3 240.9 %all-reduce.10.cloned.1.call-start = ((), (), s32[]{:S(2)}) async-start(), calls=%async_computation.1 | async-start | bytes 1048576 | tf_op jit(solution)/shard_map/psum | solution.py:93
  148.0 7.4 %collective-permute-start = (f32[64,2,1,128]{3,2,1,0:T(1,128)S(1)}, f32[64,2,1,128]{3,2,1,0:T(1,128)S(1)}, u32[]{:S(2)}, u32[]{:S(2)}) collective-permute-start(f32[64,2,1,128]{3,2,1,0:T(1,128)S(1)} %get-tuple-element.27), channel_id=1, source_target_pairs={{1,0},{3,2},{5,4},{7,6},{9,8},{11,10},{13,12},{15,14},{17,16},{19,... | collective-permute-start | bytes 196616 | tf_op jit(solution)/shard_map/ppermute | solution.py:28
  149.3 6.4 %collective-permute-start.1 = (f32[64,2,1,128]{3,2,1,0:T(1,128)S(1)}, f32[64,2,1,128]{3,2,1,0:T(1,128)S(1)}, u32[]{:S(2)}, u32[]{:S(2)}) collective-permute-start(f32[64,2,1,128]{3,2,1,0:T(1,128)S(1)} %get-tuple-element.26), channel_id=1, source_target_pairs={{0,1},{2,3},{4,5},{6,7},{8,9},{10,11},{12,13},{14,15},{16,17},{18,... | collective-permute-start | bytes 196616 | tf_op jit(solution)/shard_map/ppermute | solution.py:25
  158.1 46.7 %copy-start.2 = (s32[1,1,32]{2,1,0:T(1,128)S(1)}, s32[1,1,32]{2,1,0:T(1,128)}, u32[]{:S(2)}) copy-start(s32[1,1,32]{2,1,0:T(1,128)} %param.16) | copy-start | bytes 388
  197.8 8.4 %collective-permute-start.2 = (f32[64,2,1,128]{3,2,1,0:T(1,128)S(1)}, f32[64,2,1,128]{3,2,1,0:T(1,128)S(1)}, u32[]{:S(2)}, u32[]{:S(2)}) collective-permute-start(f32[64,2,1,128]{3,2,1,0:T(1,128)S(1)} %get-tuple-element.25), channel_id=1, source_target_pairs={{1,0},{3,2},{5,4},{7,6},{9,8},{11,10},{13,12},{15,14},{17,16},{19,... | collective-permute-start | bytes 196616 | tf_op jit(solution)/shard_map/ppermute | solution.py:28
  199.1 7.1 %collective-permute-start.3 = (f32[64,2,1,128]{3,2,1,0:T(1,128)S(1)}, f32[64,2,1,128]{3,2,1,0:T(1,128)S(1)}, u32[]{:S(2)}, u32[]{:S(2)}) collective-permute-start(f32[64,2,1,128]{3,2,1,0:T(1,128)S(1)} %get-tuple-element.24), channel_id=1, source_target_pairs={{0,1},{2,3},{4,5},{6,7},{8,9},{10,11},{12,13},{14,15},{16,17},{18,... | collective-permute-start | bytes 196616 | tf_op jit(solution)/shard_map/ppermute | solution.py:25
  305.3 7.4 %collective-permute-start.4 = (f32[64,2,1,128]{3,2,1,0:T(1,128)S(1)}, f32[64,2,1,128]{3,2,1,0:T(1,128)S(1)}, u32[]{:S(2)}, u32[]{:S(2)}) collective-permute-start(f32[64,2,1,128]{3,2,1,0:T(1,128)S(1)} %get-tuple-element.23), channel_id=1, source_target_pairs={{1,0},{3,2},{5,4},{7,6},{9,8},{11,10},{13,12},{15,14},{17,16},{19,... | collective-permute-start | bytes 196616 | tf_op jit(solution)/shard_map/ppermute | solution.py:28
  306.6 6.4 %collective-permute-start.5 = (f32[64,2,1,128]{3,2,1,0:T(1,128)S(1)}, f32[64,2,1,128]{3,2,1,0:T(1,128)S(1)}, u32[]{:S(2)}, u32[]{:S(2)}) collective-permute-start(f32[64,2,1,128]{3,2,1,0:T(1,128)S(1)} %get-tuple-element.22), channel_id=1, source_target_pairs={{0,1},{2,3},{4,5},{6,7},{8,9},{10,11},{12,13},{14,15},{16,17},{18,... | collective-permute-start | bytes 196616 | tf_op jit(solution)/shard_map/ppermute | solution.py:25
Sparse Core Ops, SparseCore 0:
  51.4 87.2 all-reduce.7
  206.3 85.8 all-reduce.9
where the time goes:
time: 364 us; the launch traced here: 363 us
  waiting for transfers between devices  169 us (46%)
  blocking collectives  119 us (33%)
  other arithmetic  29.7 us (8%)
  between operations  20 us (5%)
  starting transfers between devices  17.6 us (5%)
  matrix products  5.56 us (2%)
    psum x2, waiting for transfers between devices, pull_back(): return lax.psum(summed, 'ray')  168 us
    psum x3, blocking collectives, ray_total(): return lax.psum(jnp.sum(values * values), 'ray')  95.7 us
    ppermute x3, starting transfers between devices, with_halo(): lax.ppermute(lax.slice_in_dim(block, block.shape[dim] - width, None, axis...  13.6 us
    psum x2, blocking collectives, on_device(): ray_sums = lax.psum(partial_value, 'vox')  11.9 us
    reduce_sum x4, other arithmetic, slab_total(): return lax.psum(jnp.sum(values * values), 'vox')  11.6 us
    psum x2, blocking collectives, slab_total(): return lax.psum(jnp.sum(values * values), 'vox')  11.1 us
    concatenate x3, other arithmetic, with_halo(): block = jnp.concatenate([low, block, high], axis=dim)  8.48 us
  transfers between devices with their start and end apart: 8, of which 4 were waited for; matrix products, arithmetic and copies ran while one was open for 3% of the time, Pallas kernels for 0%

commit v1 on v0

v1 whole, which is shorter than its diff:
```python
import jax
import jax.numpy as jnp
from jax import lax
from jax.sharding import PartitionSpec as P

ALT = 64
EPOCHS = 2
LAT = 128
LON_DEV = 8
RAY_TILE = 128
RT = 8
LINES = ALT * EPOCHS * LON_DEV

LATERAL = 1.0
VERTICAL = 4.0
TEMPORAL = 0.5
CENTRE = 2.0 * (2.0 * LATERAL + VERTICAL + TEMPORAL)


def gather_rays(block, join_last=True):
    count = lax.axis_size("ray")
    if count & (count - 1):
        return lax.all_gather(block, "ray", tiled=True)
    step = count // 2
    while step:
        other = lax.ppermute(block, "ray", [(i, i ^ step) for i in range(count)])
        block = jnp.concatenate([block, other], axis=0)
        step //= 2
    return block


def ray_sum(value):
    count = lax.axis_size("ray")
    if count & (count - 1):
        return lax.psum(value, "ray")
    step = count // 2
    while step:
        value = value + lax.ppermute(value, "ray", [(i, i ^ step) for i in range(count)])
        step //= 2
    return value


def vox_sum(value):
    count = lax.axis_size("vox")
    if count == 1:
        return value
    if count == 2:
        return value + lax.ppermute(value, "vox", [(0, 1), (1, 0)])
    return lax.psum(value, "vox")


def halo_of(low_edge, high_edge):
    count = lax.axis_size("vox")
    if count == 1:
        return jnp.zeros_like(high_edge), jnp.zeros_like(low_edge)
    if count == 2:
        first = lax.axis_index("vox") == 0
        other = lax.ppermute(jnp.where(first, high_edge, low_edge), "vox", [(0, 1), (1, 0)])
        none = jnp.zeros_like(other)
        return jnp.where(first, none, other), jnp.where(first, other, none)
    forward = [(i, i + 1) for i in range(count - 1)]
    backward = [(target, source) for source, target in forward]
    return lax.ppermute(high_edge, "vox", forward), lax.ppermute(low_edge, "vox", backward)


def laplace(field):
    inner = field[:, :, 1:-1]
    padded = jnp.pad(field, ((1, 1), (1, 1), (0, 0), (1, 1)))
    lateral = padded[1:-1, 1:-1, 2:, 1:-1] + padded[1:-1, 1:-1, :-2, 1:-1]
    lateral = lateral + padded[1:-1, 1:-1, 1:-1, 2:] + padded[1:-1, 1:-1, 1:-1, :-2]
    vertical = padded[2:, 1:-1, 1:-1, 1:-1] + padded[:-2, 1:-1, 1:-1, 1:-1]
    temporal = padded[1:-1, 2:, 1:-1, 1:-1] + padded[1:-1, :-2, 1:-1, 1:-1]
    return CENTRE * inner - LATERAL * lateral - VERTICAL * vertical - TEMPORAL * temporal


def on_device(
    tiles,
    tile_scale,
    tile_row,
    tile_col,
    tile_count,
    delays,
    ray_receiver,
    receiver_weight,
    smooth_scale,
):
    block = tiles[0, 0]
    row_index = tile_row[0, 0]
    col_index = tile_col[0, 0]
    slots = block.shape[0]
    rays_n = lax.axis_size("ray")
    live = (jnp.arange(slots) < tile_count[0, 0]).astype(jnp.float32)
    effective = tile_scale[0, 0] * live
    table_size = receiver_weight.shape[0]
    matches = ray_receiver[:, None] == jnp.arange(table_size)[None, :]
    ray_weight = jnp.sum(jnp.where(matches, receiver_weight[None, :], 0.0), axis=1)
    ray_weight = ray_weight.reshape(RT, RAY_TILE)
    damping = smooth_scale[:, None, None, None]
    share_rows = ALT // rays_n
    offset = lax.axis_index("ray") * share_rows
    ray_onehot = (row_index[None, :] == jnp.arange(RT)[:, None]).astype(jnp.float32)
    vox_n = lax.axis_size("vox")
    vox_at = lax.axis_index("vox")
    places = jnp.arange(LON_DEV + 2)[None, None, :, None]
    inside = ((places > 0) | (vox_at > 0)) & ((places < LON_DEV + 1) | (vox_at < vox_n - 1))

    def adjoint_lines(weighted):
        picked = jnp.take(weighted.astype(jnp.bfloat16), row_index, axis=0)
        return (
            jnp.einsum("ktl,kt->kl", block, picked, preferred_element_type=jnp.float32)
            * effective[:, None]
        )

    def forward_share(field):
        lines = jnp.take(field.reshape(LINES, LAT), col_index, axis=0).astype(jnp.bfloat16)
        rays = (
            jnp.einsum("ktl,kl->kt", block, lines, preferred_element_type=jnp.float32)
            * effective[:, None]
        )
        return jnp.dot(ray_onehot, rays, precision=lax.Precision.HIGHEST)

    def row_of(value):
        return jnp.full((1, LAT), value, jnp.float32)

    def scatter(lines, onehot):
        high = lines.astype(jnp.bfloat16)
        low = (lines - high.astype(jnp.float32)).astype(jnp.bfloat16)
        both = jnp.dot(
            onehot, jnp.concatenate([high, low], axis=1), preferred_element_type=jnp.float32
        )
        return (both[:, :LAT] + both[:, LAT:]).reshape(ALT, EPOCHS, LON_DEV, LAT)

    u0 = ray_weight * delays.reshape(RT, RAY_TILE)
    contrib = adjoint_lines(ray_weight * u0)
    names = jnp.pad(col_index.astype(jnp.float32), (0, LAT - slots))[None, :]
    extra = jnp.concatenate([names, row_of(jnp.sum(u0 * u0)), jnp.zeros((6, LAT))], axis=0)
    seen = gather_rays(jnp.concatenate([contrib, extra], axis=0)).reshape(rays_n, slots + 8, LAT)
    cols = seen[:, slots, :slots].astype(jnp.int32).reshape(1, rays_n * slots)
    onehot = (cols == jnp.arange(LINES)[:, None]).astype(jnp.bfloat16)
    left_sq = jnp.sum(seen[:, slots + 1, 0])
    v0 = scatter(seen[:, :slots].reshape(rays_n * slots, LAT), onehot)

    share = forward_share(v0)
    summed = vox_sum(jnp.concatenate([share, jnp.full((8, LAT), jnp.sum(v0 * v0))], axis=0))
    v0_norm = jnp.sqrt(summed[8, 0])
    left0 = jnp.sqrt(left_sq)
    right0 = v0_norm / left0
    v0 = v0 / v0_norm
    r1 = ray_weight * summed[:8] / v0_norm - (right0 / left0) * u0
    contrib1 = adjoint_lines(ray_weight * r1)
    extra1 = jnp.concatenate([row_of(jnp.sum(r1 * r1)), jnp.zeros((7, LAT))], axis=0)
    low2, high2 = halo_of(v0[:, :, :2], v0[:, :, -2:])
    wide = jnp.concatenate([low2, v0, high2], axis=2)
    s1 = jnp.where(inside, damping * laplace(wide), 0.0)
    s1_sq = vox_sum(jnp.full((8, LAT), jnp.sum(s1[:, :, 1:-1] * s1[:, :, 1:-1])))[0, 0]
    smoothing = laplace(damping * s1)
    seen1 = gather_rays(jnp.concatenate([contrib1, extra1], axis=0))
    seen1 = seen1.reshape(rays_n, slots + 8, LAT)
    left1_sq = jnp.sum(seen1[:, slots, 0]) + s1_sq
    left1 = jnp.sqrt(left1_sq)
    pulled = scatter(seen1[:, :slots].reshape(rays_n * slots, LAT), onehot)
    v1 = (pulled + smoothing) / left1 - left1 * v0

    share1 = forward_share(v1)
    summed1 = vox_sum(jnp.concatenate([share1, jnp.full((8, LAT), jnp.sum(v1 * v1))], axis=0))
    right1 = jnp.sqrt(summed1[8, 0])
    low1, high1 = halo_of(v1[:, :, :1], v1[:, :, -1:])
    s2 = damping * laplace(jnp.concatenate([low1, v1, high1], axis=2)) / right1
    s2 = s2 - (right1 / left1) * s1[:, :, 1:-1]
    r2 = ray_weight * summed1[:8] / right1 - (right1 / left1) * r1
    s2_sq = vox_sum(jnp.full((8, LAT), jnp.sum(s2 * s2)))[0, 0]
    left2_sq = ray_sum(jnp.full((8, LAT), jnp.sum(r2 * r2)))[0, 0] + s2_sq
    left2 = jnp.sqrt(left2_sq)

    diag0 = right0
    diag1 = jnp.sqrt(diag0 * diag0 + left1_sq)
    cosine1, sine1 = diag0 / diag1, left1 / diag1
    coupling1 = sine1 * right1
    diag_bar = -cosine1 * right1
    step1 = cosine1 * left0
    resid1 = sine1 * left0
    diag2 = jnp.sqrt(diag_bar * diag_bar + left2_sq)
    step2 = diag_bar / diag2 * resid1
    mine0 = lax.dynamic_slice_in_dim(v0, offset, share_rows, 0)
    mine1 = lax.dynamic_slice_in_dim(v1, offset, share_rows, 0) / right1
    density = step1 / diag1 * mine0 + step2 / diag2 * (mine1 - coupling1 / diag1 * mine0)
    return (density, (r2 / left2).reshape(-1))


def solution(mesh):
    in_specs = (
        P("ray", "vox", None, None, None),
        P("ray", "vox", None),
        P("ray", "vox", None),
        P("ray", "vox", None),
        P("ray", "vox"),
        P("ray"),
        P("ray"),
        P("ray"),
        P(),
    )
    out_specs = (P("ray", None, "vox", None), P("ray"))
    return jax.shard_map(
        on_device, mesh=mesh, in_specs=in_specs, out_specs=out_specs, check_vma=False
    )
```

time: 364 us -> 96.5 us (0.27)
  waiting for transfers between devices: 169 us -> 20.5 us
  blocking collectives: 119 us -> 0 us
  between operations: 20 us -> 6.88 us
  starting transfers between devices: 17.6 us -> 29.3 us
  local copies, waits for them, and re-layouts: 2.65 us -> 10.9 us
  other arithmetic: 29.7 us -> 25.1 us
    psum x2 -> x0, waiting for transfers between devices: 168 us -> none  [pull_back(): return lax.psum(summed, 'ray')]
    psum x7 -> x0, blocking collectives: 119 us -> none  [the longest x3 95.7 us: ray_total(): return lax.psum(jnp.sum(values * values), 'ray')]
    ppermute x6 -> x18, waiting for transfers between devices: 0.69 us -> 20.5 us  [the longest x8 8.69 us: gather_rays(): other = lax.ppermute(block, 'ray', [(i, i ^ step) for i in range(count)])]
    ppermute x6 -> x18, starting transfers between devices: 17.5 us -> 29.3 us  [the longest x8 15 us: gather_rays(): other = lax.ppermute(block, 'ray', [(i, i ^ step) for i in range(count)])]
    concatenate x3 -> x5, other arithmetic: 8.48 us -> 2.64 us  [the longest x1 2.4 us: on_device(): s2 = damping * laplace(jnp.concatenate([low1, v1, high1], axis=2)) / right1]
    reduce_sum x7 -> x9, other arithmetic: 14.1 us -> 8.88 us  [the longest x1 2.19 us: on_device(): jnp.sum(v1 * v1)]
    add x1 -> x10, other arithmetic: 0.63 us -> 5.39 us  [the longest x4 2.59 us: vox_sum(): return value + lax.ppermute(value, 'vox', [(0, 1), (1, 0)])]
  transfers between devices with their start and end apart: 8 -> 18, of which waited for: 4 -> 13; matrix products, arithmetic and copies ran while one was open for 3% -> 12% of each run, Pallas kernels for 0% -> 0%
where the time goes in v1:
time: 96.5 us; the launch traced here: 96 us
  starting transfers between devices  29.3 us (30%)
  other arithmetic  25.1 us (26%)
  waiting for transfers between devices  20.5 us (21%)
  local copies, waits for them, and re-layouts  10.9 us (11%)
  between operations  6.88 us (7%)
  matrix products  3.38 us (4%)
    ppermute x8, starting transfers between devices, gather_rays(): other = lax.ppermute(block, 'ray', [(i, i ^ step) for i in range(count)])  15 us
    ppermute x8, waiting for transfers between devices, gather_rays(): other = lax.ppermute(block, 'ray', [(i, i ^ step) for i in range(count)])  8.69 us
    ppermute x4, starting transfers between devices, vox_sum(): return value + lax.ppermute(value, 'vox', [(0, 1), (1, 0)])  6.75 us
    ppermute x4, waiting for transfers between devices, ray_sum(): lax.ppermute(value, 'ray', [(i, i ^ step) for i in range(count)])  5.96 us
    ppermute x4, waiting for transfers between devices, vox_sum(): return value + lax.ppermute(value, 'vox', [(0, 1), (1, 0)])  5.81 us
    ppermute x4, starting transfers between devices, ray_sum(): lax.ppermute(value, 'ray', [(i, i ^ step) for i in range(count)])  4.31 us
    ppermute x2, starting transfers between devices, halo_of(): lax.ppermute(jnp.where(first, high_edge, low_edge), 'vox', [(0, 1), (1, 0)])  3.17 us
    add x4, other arithmetic, vox_sum(): return value + lax.ppermute(value, 'vox', [(0, 1), (1, 0)])  2.59 us
  transfers between devices with their start and end apart: 18, of which 13 were waited for; matrix products, arithmetic and copies ran while one was open for 12% of the time, Pallas kernels for 0%

profile of v1, /device:TPU:0, one launch (start us, length us, event | category | flops | bytes accessed | tf_op | source)
XLA Modules:
  0.0 96.0 jit_solution(15632978321119254266)
XLA Ops:
  0.7 0.7 compare_and_fusion.1
  1.4 0.7 compare_select_fusion.1
  2.1 0.8 select_reduce_fusion
  2.9 1.3 %multiply_reduce_fusion.5 = f32[]{:T(128)} fusion(f32[1024]{0:T(1024)S(1)} %select_reduce_fusion, f32[1024]{0:T(1024)} %param.18), kind=kLoop, calls=%fused_computation.156 | loop fusion | flops 3071 | bytes 8196 | tf_op jit(solution)/shard_map/reduce_sum | solution.py:136
  4.2 0.7 fusion.76
  5.5 0.7 bitcast_convert_fusion.2
  6.2 0.7 compare_select_fusion.2
  8.0 0.7 broadcast_in_dim.88
  8.7 4.1 %collective-permute-start = (f32[40,128]{1,0:T(8,128)S(1)}, f32[40,128]{1,0:T(8,128)S(1)}, u32[]{:S(2)}, u32[]{:S(2)}) collective-permute-start(f32[40,128]{1,0:T(8,128)S(1)} %pad_maximum_fusion.4), channel_id=1, source_target_pairs={{0,16},{2,18},{4,20},{6,22},{8,24},{10,26},{12,28},{14,30},{16,0},... | collective-permute-start | bytes 61448 | tf_op jit(solution)/shard_map/ppermute | solution.py:26
  12.8 1.8 %collective-permute-done = f32[40,128]{1,0:T(8,128)S(1)} collective-permute-done((f32[40,128]{1,0:T(8,128)S(1)}, f32[40,128]{1,0:T(8,128)S(1)}, u32[]{:S(2)}, u32[]{:S(2)}) %collective-permute-start) | collective-permute-done | bytes 20512 | tf_op jit(solution)/shard_map/ppermute | solution.py:26
  14.6 2.0 %collective-permute-start.1 = (f32[80,128]{1,0:T(8,128)S(1)}, f32[80,128]{1,0:T(8,128)S(1)}, u32[]{:S(2)}, u32[]{:S(2)}) collective-permute-start(f32[80,128]{1,0:T(8,128)S(1)} %concatenate.69), channel_id=1, source_target_pairs={{0,8},{2,10},{4,12},{6,14},{8,0},{10,2},{12,4},{14,6},{16,24},{18,... | collective-permute-start | bytes 122888 | tf_op jit(solution)/shard_map/ppermute | solution.py:26
  16.5 2.1 %collective-permute-done.1 = f32[80,128]{1,0:T(8,128)S(1)} collective-permute-done((f32[80,128]{1,0:T(8,128)S(1)}, f32[80,128]{1,0:T(8,128)S(1)}, u32[]{:S(2)}, u32[]{:S(2)}) %collective-permute-start.1) | collective-permute-done | bytes 40992 | tf_op jit(solution)/shard_map/ppermute | solution.py:26
  18.7 2.0 %collective-permute-start.2 = (f32[160,128]{1,0:T(8,128)S(1)}, f32[160,128]{1,0:T(8,128)S(1)}, u32[]{:S(2)}, u32[]{:S(2)}) collective-permute-start(f32[160,128]{1,0:T(8,128)S(1)} %concatenate.70), channel_id=1, source_target_pairs={{0,4},{2,6},{4,0},{6,2},{8,12},{10,14},{12,8},{14,10},{16,20},{18,... | collective-permute-start | bytes 245768 | tf_op jit(solution)/shard_map/ppermute | solution.py:26
  20.6 0.7 compare_and_fusion
  21.3 1.9 %collective-permute-done.2 = f32[160,128]{1,0:T(8,128)S(1)} collective-permute-done((f32[160,128]{1,0:T(8,128)S(1)}, f32[160,128]{1,0:T(8,128)S(1)}, u32[]{:S(2)}, u32[]{:S(2)}) %collective-permute-start.2) | collective-permute-done | bytes 81952 | tf_op jit(solution)/shard_map/ppermute | solution.py:26
  23.3 0.7 compare_select_fusion
  23.9 0.7 collective-permute-done.3
  25.3 0.7 multiply_reduce_fusion.2
  27.6 0.7 concatenate.74
  28.2 2.0 %collective-permute-start.4 = (f32[16,128]{1,0:T(8,128)S(1)}, f32[16,128]{1,0:T(8,128)S(1)}, u32[]{:S(2)}, u32[]{:S(2)}) collective-permute-start(f32[16,128]{1,0:T(8,128)S(1)} %concatenate.74), channel_id=1, source_target_pairs={{0,1},{1,0},{2,3},{3,2},{4,5},{5,4},{6,7},{7,6},{8,9},{9,8},{10,11... | collective-permute-start | bytes 24584 | tf_op jit(solution)/shard_map/ppermute | solution.py:48
  32.0 0.6 pad_add_fusion.1
  35.7 0.7 broadcast_in_dim.90
  36.4 3.0 %collective-permute-start.5 = (f32[40,128]{1,0:T(8,128)S(1)}, f32[40,128]{1,0:T(8,128)S(1)}, u32[]{:S(2)}, u32[]{:S(2)}) collective-permute-start(f32[40,128]{1,0:T(8,128)S(1)} %pad_maximum_fusion.5), channel_id=1, source_target_pairs={{0,16},{2,18},{4,20},{6,22},{8,24},{10,26},{12,28},{14,30},{16,0},... | collective-permute-start | bytes 61448 | tf_op jit(solution)/shard_map/ppermute | solution.py:26
  39.4 1.6 %collective-permute-start.9 = (f32[64,2,2,128]{3,2,1,0:T(2,128)S(1)}, f32[64,2,2,128]{3,2,1,0:T(2,128)S(1)}, u32[]{:S(2)}, u32[]{:S(2)}) collective-permute-start(f32[64,2,2,128]{3,2,1,0:T(2,128)S(1)} %slice_select_fusion), channel_id=1, source_target_pairs={{0,1},{1,0},{2,3},{3,2},{4,5},{5,4},{6,7},{7,6},{8,9},{9,8},{10,11... | collective-permute-start | bytes 393224 | tf_op jit(solution)/shard_map/ppermute | solution.py:58
  41.1 2.0 %collective-permute-start.6 = (f32[80,128]{1,0:T(8,128)S(1)}, f32[80,128]{1,0:T(8,128)S(1)}, u32[]{:S(2)}, u32[]{:S(2)}) collective-permute-start(f32[80,128]{1,0:T(8,128)S(1)} %pad_maximum_fusion.3), channel_id=1, source_target_pairs={{0,8},{2,10},{4,12},{6,14},{8,0},{10,2},{12,4},{14,6},{16,24},{18,... | collective-permute-start | bytes 122888 | tf_op jit(solution)/shard_map/ppermute | solution.py:26
  43.1 2.1 %collective-permute-done.6 = f32[80,128]{1,0:T(8,128)S(1)} collective-permute-done((f32[80,128]{1,0:T(8,128)S(1)}, f32[80,128]{1,0:T(8,128)S(1)}, u32[]{:S(2)}, u32[]{:S(2)}) %collective-permute-start.6) | collective-permute-done | bytes 40992 | tf_op jit(solution)/shard_map/ppermute | solution.py:26
  45.2 2.0 %collective-permute-start.7 = (f32[160,128]{1,0:T(8,128)S(1)}, f32[160,128]{1,0:T(8,128)S(1)}, u32[]{:S(2)}, u32[]{:S(2)}) collective-permute-start(f32[160,128]{1,0:T(8,128)S(1)} %concatenate.77), channel_id=1, source_target_pairs={{0,4},{2,6},{4,0},{6,2},{8,12},{10,14},{12,8},{14,10},{16,20},{18,... | collective-permute-start | bytes 245768 | tf_op jit(solution)/shard_map/ppermute | solution.py:26
  47.5 1.1 %broadcast_multiply_fusion = (f32[64,2,10,128]{3,2,1,0:T(8,128)S(1)}, f32[64,2,10,128]{3,2,1,0:T(8,128)S(1)}) fusion(f32[64]{0:T(128)S(1)} %copy-done.4, f32[64,2,12,128]{3,2,1,0:T(8,128)S(1)} %pad_maximum_fusion, f32[64,2,8,128]{3,2,1,0:T(8,128)S(1)} %bitcast.88, f32[64,2,2,128]{3,2,1,0:T(2,128)S(1)} %get-tuple-element.18, ...), kind=kLoop, calls=%fused_computation.90 | loop fusion | flops 2621440 | bytes 4195328 | tf_op jit(solution)/shard_map/mul | solution.py:156
  48.6 1.0 %copy-done.1 = f32[64,2,10,128]{3,2,1,0:T(8,128)} copy-done((f32[64,2,10,128]{3,2,1,0:T(8,128)}, f32[64,2,10,128]{3,2,1,0:T(8,128)S(1)}, u32[]{:S(2)}) %copy-start.1) | copy-done | bytes 655384
  49.6 0.7 multiply_reduce_fusion.1
  51.0 1.6 %collective-permute-start.10 = (f32[8,128]{1,0:T(8,128)S(1)}, f32[8,128]{1,0:T(8,128)S(1)}, u32[]{:S(2)}, u32[]{:S(2)}) collective-permute-start(f32[8,128]{1,0:T(8,128)S(1)} %broadcast_in_dim.95), channel_id=1, source_target_pairs={{0,1},{1,0},{2,3},{3,2},{4,5},{5,4},{6,7},{7,6},{8,9},{9,8},{10,11... | collective-permute-start | bytes 12296 | tf_op jit(solution)/shard_map/ppermute | solution.py:48
  52.7 2.0 %collective-permute-done.10 = f32[8,128]{1,0:T(8,128)S(1)} collective-permute-done((f32[8,128]{1,0:T(8,128)S(1)}, f32[8,128]{1,0:T(8,128)S(1)}, u32[]{:S(2)}, u32[]{:S(2)}) %collective-permute-start.10) | collective-permute-done | bytes 4128 | tf_op jit(solution)/shard_map/ppermute | solution.py:48
  57.1 0.9 slice_add_fusion.5
  59.3 2.2 %multiply_reduce_fusion = (f32[]{:T(128)}, f32[64,2,8,128]{3,2,1,0:T(8,128)S(1)}) fusion(f32[64,2,8,128]{3,2,1,0:T(8,128)S(1)} %bitcast.89, f32[]{:T(128)S(6)} %sqrt.31, f32[64,2,8,128]{3,2,1,0:T(8,128)} %bitcast.92, f32[64,2,10,128]{3,2,1,0:T(8,128)S(1)} %get-tuple-element.8), kind=kLoop, calls=%fused_computation.88 | loop fusion | flops 2228223 | bytes 4194312 | tf_op jit(solution)/shard_map/reduce_sum | solution.py:165
  63.0 0.7 concatenate.84
  63.7 1.6 %collective-permute-start.11 = (f32[16,128]{1,0:T(8,128)S(1)}, f32[16,128]{1,0:T(8,128)S(1)}, u32[]{:S(2)}, u32[]{:S(2)}) collective-permute-start(f32[16,128]{1,0:T(8,128)S(1)} %concatenate.84), channel_id=1, source_target_pairs={{0,1},{1,0},{2,3},{3,2},{4,5},{5,4},{6,7},{7,6},{8,9},{9,8},{10,11... | collective-permute-start | bytes 24584 | tf_op jit(solution)/shard_map/ppermute | solution.py:48
  65.3 2.1 %collective-permute-done.11 = f32[16,128]{1,0:T(8,128)S(1)} collective-permute-done((f32[16,128]{1,0:T(8,128)S(1)}, f32[16,128]{1,0:T(8,128)S(1)}, u32[]{:S(2)}, u32[]{:S(2)}) %collective-permute-start.11) | collective-permute-done | bytes 8224 | tf_op jit(solution)/shard_map/ppermute | solution.py:48
  67.4 0.6 pad_add_fusion
  70.6 2.6 %collective-permute-start.12 = (f32[8,128]{1,0:T(8,128)S(1)}, f32[8,128]{1,0:T(8,128)S(1)}, u32[]{:S(2)}, u32[]{:S(2)}) collective-permute-start(f32[8,128]{1,0:T(8,128)S(1)} %broadcast_in_dim.96), channel_id=1, source_target_pairs={{0,16},{2,18},{4,20},{6,22},{8,24},{10,26},{12,28},{14,30},{16,0},... | collective-permute-start | bytes 12296 | tf_op jit(solution)/shard_map/ppermute | solution.py:38
  73.1 2.0 %collective-permute-done.12 = f32[8,128]{1,0:T(8,128)S(1)} collective-permute-done((f32[8,128]{1,0:T(8,128)S(1)}, f32[8,128]{1,0:T(8,128)S(1)}, u32[]{:S(2)}, u32[]{:S(2)}) %collective-permute-start.12) | collective-permute-done | bytes 4128 | tf_op jit(solution)/shard_map/ppermute | solution.py:38
  75.8 1.5 %collective-permute-start.13 = (f32[8,128]{1,0:T(8,128)S(1)}, f32[8,128]{1,0:T(8,128)S(1)}, u32[]{:S(2)}, u32[]{:S(2)}) collective-permute-start(f32[8,128]{1,0:T(8,128)S(1)} %broadcast_add_fusion.1), channel_id=1, source_target_pairs={{0,8},{2,10},{4,12},{6,14},{8,0},{10,2},{12,4},{14,6},{16,24},{18,... | collective-permute-start | bytes 12296 | tf_op jit(solution)/shard_map/ppermute | solution.py:38
  77.4 1.6 %collective-permute-start.16 = (f32[64,2,1,128]{3,2,1,0:T(1,128)S(1)}, f32[64,2,1,128]{3,2,1,0:T(1,128)S(1)}, u32[]{:S(2)}, u32[]{:S(2)}) collective-permute-start(f32[64,2,1,128]{3,2,1,0:T(1,128)S(1)} %broadcast_select_fusion.2), channel_id=1, source_target_pairs={{0,1},{1,0},{2,3},{3,2},{4,5},{5,4},{6,7},{7,6},{8,9},{9,8},{10,11... | collective-permute-start | bytes 196616 | tf_op jit(solution)/shard_map/ppermute | solution.py:58
  79.5 0.6 fusion.86
  80.3 3.5 %collective-permute-done.14 = f32[8,128]{1,0:T(8,128)S(1)} collective-permute-done((f32[8,128]{1,0:T(8,128)S(1)}, f32[8,128]{1,0:T(8,128)S(1)}, u32[]{:S(2)}, u32[]{:S(2)}) %collective-permute-start.14) | collective-permute-done | bytes 4128 | tf_op jit(solution)/shard_map/ppermute | solution.py:38
  83.9 2.4 %select_maximum_fusion = f32[66,4,10,130]{3,2,1,0:T(8,128)S(1)} fusion(f32[64,2,1,128]{3,2,1,0:T(1,128)S(1)} %get-tuple-element.21, f32[64,2,8,128]{3,2,1,0:T(8,128)S(1)} %get-tuple-element.7, f32[64,2,1,128]{3,2,1,0:T(1,128)S(1)} %get-tuple-element.20), kind=kLoop, calls=%fused_computation.22 | loop fusion | flops 7550400 | bytes 2028160 | tf_op jit(solution)/shard_map/concatenate | solution.py:168
  86.3 1.5 %fusion.50 = f32[]{:T(128)} fusion(f32[66,4,10,130]{3,2,1,0:T(8,128)S(1)} %select_maximum_fusion, f32[64,2,8,128]{3,2,1,0:T(8,128)S(1)} %get-tuple-element.7, f32[64,2,1,128]{3,2,1,0:T(1,128)S(1)} %get-tuple-element.20, f32[64,2,1,128]{3,2,1,0:T(1,128)S(1)} %get-tuple-element.21, f32[64,2,10,128]{3,2,1,0:T(8,128)S(1)} %copy-done.2, f32[]{:T(128)S(6)} %div.86, ...), kind=kLoop, calls=%fused_computation.92 | loop fusion | flops 2490367 | bytes 4325644 | tf_op jit(solution)/shard_map/reduce_sum | solution.py:171
  88.4 1.6 %collective-permute-start.17 = (f32[8,128]{1,0:T(8,128)S(1)}, f32[8,128]{1,0:T(8,128)S(1)}, u32[]{:S(2)}, u32[]{:S(2)}) collective-permute-start(f32[8,128]{1,0:T(8,128)S(1)} %broadcast_in_dim.98), channel_id=1, source_target_pairs={{0,1},{1,0},{2,3},{3,2},{4,5},{5,4},{6,7},{7,6},{8,9},{9,8},{10,11... | collective-permute-start | bytes 12296 | tf_op jit(solution)/shard_map/ppermute | solution.py:48
  90.8 1.3 %collective-permute-done.17 = f32[8,128]{1,0:T(8,128)S(1)} collective-permute-done((f32[8,128]{1,0:T(8,128)S(1)}, f32[8,128]{1,0:T(8,128)S(1)}, u32[]{:S(2)}, u32[]{:S(2)}) %collective-permute-start.17) | collective-permute-done | bytes 4128 | tf_op jit(solution)/shard_map/ppermute | solution.py:48
  (89 shorter events, 18.8 us)
Async XLA Ops:
  0.6 6.9 %copy-start = (bf16[1,1,32,128,128]{4,3,2,1,0:T(8,128)(2,1)S(1)}, bf16[1,1,32,128,128]{4,3,2,1,0:T(8,128)(2,1)}, u32[]{:S(2)}) copy-start(bf16[1,1,32,128,128]{4,3,2,1,0:T(8,128)(2,1)} %param.13) | copy-start | bytes 3145732
  0.6 26.7 %copy-start.5 = (s32[1,1,32]{2,1,0:T(1,128)S(1)}, s32[1,1,32]{2,1,0:T(1,128)}, u32[]{:S(2)}) copy-start(s32[1,1,32]{2,1,0:T(1,128)} %param.15) | copy-start | bytes 388
  7.5 26.4 %copy-start.3 = (f32[1024]{0:T(1024)S(1)}, f32[1024]{0:T(1024)}, u32[]{:S(2)}) copy-start(f32[1024]{0:T(1024)} %param.18) | copy-start | bytes 12292
  8.7 5.9 %collective-permute-start = (f32[40,128]{1,0:T(8,128)S(1)}, f32[40,128]{1,0:T(8,128)S(1)}, u32[]{:S(2)}, u32[]{:S(2)}) collective-permute-start(f32[40,128]{1,0:T(8,128)S(1)} %pad_maximum_fusion.4), channel_id=1, source_target_pairs={{0,16},{2,18},{4,20},{6,22},{8,24},{10,26},{12,28},{14,30},{16,0},... | collective-permute-start | bytes 61448 | tf_op jit(solution)/shard_map/ppermute | solution.py:26
  14.6 4.1 %collective-permute-start.1 = (f32[80,128]{1,0:T(8,128)S(1)}, f32[80,128]{1,0:T(8,128)S(1)}, u32[]{:S(2)}, u32[]{:S(2)}) collective-permute-start(f32[80,128]{1,0:T(8,128)S(1)} %concatenate.69), channel_id=1, source_target_pairs={{0,8},{2,10},{4,12},{6,14},{8,0},{10,2},{12,4},{14,6},{16,24},{18,... | collective-permute-start | bytes 122888 | tf_op jit(solution)/shard_map/ppermute | solution.py:26
  18.7 4.5 %collective-permute-start.2 = (f32[160,128]{1,0:T(8,128)S(1)}, f32[160,128]{1,0:T(8,128)S(1)}, u32[]{:S(2)}, u32[]{:S(2)}) collective-permute-start(f32[160,128]{1,0:T(8,128)S(1)} %concatenate.70), channel_id=1, source_target_pairs={{0,4},{2,6},{4,0},{6,2},{8,12},{10,14},{12,8},{14,10},{16,20},{18,... | collective-permute-start | bytes 245768 | tf_op jit(solution)/shard_map/ppermute | solution.py:26
  23.2 1.5 %collective-permute-start.3 = (f32[320,128]{1,0:T(8,128)S(1)}, f32[320,128]{1,0:T(8,128)S(1)}, u32[]{:S(2)}, u32[]{:S(2)}) collective-permute-start(f32[320,128]{1,0:T(8,128)S(1)} %concatenate.71), channel_id=1, source_target_pairs={{0,2},{2,0},{4,6},{6,4},{8,10},{10,8},{12,14},{14,12},{16,18},{18,... | collective-permute-start | bytes 491528 | tf_op jit(solution)/shard_map/ppermute | solution.py:26
  25.3 22.2 %copy-start.4 = (f32[64]{0:T(128)S(1)}, f32[64]{0:T(128)}, u32[]{:S(2)}) copy-start(f32[64]{0:T(128)} %param.21) | copy-start | bytes 772
  28.2 3.7 %collective-permute-start.4 = (f32[16,128]{1,0:T(8,128)S(1)}, f32[16,128]{1,0:T(8,128)S(1)}, u32[]{:S(2)}, u32[]{:S(2)}) collective-permute-start(f32[16,128]{1,0:T(8,128)S(1)} %concatenate.74), channel_id=1, source_target_pairs={{0,1},{1,0},{2,3},{3,2},{4,5},{5,4},{6,7},{7,6},{8,9},{9,8},{10,11... | collective-permute-start | bytes 24584 | tf_op jit(solution)/shard_map/ppermute | solution.py:48
  36.4 4.7 %collective-permute-start.5 = (f32[40,128]{1,0:T(8,128)S(1)}, f32[40,128]{1,0:T(8,128)S(1)}, u32[]{:S(2)}, u32[]{:S(2)}) collective-permute-start(f32[40,128]{1,0:T(8,128)S(1)} %pad_maximum_fusion.5), channel_id=1, source_target_pairs={{0,16},{2,18},{4,20},{6,22},{8,24},{10,26},{12,28},{14,30},{16,0},... | collective-permute-start | bytes 61448 | tf_op jit(solution)/shard_map/ppermute | solution.py:26
  39.4 7.8 %collective-permute-start.9 = (f32[64,2,2,128]{3,2,1,0:T(2,128)S(1)}, f32[64,2,2,128]{3,2,1,0:T(2,128)S(1)}, u32[]{:S(2)}, u32[]{:S(2)}) collective-permute-start(f32[64,2,2,128]{3,2,1,0:T(2,128)S(1)} %slice_select_fusion), channel_id=1, source_target_pairs={{0,1},{1,0},{2,3},{3,2},{4,5},{5,4},{6,7},{7,6},{8,9},{9,8},{10,11... | collective-permute-start | bytes 393224 | tf_op jit(solution)/shard_map/ppermute | solution.py:58
  41.1 4.1 %collective-permute-start.6 = (f32[80,128]{1,0:T(8,128)S(1)}, f32[80,128]{1,0:T(8,128)S(1)}, u32[]{:S(2)}, u32[]{:S(2)}) collective-permute-start(f32[80,128]{1,0:T(8,128)S(1)} %pad_maximum_fusion.3), channel_id=1, source_target_pairs={{0,8},{2,10},{4,12},{6,14},{8,0},{10,2},{12,4},{14,6},{16,24},{18,... | collective-permute-start | bytes 122888 | tf_op jit(solution)/shard_map/ppermute | solution.py:26
  45.2 7.4 %collective-permute-start.7 = (f32[160,128]{1,0:T(8,128)S(1)}, f32[160,128]{1,0:T(8,128)S(1)}, u32[]{:S(2)}, u32[]{:S(2)}) collective-permute-start(f32[160,128]{1,0:T(8,128)S(1)} %concatenate.77), channel_id=1, source_target_pairs={{0,4},{2,6},{4,0},{6,2},{8,12},{10,14},{12,8},{14,10},{16,20},{18,... | collective-permute-start | bytes 245768 | tf_op jit(solution)/shard_map/ppermute | solution.py:26
  48.6 1.0 %copy-start.1 = (f32[64,2,10,128]{3,2,1,0:T(8,128)}, f32[64,2,10,128]{3,2,1,0:T(8,128)S(1)}, u32[]{:S(2)}) copy-start(f32[64,2,10,128]{3,2,1,0:T(8,128)S(1)} %get-tuple-element.9) | copy-start | bytes 1966084
  51.0 3.7 %collective-permute-start.10 = (f32[8,128]{1,0:T(8,128)S(1)}, f32[8,128]{1,0:T(8,128)S(1)}, u32[]{:S(2)}, u32[]{:S(2)}) collective-permute-start(f32[8,128]{1,0:T(8,128)S(1)} %broadcast_in_dim.95), channel_id=1, source_target_pairs={{0,1},{1,0},{2,3},{3,2},{4,5},{5,4},{6,7},{7,6},{8,9},{9,8},{10,11... | collective-permute-start | bytes 12296 | tf_op jit(solution)/shard_map/ppermute | solution.py:48
  52.6 3.3 %collective-permute-start.8 = (f32[320,128]{1,0:T(8,128)S(1)}, f32[320,128]{1,0:T(8,128)S(1)}, u32[]{:S(2)}, u32[]{:S(2)}) collective-permute-start(f32[320,128]{1,0:T(8,128)S(1)} %concatenate.78), channel_id=1, source_target_pairs={{0,2},{2,0},{4,6},{6,4},{8,10},{10,8},{12,14},{14,12},{16,18},{18,... | collective-permute-start | bytes 491528 | tf_op jit(solution)/shard_map/ppermute | solution.py:26
  61.5 24.8 %copy-start.2 = (f32[64,2,10,128]{3,2,1,0:T(8,128)S(1)}, f32[64,2,10,128]{3,2,1,0:T(8,128)}, u32[]{:S(2)}) copy-start(f32[64,2,10,128]{3,2,1,0:T(8,128)} %copy-done.1) | copy-start | bytes 1966084
  63.7 3.7 %collective-permute-start.11 = (f32[16,128]{1,0:T(8,128)S(1)}, f32[16,128]{1,0:T(8,128)S(1)}, u32[]{:S(2)}, u32[]{:S(2)}) collective-permute-start(f32[16,128]{1,0:T(8,128)S(1)} %concatenate.84), channel_id=1, source_target_pairs={{0,1},{1,0},{2,3},{3,2},{4,5},{5,4},{6,7},{7,6},{8,9},{9,8},{10,11... | collective-permute-start | bytes 24584 | tf_op jit(solution)/shard_map/ppermute | solution.py:48
  70.6 4.6 %collective-permute-start.12 = (f32[8,128]{1,0:T(8,128)S(1)}, f32[8,128]{1,0:T(8,128)S(1)}, u32[]{:S(2)}, u32[]{:S(2)}) collective-permute-start(f32[8,128]{1,0:T(8,128)S(1)} %broadcast_in_dim.96), channel_id=1, source_target_pairs={{0,16},{2,18},{4,20},{6,22},{8,24},{10,26},{12,28},{14,30},{16,0},... | collective-permute-start | bytes 12296 | tf_op jit(solution)/shard_map/ppermute | solution.py:38
  75.8 3.7 %collective-permute-start.13 = (f32[8,128]{1,0:T(8,128)S(1)}, f32[8,128]{1,0:T(8,128)S(1)}, u32[]{:S(2)}, u32[]{:S(2)}) collective-permute-start(f32[8,128]{1,0:T(8,128)S(1)} %broadcast_add_fusion.1), channel_id=1, source_target_pairs={{0,8},{2,10},{4,12},{6,14},{8,0},{10,2},{12,4},{14,6},{16,24},{18,... | collective-permute-start | bytes 12296 | tf_op jit(solution)/shard_map/ppermute | solution.py:38
  77.4 6.4 %collective-permute-start.16 = (f32[64,2,1,128]{3,2,1,0:T(1,128)S(1)}, f32[64,2,1,128]{3,2,1,0:T(1,128)S(1)}, u32[]{:S(2)}, u32[]{:S(2)}) collective-permute-start(f32[64,2,1,128]{3,2,1,0:T(1,128)S(1)} %broadcast_select_fusion.2), channel_id=1, source_target_pairs={{0,1},{1,0},{2,3},{3,2},{4,5},{5,4},{6,7},{7,6},{8,9},{9,8},{10,11... | collective-permute-start | bytes 196616 | tf_op jit(solution)/shard_map/ppermute | solution.py:58
  80.1 3.7 %collective-permute-start.14 = (f32[8,128]{1,0:T(8,128)S(1)}, f32[8,128]{1,0:T(8,128)S(1)}, u32[]{:S(2)}, u32[]{:S(2)}) collective-permute-start(f32[8,128]{1,0:T(8,128)S(1)} %fusion.86), channel_id=1, source_target_pairs={{0,4},{2,6},{4,0},{6,2},{8,12},{10,14},{12,8},{14,10},{16,20},{18,... | collective-permute-start | bytes 12296 | tf_op jit(solution)/shard_map/ppermute | solution.py:38
  83.8 6.5 %collective-permute-start.15 = (f32[8,128]{1,0:T(8,128)S(1)}, f32[8,128]{1,0:T(8,128)S(1)}, u32[]{:S(2)}, u32[]{:S(2)}) collective-permute-start(f32[8,128]{1,0:T(8,128)S(1)} %add.145), channel_id=1, source_target_pairs={{0,2},{2,0},{4,6},{6,4},{8,10},{10,8},{12,14},{14,12},{16,18},{18,... | collective-permute-start | bytes 12296 | tf_op jit(solution)/shard_map/ppermute | solution.py:38
  88.4 3.7 %collective-permute-start.17 = (f32[8,128]{1,0:T(8,128)S(1)}, f32[8,128]{1,0:T(8,128)S(1)}, u32[]{:S(2)}, u32[]{:S(2)}) collective-permute-start(f32[8,128]{1,0:T(8,128)S(1)} %broadcast_in_dim.98), channel_id=1, source_target_pairs={{0,1},{1,0},{2,3},{3,2},{4,5},{5,4},{6,7},{7,6},{8,9},{9,8},{10,11... | collective-permute-start | bytes 12296 | tf_op jit(solution)/shard_map/ppermute | solution.py:48

commit v2 on v0

v2 whole, which is shorter than its diff:
```python
import functools

import jax
import jax.numpy as jnp
from jax import lax
from jax.experimental import pallas as pl
from jax.experimental.pallas import tpu as pltpu
from jax.sharding import PartitionSpec as P

ALT = 64
EPOCHS = 2
LAT = 128
LON_DEV = 8
RAY_TILE = 128
RT = 8
PAIRS = ALT * EPOCHS
LINES = PAIRS * LON_DEV
PAD = EPOCHS
UNROLL = 8

LATERAL = 1.0
VERTICAL = 4.0
TEMPORAL = 0.5
CENTRE = 2.0 * (2.0 * LATERAL + VERTICAL + TEMPORAL)

F32 = jnp.float32
BF16 = jnp.bfloat16
VM = pl.BlockSpec(memory_space=pltpu.VMEM)
SM = pl.BlockSpec(memory_space=pltpu.SMEM)


def local_call(body, name, in_specs, out_shapes, scratch=()):
    return pl.pallas_call(
        body,
        name=name,
        in_specs=in_specs,
        out_specs=[VM] * len(out_shapes),
        out_shape=[jax.ShapeDtypeStruct(shape, dtype) for shape, dtype in out_shapes],
        scratch_shapes=list(scratch),
        compiler_params=pltpu.CompilerParams(vmem_limit_bytes=32 << 20),
    )


def pairs_of(count, step):
    return [(i, i ^ step) for i in range(count)]


def hops(count):
    steps = []
    while count > 1:
        count //= 2
        steps.append(count)
    return steps


def gather_rays(block, during=()):
    count = lax.axis_size("ray")
    done, given = list(during), None
    if count & (count - 1) or count == 1:
        whole = lax.all_gather(block, "ray", tiled=True)
        half = whole.shape[0] // 2
        block, other = whole[:half], whole[half:]
    else:
        for step in hops(count):
            other = lax.ppermute(block, "ray", pairs_of(count, step))
            if step == 1:
                break
            joined = jnp.concatenate([block, other], axis=0)
            if done:
                given = done.pop(0)(given)
                joined, given = lax.optimization_barrier((joined, given))
            block = joined
    while done:
        given = done.pop(0)(given)
    return block, other, given


def vox_others(value):
    count = lax.axis_size("vox")
    if count == 1:
        return jnp.zeros_like(value)
    if count == 2:
        return lax.ppermute(value, "vox", [(0, 1), (1, 0)])
    return lax.psum(value, "vox") - value


def last_sums(value, step_of):
    count, slabs = lax.axis_size("ray"), lax.axis_size("vox")
    if slabs != 2 or count & (count - 1) or count < 8:
        mine = step_of(None)
        return lax.psum(value, "ray"), mine, vox_others(mine)
    for step in hops(count)[:-2]:
        value = value + lax.ppermute(value, "ray", pairs_of(count, step))
        if step == count // 2:
            mine = step_of(None)
            value, mine = lax.optimization_barrier((value, mine))
    both = jnp.concatenate([value, mine], axis=0)
    both = lax.ppermute(both, ("ray", "vox"), [(i, i ^ 5) for i in range(2 * count)])
    value = value + both[:8]
    return value, lax.ppermute(value, "ray", pairs_of(count, 1)), mine, both[8:]


def halo_of(low_edge, high_edge):
    count = lax.axis_size("vox")
    if count == 1:
        return jnp.zeros_like(high_edge), jnp.zeros_like(low_edge)
    forward = [(i, i + 1) for i in range(count - 1)]
    backward = [(target, source) for source, target in forward]
    return lax.ppermute(high_edge, "vox", forward), lax.ppermute(low_edge, "vox", backward)


def first_halo(sums, field):
    if lax.axis_size("vox") == 2 and lax.axis_size("ray") % 2 == 0:
        other = lax.ppermute(sums, "vox", [(0, 1), (1, 0)])
        column = other[RT + 8 :]
        partner = lax.ppermute(column, "ray", pairs_of(lax.axis_size("ray"), 1))
        return other, (column, partner, column, partner), True
    low = halo_of(field[PAD:-PAD, 0], field[PAD:-PAD, -1])
    far = halo_of(field[PAD:-PAD, 1], field[PAD:-PAD, -2])
    return vox_others(sums), (low[0], far[0], low[1], far[1]), False


def next_halo(sums, field):
    if lax.axis_size("vox") == 2:
        other = lax.ppermute(sums, "vox", [(0, 1), (1, 0)])
        column = other[RT + 8 :]
        return other, (column, column)
    return vox_others(sums), halo_of(field[PAD:-PAD, 0], field[PAD:-PAD, -1])


def total(values):
    return jnp.sum(values, axis=(0, 1), keepdims=True)


def sub_iota(shape=(8, LAT)):
    return lax.broadcasted_iota(jnp.int32, shape, 0)


def lane_iota(shape=(8, LAT)):
    return lax.broadcasted_iota(jnp.int32, shape, 1)


def pull_lines(weighted, tiles_ref, pick_ref, out_ref, slots):
    rays = weighted.astype(BF16)
    for k in range(slots):
        product = jnp.dot(rays, tiles_ref[k], preferred_element_type=F32)
        out_ref[pl.ds(k, 1), :] = jnp.sum(pick_ref[k] * product, axis=0, keepdims=True)


def push_lines(lines, tiles_ref, pick_ref, slots):
    rays = jnp.zeros((RT, RAY_TILE), F32)
    for k in range(slots):
        line = jnp.broadcast_to(lines[k : k + 1], (RT, LAT)).astype(BF16)
        product = lax.dot_general(
            line, tiles_ref[k], (((1,), (1,)), ((), ())), preferred_element_type=F32
        )
        rays = rays + pick_ref[k] * product
    return rays


def both_parts(lines):
    high = lines.astype(BF16)
    low = (lines - high.astype(F32)).astype(BF16)
    return jnp.concatenate([high, low], axis=1)


def across(values, sub, lane):
    up = jnp.where(lane == 0, 0.0, pltpu.roll(values, 1, 1))
    down = jnp.where(lane == LAT - 1, 0.0, pltpu.roll(values, LAT - 1, 1))
    return up + down


def column_stencil(column, beside, lane, sub):
    up = jnp.where(sub < EPOCHS, 0.0, pltpu.roll(column, EPOCHS, 0))
    down = jnp.where(sub >= PAIRS - EPOCHS, 0.0, pltpu.roll(column, PAIRS - EPOCHS, 0))
    later = pltpu.roll(column, PAIRS - 1, 0)
    earlier = pltpu.roll(column, 1, 0)
    epoch = jnp.where(sub % EPOCHS == 0, later, earlier)
    return (
        CENTRE * column
        - LATERAL * (beside + across(column, sub, lane))
        - VERTICAL * (up + down)
        - TEMPORAL * epoch
    )


def slab_stencil(pair, field_ref, low_ref, high_ref, sub, lane):
    here = field_ref[pair + PAD]
    below = jnp.where(sub == 0, low_ref[pl.ds(pair, 1), :], pltpu.roll(here, 1, 0))
    above = jnp.where(sub == LON_DEV - 1, high_ref[pl.ds(pair, 1), :], pltpu.roll(here, LON_DEV - 1, 0))
    epoch = field_ref[(pair ^ 1) + PAD]
    return (
        CENTRE * here
        - LATERAL * (below + above + across(here, sub, lane))
        - VERTICAL * (field_ref[pair] + field_ref[pair + 2 * PAD])
        - TEMPORAL * epoch
    )


def start_body(slots, row_ref, col_ref, scale_ref, count_ref, table_ref, receiver_ref, delays_ref, tiles_ref,
               packet_ref, weight_ref, start_ref, pick_ref, own_ref):
    sub, lane = sub_iota(), lane_iota()
    receivers = receiver_ref[...]
    weight = jnp.zeros((RT, RAY_TILE), F32)
    for j in range(table_ref.shape[0]):
        weight = jnp.where(receivers == j, table_ref[j], weight)
    weight_ref[...] = weight
    start = weight * delays_ref[...]
    start_ref[...] = start
    names = jnp.zeros((8, LAT), jnp.int32)
    for k in range(slots):
        live = jnp.where(k < count_ref[0], scale_ref[k], 0.0)
        pick_ref[k] = jnp.where(sub == row_ref[k], live, 0.0)
        own_ref[pl.ds(k, 1), :] = jnp.full((1, LAT), col_ref[k], jnp.int32)
        names = jnp.where(lane == k, col_ref[k], names)
    pull_lines(weight * start, tiles_ref, pick_ref, packet_ref, slots)
    square = total(start * start)
    packet_ref[slots:, :] = jnp.where(
        sub == 0, names.astype(F32), jnp.where(sub == 1, square, 0.0)
    )


def names_of(ref, slots):
    blocks = ref.shape[0] // (slots + 8)
    per = LAT // slots
    pieces = []
    for first in range(0, blocks, per):
        row = ref[pl.ds(first * (slots + 8) + slots, 1), :]
        for j in range(1, min(per, blocks - first)):
            row = row + pltpu.roll(ref[pl.ds((first + j) * (slots + 8) + slots, 1), :], j * slots, 1)
        if blocks - first < per:
            row = jnp.where(lane_iota((1, LAT)) < (blocks - first) * slots, row, -1.0)
        pieces.append(row.astype(jnp.int32))
    return pieces


def lines_in(ref, slots):
    blocks = ref.shape[0] // (slots + 8)
    return [ref[b * (slots + 8) : b * (slots + 8) + slots, :] for b in range(blocks)]


def padded_lines(ref_a, ref_b, slots):
    per = LAT // slots
    rows = []
    for ref in (ref_a, ref_b):
        lines = lines_in(ref, slots)
        rows += lines
        if len(lines) % per:
            rows.append(jnp.zeros(((per - len(lines) % per) * slots, LAT), F32))
    return jnp.concatenate(rows, axis=0)


def rows_sum(ref, slots, at):
    blocks = ref.shape[0] // (slots + 8)
    out = ref[pl.ds(slots + at, 1), :]
    for b in range(1, blocks):
        out = out + ref[pl.ds(b * (slots + 8) + slots + at, 1), :]
    return out


CHUNK = 128


def onehot_of(names, ids):
    return jnp.concatenate(
        [jnp.where(ids == piece, 1.0, 0.0).astype(BF16) for piece in names], axis=1
    )


def edge_of(field_ref, at):
    return field_ref[PAD : PAIRS + PAD, at, :]


def first_body(slots, mine_ref, other_ref, own_ref, pick_ref, tiles_ref,
               field_ref, lines_ref, out_ref, left_ref, names_ref):
    names = names_of(mine_ref, slots) + names_of(other_ref, slots)
    for j, piece in enumerate(names):
        names_ref[pl.ds(j, 1), :] = piece
    parts = both_parts(padded_lines(mine_ref, other_ref, slots))

    def take(ids):
        found = jnp.dot(onehot_of(names, ids), parts, preferred_element_type=F32)
        return found[:, :LAT] + found[:, LAT:]

    lines = take(own_ref[...])
    lines_ref[...] = lines
    rays = push_lines(lines, tiles_ref, pick_ref, slots)
    zeros = jnp.zeros((PAD, LON_DEV, LAT), F32)
    field_ref[:PAD] = zeros
    field_ref[PAIRS + PAD :] = zeros
    square = jnp.zeros((8, LAT), F32)
    for first in range(0, LINES, CHUNK):
        piece = take(sub_iota((CHUNK, LAT)) + first).reshape(CHUNK // LON_DEV, LON_DEV, LAT)
        at = first // LON_DEV + PAD
        field_ref[at : at + CHUNK // LON_DEV] = piece
        square = square + jnp.sum(piece * piece, axis=0)
    out_ref[:RT, :] = rays
    out_ref[RT : RT + 8, :] = jnp.broadcast_to(total(square), (8, LAT))
    odd = lax.axis_index("ray") % 2 == 1
    high = jnp.where(odd, edge_of(field_ref, LON_DEV - 2), edge_of(field_ref, LON_DEV - 1))
    low = jnp.where(odd, edge_of(field_ref, 1), edge_of(field_ref, 0))
    out_ref[RT + 8 :, :] = jnp.where(lax.axis_index("vox") == 0, high, low)
    left_ref[...] = jnp.broadcast_to(rows_sum(mine_ref, slots, 1) + rows_sum(other_ref, slots, 1), (8, LAT))


def second_body(slots, mine_ref, other_ref, left_ref, weight_ref, start_ref, pick_ref, tiles_ref,
                packet_ref, rays_ref, image_ref, norm_ref):
    sub = sub_iota()
    left_sq = left_ref[...]
    norm_sq = mine_ref[RT : RT + 8, :] + other_ref[RT : RT + 8, :]
    inverse = lax.rsqrt(norm_sq)
    norm = norm_sq * inverse
    weight = weight_ref[...]
    image = (mine_ref[:RT, :] + other_ref[:RT, :]) * inverse
    image_ref[...] = image
    rays = weight * image - norm / left_sq * start_ref[...]
    rays_ref[...] = rays
    norm_ref[...] = norm
    pull_lines(weight * rays, tiles_ref, pick_ref, packet_ref, slots)
    packet_ref[slots:, :] = jnp.where(sub == 0, total(rays * rays), 0.0)


def flags():
    at, count = lax.axis_index("vox"), lax.axis_size("vox")
    return (at > 0).astype(F32), (at < count - 1).astype(F32)


def smooth_body(swapped, field_ref, low_ref, low2_ref, high_ref, high2_ref, damp_ref, norm_ref,
                smooth_ref, scaled_ref, far_ref, square_ref, near_ref):
    sub, lane = sub_iota(), lane_iota()
    has_low, has_high = flags()
    inverse = 1.0 / norm_ref[...]
    col_lane, col_sub = lane_iota((PAIRS, LAT)), sub_iota((PAIRS, LAT))
    low, low2, high, high2 = low_ref[...], low2_ref[...], high_ref[...], high2_ref[...]
    if swapped:
        odd = lax.axis_index("ray") % 2 == 1
        low, low2 = jnp.where(odd, low2, low), jnp.where(odd, low, low2)
        high, high2 = low, low2
    near_ref[0] = low * has_low
    near_ref[1] = high * has_high
    scale = damp_ref[...] * damp_ref[...] * jnp.broadcast_to(inverse[:1], (PAIRS, LAT))
    far_ref[0] = scale * has_low * column_stencil(low, low2 + edge_of(field_ref, 0), col_lane, col_sub)
    far_ref[1] = scale * has_high * column_stencil(
        high, high2 + edge_of(field_ref, LON_DEV - 1), col_lane, col_sub
    )
    zeros = jnp.zeros((PAD, LON_DEV, LAT), F32)
    scaled_ref[:PAD] = zeros
    scaled_ref[PAIRS + PAD :] = zeros

    def left(pair, square):
        damped = damp_ref[pl.ds(pair, 1), :]
        value = slab_stencil(pair, field_ref, near_ref.at[0], near_ref.at[1], sub, lane) * inverse * damped
        smooth_ref[pair] = value
        scaled_ref[pair + PAD] = value * damped
        return square + value * value

    square = lax.fori_loop(0, PAIRS, left, jnp.zeros((LON_DEV, LAT), F32), unroll=UNROLL)
    square_ref[...] = jnp.broadcast_to(total(square), (8, LAT))


def onehot_body(names_ref, onehot_ref):
    pieces = [names_ref[pl.ds(j, 1), :] for j in range(onehot_ref.shape[1] // LAT)]
    for first in range(0, LINES, CHUNK):
        onehot_ref[first : first + CHUNK, :] = onehot_of(pieces, sub_iota((CHUNK, LAT)) + first)


def again_body(slots, col_ref, scaled_ref, far_ref, again_ref, lines_ref):
    sub, lane = sub_iota(), lane_iota()

    def right(pair, carry):
        again_ref[pair] = slab_stencil(pair, scaled_ref, far_ref.at[0], far_ref.at[1], sub, lane)
        return carry

    lax.fori_loop(0, PAIRS, right, 0, unroll=UNROLL)
    for k in range(slots):
        col = col_ref[k]
        lines_ref[pl.ds(k, 1), :] = again_ref[col // LON_DEV, pl.ds(col % LON_DEV, 1), :]


def third_body(slots, mine_ref, other_ref, square_ref, onehot_ref, names_ref, own_ref, lines_ref,
               again_lines_ref, again_ref, field_ref, norm_ref, pick_ref, tiles_ref,
               next_ref, out_ref, shift_ref):
    shift = jnp.broadcast_to(rows_sum(mine_ref, slots, 0) + rows_sum(other_ref, slots, 0), (8, LAT))
    shift_ref[...] = shift
    inverse = 1.0 / norm_ref[...]
    back = shift * inverse
    parts = both_parts(padded_lines(mine_ref, other_ref, slots))
    names = [names_ref[pl.ds(j, 1), :] for j in range(onehot_ref.shape[1] // LAT)]

    def take(onehot):
        found = jnp.dot(onehot, parts, preferred_element_type=F32)
        return found[:, :LAT] + found[:, LAT:]

    lines = take(onehot_of(names, own_ref[...])) + again_lines_ref[...] - lines_ref[...] * back[:1]
    rays = push_lines(lines, tiles_ref, pick_ref, slots)
    zeros = jnp.zeros((PAD, LON_DEV, LAT), F32)
    next_ref[:PAD] = zeros
    next_ref[PAIRS + PAD :] = zeros
    square = jnp.zeros((8, LAT), F32)
    cross = jnp.zeros((8, LAT), F32)
    for first in range(0, LINES, CHUNK):
        count, pair = CHUNK // LON_DEV, first // LON_DEV
        piece = take(onehot_ref[first : first + CHUNK, :]).reshape(count, LON_DEV, LAT)
        base = field_ref[pair + PAD : pair + PAD + count]
        piece = piece + again_ref[pair : pair + count] - base * back
        next_ref[pair + PAD : pair + PAD + count] = piece
        square = square + jnp.sum(piece * piece, axis=0)
        cross = cross + jnp.sum(piece * base, axis=0)
    sub = sub_iota()
    out_ref[:RT, :] = rays
    out_ref[RT : RT + 8, :] = jnp.where(
        sub == 0, total(square), jnp.where(sub == 1, total(cross) * inverse, square_ref[...])
    )
    out_ref[RT + 8 :, :] = jnp.where(
        lax.axis_index("vox") == 0, edge_of(next_ref, LON_DEV - 1), edge_of(next_ref, 0)
    )


def fourth_body(mine_ref, other_ref, shift_ref, weight_ref, rays_ref, image_ref,
                next_rays_ref, left_ref, rest_ref, norm_ref, sum_ref):
    sums = mine_ref[RT : RT + 8, :] + other_ref[RT : RT + 8, :]
    square, cross, rest = [jnp.broadcast_to(sums[j : j + 1], (8, LAT)) for j in range(3)]
    left_sq = shift_ref[...] + rest
    norm_sq = (square - 2.0 * rest * cross + rest * rest) / left_sq
    per_left = lax.rsqrt(left_sq)
    inverse = lax.rsqrt(norm_sq)
    norm = norm_sq * inverse
    rays = mine_ref[:RT, :] + other_ref[:RT, :] - rest * image_ref[...]
    rays = weight_ref[...] * rays * (per_left * inverse) - norm * per_left * rays_ref[...]
    next_rays_ref[...] = rays
    left_ref[...] = left_sq
    rest_ref[...] = rest
    norm_ref[...] = norm
    sum_ref[...] = jnp.broadcast_to(total(rays * rays), (8, LAT))


def last_smooth_body(next_ref, low_ref, high_ref, damp_ref, smooth_ref, norm_ref, left_ref, rest_ref,
                     square_ref, near_ref):
    sub, lane = sub_iota(), lane_iota()
    has_low, has_high = flags()
    near_ref[0] = low_ref[...] * has_low
    near_ref[1] = high_ref[...] * has_high
    norm, per_left = norm_ref[...], lax.rsqrt(left_ref[...])
    inverse = per_left / norm
    back = rest_ref[...] * inverse + norm * per_left

    def left(pair, square):
        damped = damp_ref[pl.ds(pair, 1), :]
        value = slab_stencil(pair, next_ref, near_ref.at[0], near_ref.at[1], sub, lane) * inverse * damped
        value = value - back * smooth_ref[pair]
        return square + value * value

    square = lax.fori_loop(0, PAIRS, left, jnp.zeros((LON_DEV, LAT), F32), unroll=UNROLL)
    square_ref[...] = jnp.broadcast_to(total(square), (8, LAT))


def end_body(share, parts, *refs):
    sums = refs[0][...]
    for ref in refs[1:parts]:
        sums = sums + ref[...]
    (left0_ref, norm0_ref, left1_ref, rest_ref, norm1_ref, rays_ref, field_ref, next_ref,
     density_ref, out_ref) = refs[parts:]
    left2_sq = sums
    out_ref[...] = rays_ref[...] * lax.rsqrt(left2_sq)
    left0_sq, norm0, left1_sq, right1 = left0_ref[...], norm0_ref[...], left1_ref[...], norm1_ref[...]
    left0, left1 = jnp.sqrt(left0_sq), jnp.sqrt(left1_sq)
    right0 = norm0 / left0
    diag1 = jnp.sqrt(right0 * right0 + left1_sq)
    cosine, sine = right0 / diag1, left1 / diag1
    coupling = sine * right1
    diag_bar = -cosine * right1
    step1, resid = cosine * left0, sine * left0
    diag2 = jnp.sqrt(diag_bar * diag_bar + left2_sq)
    step2 = diag_bar / diag2 * resid
    on_next = step2 / diag2 / (left1 * right1)
    on_first = (step1 / diag1 - step2 / diag2 * coupling / diag1 - on_next * rest_ref[...]) / norm0
    first = lax.axis_index("ray") * share + PAD
    for j in range(share):
        density_ref[j] = on_first * field_ref[first + j] + on_next * next_ref[first + j]


def on_device(
    tiles,
    tile_scale,
    tile_row,
    tile_col,
    tile_count,
    delays,
    ray_receiver,
    receiver_weight,
    smooth_scale,
):
    block = tiles[0, 0]
    slots = block.shape[0]
    rays_n = lax.axis_size("ray")
    col_index = tile_col[0, 0]
    held = (RT, RAY_TILE)
    row = ((8, LAT), F32)
    slab = ((PAIRS, LON_DEV, LAT), F32)
    padded = ((PAIRS + 2 * PAD, LON_DEV, LAT), F32)
    packet = ((slots + 8, LAT), F32)
    damp = jnp.broadcast_to(jnp.repeat(smooth_scale, EPOCHS)[:, None], (PAIRS, LAT))

    mine, weight, start, pick, own = local_call(
        functools.partial(start_body, slots), "start", [SM] * 5 + [VM] * 3,
        [packet, (held, F32), (held, F32), ((slots, RT, LAT), F32), ((slots, LAT), jnp.int32)],
    )(tile_row[0, 0], col_index, tile_scale[0, 0], tile_count[0], receiver_weight,
      ray_receiver.reshape(held), delays.reshape(held), block)
    near, far, damp = gather_rays(mine, (lambda _: damp,))
    per = LAT // slots
    names_n = 2 * -(-(near.shape[0] // (slots + 8)) // per)

    field, lines, sums, left0, names = local_call(
        functools.partial(first_body, slots), "first", [VM] * 5,
        [padded, ((slots, LAT), F32), ((RT + 8 + PAIRS, LAT), F32), row, ((names_n, LAT), jnp.int32)],
    )(near, far, own, pick, block)
    others, columns, swapped = first_halo(sums, field)
    onehot = local_call(onehot_body, "onehot", [VM], [((LINES, names_n * LAT), BF16)])(names)[0]
    others, onehot = lax.optimization_barrier((others, onehot))

    mine, rays, image, norm0 = local_call(
        functools.partial(second_body, slots), "second", [VM] * 7, [packet, (held, F32), (held, F32), row],
    )(sums, others, left0, weight, start, pick, block)
    def smooth_step(columns):
        return local_call(
            functools.partial(smooth_body, swapped), "smooth", [VM] * 7,
            [slab, padded, ((2, PAIRS, LAT), F32), row], [pltpu.VMEM((2, PAIRS, LAT), F32)],
        )(field, *columns, damp, norm0)

    def again_step(given):
        smooth, scaled, beside, square = given
        again, again_lines = local_call(
            functools.partial(again_body, slots), "again", [SM] + [VM] * 2, [slab, ((slots, LAT), F32)],
        )(col_index, scaled, beside)
        return smooth, square, again, again_lines

    near, far, given = gather_rays(mine, (lambda _: columns, smooth_step, again_step))
    smooth, square, again, again_lines = given

    following, sums, shift = local_call(
        functools.partial(third_body, slots), "third", [VM] * 13,
        [padded, ((RT + 8 + PAIRS, LAT), F32), row],
    )(near, far, square, onehot, names, own, lines, again_lines, again, field, norm0, pick, block)
    others, beside = next_halo(sums, following)
    last_rays, left1, rest, norm1, ray_square = local_call(
        fourth_body, "fourth", [VM] * 6, [(held, F32), row, row, row, row],
    )(sums, others, shift, weight, rays, image)

    def last_step(_):
        return local_call(
            last_smooth_body, "last_smooth", [VM] * 8, [row], [pltpu.VMEM((2, PAIRS, LAT), F32)],
        )(following, *beside, damp, smooth, norm1, left1, rest)[0]

    shares = last_sums(ray_square, last_step)

    share = PAIRS // rays_n
    density, rays_out = local_call(
        functools.partial(end_body, share, len(shares)), "end", [VM] * (len(shares) + 8),
        [((share, LON_DEV, LAT), F32), (held, F32)],
    )(*shares, left0, norm0, left1, rest, norm1, last_rays, field, following)
    return (density.reshape(ALT // rays_n, EPOCHS, LON_DEV, LAT), rays_out.reshape(-1))


def solution(mesh):
    in_specs = (
        P("ray", "vox", None, None, None),
        P("ray", "vox", None),
        P("ray", "vox", None),
        P("ray", "vox", None),
        P("ray", "vox"),
        P("ray"),
        P("ray"),
        P("ray"),
        P(),
    )
    out_specs = (P("ray", None, "vox", None), P("ray"))
    return jax.shard_map(
        on_device, mesh=mesh, in_specs=in_specs, out_specs=out_specs, check_vma=False
    )
```

time: 364 us -> 62 us (0.17)
  waiting for transfers between devices: 169 us -> 21.8 us
  blocking collectives: 119 us -> 0 us
  other arithmetic: 29.7 us -> 0.05 us
  between operations: 20 us -> 1.43 us
  Pallas kernels: 0 us -> 10.8 us
  starting transfers between devices: 17.6 us -> 25.5 us
  matrix products: 5.56 us -> 0 us
    psum x2 -> x0, waiting for transfers between devices: 168 us -> none  [pull_back(): return lax.psum(summed, 'ray')]
    psum x7 -> x0, blocking collectives: 119 us -> none  [the longest x3 95.7 us: ray_total(): return lax.psum(jnp.sum(values * values), 'ray')]
    ppermute x6 -> x15, waiting for transfers between devices: 0.69 us -> 21.8 us  [the longest x8 11.8 us: gather_rays(): other = lax.ppermute(block, 'ray', pairs_of(count, step))]
    reduce_sum x8 -> x0, other arithmetic: 14.9 us -> none  [the longest x4 11.6 us: slab_total(): return lax.psum(jnp.sum(values * values), 'vox')]
    pallas_call x0 -> x10, Pallas kernels: none -> 10.8 us  [the longest x1 2.17 us: again_step(): local_call(functools.partial(again_body, slots), 'again', [SM] + [VM] * 2...]
    concatenate x3 -> x6, other arithmetic: 8.48 us -> 0.04 us  [the longest x5 0.03 us: gather_rays(): joined = jnp.concatenate([block, other], axis=0)]
    ppermute x6 -> x15, starting transfers between devices: 17.5 us -> 25.5 us  [the longest x8 14.4 us: gather_rays(): other = lax.ppermute(block, 'ray', pairs_of(count, step))]
    dot_general x8 -> x0, matrix products: 5.56 us -> none  [the longest x2 3.13 us: pull_back(): jnp.dot(onehot, contrib, precision=lax.Precision.HIGHEST)]
  transfers between devices with their start and end apart: 8 -> 15, of which waited for: 4 -> 14; matrix products, arithmetic and copies ran while one was open for 3% -> 0% of each run, Pallas kernels for 0% -> 9%
where the time goes in v2:
time: 62 us; the launch traced here: 61.8 us
  starting transfers between devices  25.5 us (41%)
  waiting for transfers between devices  21.8 us (35%)
  Pallas kernels  10.8 us (17%)
  local copies, waits for them, and re-layouts  2.23 us (4%)
  between operations  1.43 us (2%)
    ppermute x8, starting transfers between devices, gather_rays(): other = lax.ppermute(block, 'ray', pairs_of(count, step))  14.4 us
    ppermute x8, waiting for transfers between devices, gather_rays(): other = lax.ppermute(block, 'ray', pairs_of(count, step))  11.8 us
    ppermute x2, starting transfers between devices, last_sums(): value = value + lax.ppermute(value, 'ray', pairs_of(count, step))  4.56 us
    ppermute x1, starting transfers between devices, last_sums(): lax.ppermute(both, ('ray', 'vox'), [(i, i ^ 5) for i in range(2 * count)])  2.7 us
    ppermute x1, waiting for transfers between devices, next_halo(): other = lax.ppermute(sums, 'vox', [(0, 1), (1, 0)])  2.58 us
    ppermute x1, waiting for transfers between devices, first_halo(): other = lax.ppermute(sums, 'vox', [(0, 1), (1, 0)])  2.38 us
    pallas_call x1, Pallas kernels, again_step(): local_call(functools.partial(again_body, slots), 'again', [SM] + [VM] * 2...  2.17 us
    ppermute x1, starting transfers between devices, first_halo(): other = lax.ppermute(sums, 'vox', [(0, 1), (1, 0)])  2 us
  transfers between devices with their start and end apart: 15, of which 14 were waited for; matrix products, arithmetic and copies ran while one was open for 0% of the time, Pallas kernels for 9%

profile of v2, /device:TPU:0, one launch (start us, length us, event | category | flops | bytes accessed | tf_op | source)
XLA Modules:
  0.0 61.8 jit_solution(1814683435318725128)
XLA Ops:
  1.3 0.6 copy-done.6
  1.9 0.0 copy-done.7
  1.9 0.0 copy-done.3
  2.0 0.0 copy-done.2
  2.0 1.2 %copy-done = bf16[1,1,32,128,128]{4,3,2,1,0:T(8,128)(2,1)S(1)} copy-done((bf16[1,1,32,128,128]{4,3,2,1,0:T(8,128)(2,1)S(1)}, bf16[1,1,32,128,128]{4,3,2,1,0:T(8,128)(2,1)}, u32[]{:S(2)}) %copy-start) | copy-done | bytes 1048600
  3.2 1.0 %start.1 = (f32[40,128]{1,0:T(8,128)S(1)}, f32[8,128]{1,0:T(8,128)S(1)}, f32[8,128]{1,0:T(8,128)S(1)}, f32[32,8,128]{2,1,0:T(8,128)S(1)}, s32[32,128]{1,0:T(8,128)S(1)}) custom-call(s32[32]{0:T(128)S(1)} %bitcast.18, s32[32]{0:T(128)S(1)} %bitcast.16, f32[32]{0:T(128)S(1)} %bitcast.19, s32[1]{0:T(128)} %bitcast.9.count_ref, f32[96]{0:T(128)S(1)} %copy-done.7, ...), custom_call_target="tpu_custom_call" | custom-call | tf_op jit(solution)/shard_map/start/pallas_call | solution.py:504
  4.3 4.1 %collective-permute-start = (f32[40,128]{1,0:T(8,128)S(1)}, f32[40,128]{1,0:T(8,128)S(1)}, u32[]{:S(2)}, u32[]{:S(2)}) collective-permute-start(f32[40,128]{1,0:T(8,128)S(1)} %get-tuple-element.53), channel_id=1, source_target_pairs={{0,16},{2,18},{4,20},{6,22},{8,24},{10,26},{12,28},{14,30},{16,0},... | collective-permute-start | bytes 61448 | tf_op jit(solution)/shard_map/ppermute | solution.py:65
  8.4 0.1 broadcast_in_dim.10
  8.4 0.1 broadcast_in_dim.11
  8.6 1.6 %collective-permute-done = f32[40,128]{1,0:T(8,128)S(1)} collective-permute-done((f32[40,128]{1,0:T(8,128)S(1)}, f32[40,128]{1,0:T(8,128)S(1)}, u32[]{:S(2)}, u32[]{:S(2)}) %collective-permute-start) | collective-permute-done | bytes 20512 | tf_op jit(solution)/shard_map/ppermute | solution.py:65
  10.1 0.1 broadcast_in_dim.12.damp_ref
  10.2 1.9 %collective-permute-start.1 = (f32[80,128]{1,0:T(8,128)S(1)}, f32[80,128]{1,0:T(8,128)S(1)}, u32[]{:S(2)}, u32[]{:S(2)}) collective-permute-start(f32[80,128]{1,0:T(8,128)S(1)} %pad_maximum_fusion.3), channel_id=1, source_target_pairs={{0,8},{2,10},{4,12},{6,14},{8,0},{10,2},{12,4},{14,6},{16,24},{18,... | collective-permute-start | bytes 122888 | tf_op jit(solution)/shard_map/ppermute | solution.py:65
  12.1 2.1 %collective-permute-done.1 = f32[80,128]{1,0:T(8,128)S(1)} collective-permute-done((f32[80,128]{1,0:T(8,128)S(1)}, f32[80,128]{1,0:T(8,128)S(1)}, u32[]{:S(2)}, u32[]{:S(2)}) %collective-permute-start.1) | collective-permute-done | bytes 40992 | tf_op jit(solution)/shard_map/ppermute | solution.py:65
  14.3 1.9 %collective-permute-start.2 = (f32[160,128]{1,0:T(8,128)S(1)}, f32[160,128]{1,0:T(8,128)S(1)}, u32[]{:S(2)}, u32[]{:S(2)}) collective-permute-start(f32[160,128]{1,0:T(8,128)S(1)} %pad_maximum_fusion.1), channel_id=1, source_target_pairs={{0,4},{2,6},{4,0},{6,2},{8,12},{10,14},{12,8},{14,10},{16,20},{18,... | collective-permute-start | bytes 245768 | tf_op jit(solution)/shard_map/ppermute | solution.py:65
  16.2 2.5 %collective-permute-done.2 = f32[160,128]{1,0:T(8,128)S(1)} collective-permute-done((f32[160,128]{1,0:T(8,128)S(1)}, f32[160,128]{1,0:T(8,128)S(1)}, u32[]{:S(2)}, u32[]{:S(2)}) %collective-permute-start.2) | collective-permute-done | bytes 81952 | tf_op jit(solution)/shard_map/ppermute | solution.py:65
  18.7 0.1 collective-permute-start.3
  18.8 1.4 %collective-permute-done.3.other_ref = f32[320,128]{1,0:T(8,128)S(1)} collective-permute-done((f32[320,128]{1,0:T(8,128)S(1)}, f32[320,128]{1,0:T(8,128)S(1)}, u32[]{:S(2)}, u32[]{:S(2)}) %collective-permute-start.3) | collective-permute-done | bytes 163872 | tf_op jit(solution)/shard_map/ppermute | solution.py:65
  20.2 1.4 %first.1 = (f32[132,8,128]{2,1,0:T(8,128)S(1)}, f32[32,128]{1,0:T(8,128)S(1)}, f32[144,128]{1,0:T(8,128)S(1)}, f32[8,128]{1,0:T(8,128)S(1)}, s32[4,128]{1,0:T(4,128)S(1)}) custom-call(f32[320,128]{1,0:T(8,128)S(1)} %constant_dynamic-update-slice_fusion.mine_ref, f32[320,128]{1,0:T(8,128)S(1)} %collective-permute-done.3.other_ref, ...), custom_call_target="tpu_custom_call" | custom-call | tf_op jit(solution)/shard_map/first/pallas_call | solution.py:513
  21.6 2.0 %collective-permute-start.4 = (f32[144,128]{1,0:T(8,128)S(1)}, f32[144,128]{1,0:T(8,128)S(1)}, u32[]{:S(2)}, u32[]{:S(2)}) collective-permute-start(f32[144,128]{1,0:T(8,128)S(1)} %get-tuple-element.57.mine_ref), channel_id=1, source_target_pairs={{0,1},{1,0},{2,3},{3,2},{4,5},{5,4},{6,7},{7,6},{8,9},{9,8},{10,11... | collective-permute-start | bytes 221192 | tf_op jit(solution)/shard_map/ppermute | solution.py:114
  23.6 0.2 onehot.1.onehot_ref
  23.7 2.4 %collective-permute-done.4.other_ref = f32[144,128]{1,0:T(8,128)S(1)} collective-permute-done((f32[144,128]{1,0:T(8,128)S(1)}, f32[144,128]{1,0:T(8,128)S(1)}, u32[]{:S(2)}, u32[]{:S(2)}) %collective-permute-start.4) | collective-permute-done | bytes 73760 | tf_op jit(solution)/shard_map/ppermute | solution.py:114
  26.1 0.4 second.1
  26.5 2.8 %collective-permute-start.5 = (f32[40,128]{1,0:T(8,128)S(1)}, f32[40,128]{1,0:T(8,128)S(1)}, u32[]{:S(2)}, u32[]{:S(2)}) collective-permute-start(f32[40,128]{1,0:T(8,128)S(1)} %get-tuple-element.63), channel_id=1, source_target_pairs={{0,16},{2,18},{4,20},{6,22},{8,24},{10,26},{12,28},{14,30},{16,0},... | collective-permute-start | bytes 61448 | tf_op jit(solution)/shard_map/ppermute | solution.py:65
  29.4 0.0 collective-permute-start.6
  29.4 1.9 %collective-permute-done.5 = f32[40,128]{1,0:T(8,128)S(1)} collective-permute-done((f32[40,128]{1,0:T(8,128)S(1)}, f32[40,128]{1,0:T(8,128)S(1)}, u32[]{:S(2)}, u32[]{:S(2)}) %collective-permute-start.5) | collective-permute-done | bytes 20512 | tf_op jit(solution)/shard_map/ppermute | solution.py:65
  31.3 0.0 collective-permute-done.6.low2_ref.high2_ref
  31.3 1.8 %collective-permute-start.7 = (f32[80,128]{1,0:T(8,128)S(1)}, f32[80,128]{1,0:T(8,128)S(1)}, u32[]{:S(2)}, u32[]{:S(2)}) collective-permute-start(f32[80,128]{1,0:T(8,128)S(1)} %pad_maximum_fusion.4), channel_id=1, source_target_pairs={{0,8},{2,10},{4,12},{6,14},{8,0},{10,2},{12,4},{14,6},{16,24},{18,... | collective-permute-start | bytes 122888 | tf_op jit(solution)/shard_map/ppermute | solution.py:65
  33.1 1.8 %smooth.1 = (f32[128,8,128]{2,1,0:T(8,128)S(1)}, f32[132,8,128]{2,1,0:T(8,128)S(1)}, f32[2,128,128]{2,1,0:T(8,128)S(1)}, f32[8,128]{1,0:T(8,128)S(1)}) custom-call(f32[132,8,128]{2,1,0:T(8,128)S(1)} %get-tuple-element.65.field_ref.refs_10_, f32[128,128]{1,0:T(8,128)S(1)} %slice.16.low_ref.high_ref, f32[128,128]{1,0:T(8,128)S(1)} %collective-permute-done.6.low2_ref.high2_ref, ...), custom_call_target="tpu_custom_call" | custom-call | tf_op jit(solution)/shard_map/smooth/pallas_call | solution.py:525
  34.9 0.4 collective-permute-done.7
  35.3 1.7 %collective-permute-start.8 = (f32[160,128]{1,0:T(8,128)S(1)}, f32[160,128]{1,0:T(8,128)S(1)}, u32[]{:S(2)}, u32[]{:S(2)}) collective-permute-start(f32[160,128]{1,0:T(8,128)S(1)} %pad_maximum_fusion.2), channel_id=1, source_target_pairs={{0,4},{2,6},{4,0},{6,2},{8,12},{10,14},{12,8},{14,10},{16,20},{18,... | collective-permute-start | bytes 245768 | tf_op jit(solution)/shard_map/ppermute | solution.py:65
  37.1 2.2 %again.1 = (f32[128,8,128]{2,1,0:T(8,128)S(1)}, f32[32,128]{1,0:T(8,128)S(1)}) custom-call(s32[32]{0:T(128)S(1)} %bitcast.17, f32[132,8,128]{2,1,0:T(8,128)S(1)} %get-tuple-element.79.scaled_ref, f32[2,128,128]{2,1,0:T(8,128)S(1)} %get-tuple-element.80.far_ref), custom_call_target="tpu_custom_call" | custom-call | tf_op jit(solution)/shard_map/again/pallas_call | solution.py:532
  39.3 0.5 collective-permute-done.8
  39.8 0.1 collective-permute-start.9
  39.9 1.4 %collective-permute-done.9.other_ref = f32[320,128]{1,0:T(8,128)S(1)} collective-permute-done((f32[320,128]{1,0:T(8,128)S(1)}, f32[320,128]{1,0:T(8,128)S(1)}, u32[]{:S(2)}, u32[]{:S(2)}) %collective-permute-start.9) | collective-permute-done | bytes 163872 | tf_op jit(solution)/shard_map/ppermute | solution.py:65
  41.3 1.4 %third.1 = (f32[132,8,128]{2,1,0:T(8,128)S(1)}, f32[144,128]{1,0:T(8,128)S(1)}, f32[8,128]{1,0:T(8,128)S(1)}) custom-call(f32[320,128]{1,0:T(8,128)S(1)} %pad_maximum_fusion.mine_ref, f32[320,128]{1,0:T(8,128)S(1)} %collective-permute-done.9.other_ref, f32[8,128]{1,0:T(8,128)S(1)} %get-tuple-element.84.square_ref, bf16[1024,512]{1,0:T(8,128)(2,1)S(1)} %onehot.1.onehot_ref, ...), custom_call_target="tpu_custom_call" | custom-call | tf_op jit(solution)/shard_map/third/pallas_call | solution.py:540
  42.6 1.8 %collective-permute-start.10 = (f32[144,128]{1,0:T(8,128)S(1)}, f32[144,128]{1,0:T(8,128)S(1)}, u32[]{:S(2)}, u32[]{:S(2)}) collective-permute-start(f32[144,128]{1,0:T(8,128)S(1)} %get-tuple-element.89.mine_ref), channel_id=1, source_target_pairs={{0,1},{1,0},{2,3},{3,2},{4,5},{5,4},{6,7},{7,6},{8,9},{9,8},{10,11... | collective-permute-start | bytes 221192 | tf_op jit(solution)/shard_map/ppermute | solution.py:125
  44.5 2.6 %collective-permute-done.10.other_ref = f32[144,128]{1,0:T(8,128)S(1)} collective-permute-done((f32[144,128]{1,0:T(8,128)S(1)}, f32[144,128]{1,0:T(8,128)S(1)}, u32[]{:S(2)}, u32[]{:S(2)}) %collective-permute-start.10) | collective-permute-done | bytes 73760 | tf_op jit(solution)/shard_map/ppermute | solution.py:125
  47.1 0.1 fourth.1
  47.2 2.8 %collective-permute-start.11 = (f32[8,128]{1,0:T(8,128)S(1)}, f32[8,128]{1,0:T(8,128)S(1)}, u32[]{:S(2)}, u32[]{:S(2)}) collective-permute-start(f32[8,128]{1,0:T(8,128)S(1)} %get-tuple-element.93), channel_id=1, source_target_pairs={{0,16},{2,18},{4,20},{6,22},{8,24},{10,26},{12,28},{14,30},{16,0},... | collective-permute-start | bytes 12296 | tf_op jit(solution)/shard_map/ppermute | solution.py:93
  50.0 1.7 %last_smooth.1.refs_2_ = f32[8,128]{1,0:T(8,128)S(1)} custom-call(f32[132,8,128]{2,1,0:T(8,128)S(1)} %get-tuple-element.94.next_ref.refs_11_, f32[128,128]{1,0:T(8,128)S(1)} %slice.17.low_ref.high_ref, f32[128,128]{1,0:T(8,128)S(1)} %slice.17.low_ref.high_ref, f32[128,128]{1,0:T(8,128)S(1)} %broadcast_in_dim.12.damp_ref, ...), custom_call_target="tpu_custom_call" | custom-call | tf_op jit(solution)/shard_map/last_smooth/pallas_call | solution.py:550
  51.7 0.1 collective-permute-done.11
  51.8 1.7 %collective-permute-start.12 = (f32[8,128]{1,0:T(8,128)S(1)}, f32[8,128]{1,0:T(8,128)S(1)}, u32[]{:S(2)}, u32[]{:S(2)}) collective-permute-start(f32[8,128]{1,0:T(8,128)S(1)} %add.9), channel_id=1, source_target_pairs={{0,8},{2,10},{4,12},{6,14},{8,0},{10,2},{12,4},{14,6},{16,24},{18,... | collective-permute-start | bytes 12296 | tf_op jit(solution)/shard_map/ppermute | solution.py:93
  53.5 1.9 %collective-permute-done.12 = f32[8,128]{1,0:T(8,128)S(1)} collective-permute-done((f32[8,128]{1,0:T(8,128)S(1)}, f32[8,128]{1,0:T(8,128)S(1)}, u32[]{:S(2)}, u32[]{:S(2)}) %collective-permute-start.12) | collective-permute-done | bytes 4128 | tf_op jit(solution)/shard_map/ppermute | solution.py:93
  55.4 2.7 %collective-permute-start.13 = (f32[16,128]{1,0:T(8,128)S(1)}, f32[16,128]{1,0:T(8,128)S(1)}, u32[]{:S(2)}, u32[]{:S(2)}) collective-permute-start(f32[16,128]{1,0:T(8,128)S(1)} %pad_maximum_fusion.5), channel_id=1, source_target_pairs={{0,5},{1,4},{2,7},{3,6},{4,1},{5,0},{6,3},{7,2},{8,13},{9,12},{10,... | collective-permute-start | bytes 24584 | tf_op jit(solution)/shard_map/ppermute | solution.py:98
  58.1 1.9 %collective-permute-done.13 = f32[16,128]{1,0:T(8,128)S(1)} collective-permute-done((f32[16,128]{1,0:T(8,128)S(1)}, f32[16,128]{1,0:T(8,128)S(1)}, u32[]{:S(2)}, u32[]{:S(2)}) %collective-permute-start.13) | collective-permute-done | bytes 8224 | tf_op jit(solution)/shard_map/ppermute | solution.py:98
  60.0 0.0 collective-permute-start.14
  60.0 1.2 %collective-permute-done.14.refs_1_ = f32[8,128]{1,0:T(8,128)S(1)} collective-permute-done((f32[8,128]{1,0:T(8,128)S(1)}, f32[8,128]{1,0:T(8,128)S(1)}, u32[]{:S(2)}, u32[]{:S(2)}) %collective-permute-start.14) | collective-permute-done | bytes 4128 | tf_op jit(solution)/shard_map/ppermute | solution.py:100
  61.1 0.7 %end.1 = (f32[8,8,128]{2,1,0:T(8,128)}, f32[8,128]{1,0:T(8,128)}) custom-call(f32[8,128]{1,0:T(8,128)S(1)} %get-tuple-element.105.refs_0_, f32[8,128]{1,0:T(8,128)S(1)} %collective-permute-done.14.refs_1_, f32[8,128]{1,0:T(8,128)S(1)} %last_smooth.1.refs_2_, f32[8,128]{1,0:T(8,128)S(1)} %get-tuple-element.104.refs_3_, ...), custom_call_target="tpu_custom_call" | custom-call | tf_op jit(solution)/shard_map/end/pallas_call | solution.py:557
  (27 shorter events, 0.1 us)
Async XLA Ops:
  1.3 0.7 %copy-start.6 = (f32[1,1,32]{2,1,0:T(1,128)S(1)}, f32[1,1,32]{2,1,0:T(1,128)}, u32[]{:S(2)}) copy-start(f32[1,1,32]{2,1,0:T(1,128)} %param.10) | copy-start | bytes 388
  1.3 0.7 %copy-start.7 = (f32[96]{0:T(128)S(1)}, f32[96]{0:T(128)}, u32[]{:S(2)}) copy-start(f32[96]{0:T(128)} %table_ref.1) | copy-start | bytes 1156
  1.3 0.7 %copy-start.3 = (f32[1024]{0:T(1024)S(1)}, f32[1024]{0:T(1024)}, u32[]{:S(2)}) copy-start(f32[1024]{0:T(1024)} %param.14) | copy-start | bytes 12292
  1.3 0.7 %copy-start.2 = (s32[1024]{0:T(1024)S(1)}, s32[1024]{0:T(1024)}, u32[]{:S(2)}) copy-start(s32[1024]{0:T(1024)} %param.15) | copy-start | bytes 12292
  1.3 0.7 %copy-start.4 = (s32[1,1,32]{2,1,0:T(1,128)S(1)}, s32[1,1,32]{2,1,0:T(1,128)}, u32[]{:S(2)}) copy-start(s32[1,1,32]{2,1,0:T(1,128)} %param.12) | copy-start | bytes 388
  1.3 0.7 %copy-start.5 = (s32[1,1,32]{2,1,0:T(1,128)S(1)}, s32[1,1,32]{2,1,0:T(1,128)}, u32[]{:S(2)}) copy-start(s32[1,1,32]{2,1,0:T(1,128)} %param.11) | copy-start | bytes 388
  2.0 1.2 %copy-start = (bf16[1,1,32,128,128]{4,3,2,1,0:T(8,128)(2,1)S(1)}, bf16[1,1,32,128,128]{4,3,2,1,0:T(8,128)(2,1)}, u32[]{:S(2)}) copy-start(bf16[1,1,32,128,128]{4,3,2,1,0:T(8,128)(2,1)} %param.9) | copy-start | bytes 3145732
  3.2 16.9 %copy-start.1 = (bf16[1,1,32,128,128]{4,3,2,1,0:T(8,128)(2,1)S(1)}, bf16[1,1,32,128,128]{4,3,2,1,0:T(8,128)(2,1)}, u32[]{:S(2)}) copy-start(bf16[1,1,32,128,128]{4,3,2,1,0:T(8,128)(2,1)} %param.9) | copy-start | bytes 3145732
  4.2 4.1 %copy-start.8 = (f32[64]{0:T(128)S(1)}, f32[64]{0:T(128)}, u32[]{:S(2)}) copy-start(f32[64]{0:T(128)} %param.17) | copy-start | bytes 772
  4.3 5.9 %collective-permute-start = (f32[40,128]{1,0:T(8,128)S(1)}, f32[40,128]{1,0:T(8,128)S(1)}, u32[]{:S(2)}, u32[]{:S(2)}) collective-permute-start(f32[40,128]{1,0:T(8,128)S(1)} %get-tuple-element.53), channel_id=1, source_target_pairs={{0,16},{2,18},{4,20},{6,22},{8,24},{10,26},{12,28},{14,30},{16,0},... | collective-permute-start | bytes 61448 | tf_op jit(solution)/shard_map/ppermute | solution.py:65
  10.2 4.0 %collective-permute-start.1 = (f32[80,128]{1,0:T(8,128)S(1)}, f32[80,128]{1,0:T(8,128)S(1)}, u32[]{:S(2)}, u32[]{:S(2)}) collective-permute-start(f32[80,128]{1,0:T(8,128)S(1)} %pad_maximum_fusion.3), channel_id=1, source_target_pairs={{0,8},{2,10},{4,12},{6,14},{8,0},{10,2},{12,4},{14,6},{16,24},{18,... | collective-permute-start | bytes 122888 | tf_op jit(solution)/shard_map/ppermute | solution.py:65
  14.3 4.4 %collective-permute-start.2 = (f32[160,128]{1,0:T(8,128)S(1)}, f32[160,128]{1,0:T(8,128)S(1)}, u32[]{:S(2)}, u32[]{:S(2)}) collective-permute-start(f32[160,128]{1,0:T(8,128)S(1)} %pad_maximum_fusion.1), channel_id=1, source_target_pairs={{0,4},{2,6},{4,0},{6,2},{8,12},{10,14},{12,8},{14,10},{16,20},{18,... | collective-permute-start | bytes 245768 | tf_op jit(solution)/shard_map/ppermute | solution.py:65
  18.7 1.5 %collective-permute-start.3 = (f32[320,128]{1,0:T(8,128)S(1)}, f32[320,128]{1,0:T(8,128)S(1)}, u32[]{:S(2)}, u32[]{:S(2)}) collective-permute-start(f32[320,128]{1,0:T(8,128)S(1)} %constant_dynamic-update-slice_fusion.mine_ref), channel_id=1, source_target_pairs={{0,2},{2,0},{4,6},{6,4},{8,10},{10,8},{12,14},{14,12},{16,18},{18,... | collective-permute-start | bytes 491528 | tf_op jit(solution)/shard_map/ppermute | solution.py:65
  21.6 4.6 %collective-permute-start.4 = (f32[144,128]{1,0:T(8,128)S(1)}, f32[144,128]{1,0:T(8,128)S(1)}, u32[]{:S(2)}, u32[]{:S(2)}) collective-permute-start(f32[144,128]{1,0:T(8,128)S(1)} %get-tuple-element.57.mine_ref), channel_id=1, source_target_pairs={{0,1},{1,0},{2,3},{3,2},{4,5},{5,4},{6,7},{7,6},{8,9},{9,8},{10,11... | collective-permute-start | bytes 221192 | tf_op jit(solution)/shard_map/ppermute | solution.py:114
  26.5 4.7 %collective-permute-start.5 = (f32[40,128]{1,0:T(8,128)S(1)}, f32[40,128]{1,0:T(8,128)S(1)}, u32[]{:S(2)}, u32[]{:S(2)}) collective-permute-start(f32[40,128]{1,0:T(8,128)S(1)} %get-tuple-element.63), channel_id=1, source_target_pairs={{0,16},{2,18},{4,20},{6,22},{8,24},{10,26},{12,28},{14,30},{16,0},... | collective-permute-start | bytes 61448 | tf_op jit(solution)/shard_map/ppermute | solution.py:65
  29.4 1.9 %collective-permute-start.6 = (f32[128,128]{1,0:T(8,128)S(1)}, f32[128,128]{1,0:T(8,128)S(1)}, u32[]{:S(2)}, u32[]{:S(2)}) collective-permute-start(f32[128,128]{1,0:T(8,128)S(1)} %slice.16.low_ref.high_ref), channel_id=1, source_target_pairs={{0,2},{2,0},{4,6},{6,4},{8,10},{10,8},{12,14},{14,12},{16,18},{18,... | collective-permute-start | bytes 196616 | tf_op jit(solution)/shard_map/ppermute | solution.py:116
  31.3 4.1 %collective-permute-start.7 = (f32[80,128]{1,0:T(8,128)S(1)}, f32[80,128]{1,0:T(8,128)S(1)}, u32[]{:S(2)}, u32[]{:S(2)}) collective-permute-start(f32[80,128]{1,0:T(8,128)S(1)} %pad_maximum_fusion.4), channel_id=1, source_target_pairs={{0,8},{2,10},{4,12},{6,14},{8,0},{10,2},{12,4},{14,6},{16,24},{18,... | collective-permute-start | bytes 122888 | tf_op jit(solution)/shard_map/ppermute | solution.py:65
  35.3 4.4 %collective-permute-start.8 = (f32[160,128]{1,0:T(8,128)S(1)}, f32[160,128]{1,0:T(8,128)S(1)}, u32[]{:S(2)}, u32[]{:S(2)}) collective-permute-start(f32[160,128]{1,0:T(8,128)S(1)} %pad_maximum_fusion.2), channel_id=1, source_target_pairs={{0,4},{2,6},{4,0},{6,2},{8,12},{10,14},{12,8},{14,10},{16,20},{18,... | collective-permute-start | bytes 245768 | tf_op jit(solution)/shard_map/ppermute | solution.py:65
  39.8 1.5 %collective-permute-start.9 = (f32[320,128]{1,0:T(8,128)S(1)}, f32[320,128]{1,0:T(8,128)S(1)}, u32[]{:S(2)}, u32[]{:S(2)}) collective-permute-start(f32[320,128]{1,0:T(8,128)S(1)} %pad_maximum_fusion.mine_ref), channel_id=1, source_target_pairs={{0,2},{2,0},{4,6},{6,4},{8,10},{10,8},{12,14},{14,12},{16,18},{18,... | collective-permute-start | bytes 491528 | tf_op jit(solution)/shard_map/ppermute | solution.py:65
  42.6 4.4 %collective-permute-start.10 = (f32[144,128]{1,0:T(8,128)S(1)}, f32[144,128]{1,0:T(8,128)S(1)}, u32[]{:S(2)}, u32[]{:S(2)}) collective-permute-start(f32[144,128]{1,0:T(8,128)S(1)} %get-tuple-element.89.mine_ref), channel_id=1, source_target_pairs={{0,1},{1,0},{2,3},{3,2},{4,5},{5,4},{6,7},{7,6},{8,9},{9,8},{10,11... | collective-permute-start | bytes 221192 | tf_op jit(solution)/shard_map/ppermute | solution.py:125
  47.2 4.6 %collective-permute-start.11 = (f32[8,128]{1,0:T(8,128)S(1)}, f32[8,128]{1,0:T(8,128)S(1)}, u32[]{:S(2)}, u32[]{:S(2)}) collective-permute-start(f32[8,128]{1,0:T(8,128)S(1)} %get-tuple-element.93), channel_id=1, source_target_pairs={{0,16},{2,18},{4,20},{6,22},{8,24},{10,26},{12,28},{14,30},{16,0},... | collective-permute-start | bytes 12296 | tf_op jit(solution)/shard_map/ppermute | solution.py:93
  51.8 3.6 %collective-permute-start.12 = (f32[8,128]{1,0:T(8,128)S(1)}, f32[8,128]{1,0:T(8,128)S(1)}, u32[]{:S(2)}, u32[]{:S(2)}) collective-permute-start(f32[8,128]{1,0:T(8,128)S(1)} %add.9), channel_id=1, source_target_pairs={{0,8},{2,10},{4,12},{6,14},{8,0},{10,2},{12,4},{14,6},{16,24},{18,... | collective-permute-start | bytes 12296 | tf_op jit(solution)/shard_map/ppermute | solution.py:93
  55.4 4.5 %collective-permute-start.13 = (f32[16,128]{1,0:T(8,128)S(1)}, f32[16,128]{1,0:T(8,128)S(1)}, u32[]{:S(2)}, u32[]{:S(2)}) collective-permute-start(f32[16,128]{1,0:T(8,128)S(1)} %pad_maximum_fusion.5), channel_id=1, source_target_pairs={{0,5},{1,4},{2,7},{3,6},{4,1},{5,0},{6,3},{7,2},{8,13},{9,12},{10,... | collective-permute-start | bytes 24584 | tf_op jit(solution)/shard_map/ppermute | solution.py:98
  60.0 1.2 %collective-permute-start.14 = (f32[8,128]{1,0:T(8,128)S(1)}, f32[8,128]{1,0:T(8,128)S(1)}, u32[]{:S(2)}, u32[]{:S(2)}) collective-permute-start(f32[8,128]{1,0:T(8,128)S(1)} %get-tuple-element.105.refs_0_), channel_id=1, source_target_pairs={{0,2},{2,0},{4,6},{6,4},{8,10},{10,8},{12,14},{14,12},{16,18},{18,... | collective-permute-start | bytes 12296 | tf_op jit(solution)/shard_map/ppermute | solution.py:100

commit v3 on v2

--- a/solution.py
+++ b/solution.py
@@ -84,16 +84,17 @@
     return lax.psum(value, "vox") - value
 
 
-def last_sums(value, step_of):
+def last_sums(value, given, step_of):
     count, slabs = lax.axis_size("ray"), lax.axis_size("vox")
-    if slabs != 2 or count & (count - 1) or count < 8:
-        mine = step_of(None)
+    if slabs != 2 or count & (count - 1) or count < 16:
+        mine = step_of(given)
         return lax.psum(value, "ray"), mine, vox_others(mine)
     for step in hops(count)[:-2]:
         value = value + lax.ppermute(value, "ray", pairs_of(count, step))
-        if step == count // 2:
-            mine = step_of(None)
-            value, mine = lax.optimization_barrier((value, mine))
+        if step == count // 4:
+            given = step_of(given)
+        value, given = lax.optimization_barrier((value, given))
+    mine = given
     both = jnp.concatenate([value, mine], axis=0)
     both = lax.ppermute(both, ("ray", "vox"), [(i, i ^ 5) for i in range(2 * count)])
     value = value + both[:8]
@@ -121,11 +122,11 @@
 
 
 def next_halo(sums, field):
-    if lax.axis_size("vox") == 2:
+    if lax.axis_size("vox") == 2 and lax.axis_size("ray") % 2 == 0:
         other = lax.ppermute(sums, "vox", [(0, 1), (1, 0)])
-        column = other[RT + 8 :]
-        return other, (column, column)
-    return vox_others(sums), halo_of(field[PAD:-PAD, 0], field[PAD:-PAD, -1])
+        half = other[RT + 8 :]
+        return other, (half, lax.ppermute(half, "ray", pairs_of(lax.axis_size("ray"), 1))), True
+    return vox_others(sums), halo_of(field[PAD:-PAD, 0], field[PAD:-PAD, -1]), False
 
 
 def total(values):
@@ -147,14 +148,19 @@
         out_ref[pl.ds(k, 1), :] = jnp.sum(pick_ref[k] * product, axis=0, keepdims=True)
 
 
-def push_lines(lines, tiles_ref, pick_ref, slots):
+def push_lines(lines, tiles_ref, pick_ref, turned_ref, slots):
+    lane = lane_iota((RAY_TILE, LAT))
+    wide = jnp.concatenate([lines.astype(BF16), jnp.zeros((LAT - slots, LAT), BF16)], axis=0)
+    turned = jnp.zeros((RAY_TILE, LAT), F32)
+    for k in range(slots):
+        product = lax.dot_general(
+            tiles_ref[k], wide, (((1,), (1,)), ((), ())), preferred_element_type=F32
+        )
+        turned = jnp.where(lane == k, product, turned)
+    turned_ref[...] = turned.T
     rays = jnp.zeros((RT, RAY_TILE), F32)
     for k in range(slots):
-        line = jnp.broadcast_to(lines[k : k + 1], (RT, LAT)).astype(BF16)
-        product = lax.dot_general(
-            line, tiles_ref[k], (((1,), (1,)), ((), ())), preferred_element_type=F32
-        )
-        rays = rays + pick_ref[k] * product
+        rays = rays + pick_ref[k] * turned_ref[pl.ds(k, 1), :]
     return rays
 
 
@@ -197,8 +203,30 @@
     )
 
 
-def start_body(slots, row_ref, col_ref, scale_ref, count_ref, table_ref, receiver_ref, delays_ref, tiles_ref,
-               packet_ref, weight_ref, start_ref, pick_ref, own_ref):
+PULLS = 1
+
+
+def start_body(slots, count_ref, row_in, col_in, scale_in, table_in, receiver_in, delays_in, tiles_in,
+               packet_ref, weight_ref, start_ref, pick_ref, own_ref, tiles_ref,
+               row_ref, col_ref, scale_ref, table_ref, receiver_ref, delays_ref, sems):
+    part = slots // PULLS
+    copies = [
+        pltpu.make_async_copy(source, target, sems.at[j])
+        for j, (source, target) in enumerate([
+            (receiver_in, receiver_ref), (table_in, table_ref), (delays_in, delays_ref),
+            (scale_in, scale_ref), (row_in, row_ref), (col_in, col_ref),
+        ])
+    ]
+    pulls = [
+        pltpu.make_async_copy(
+            tiles_in.at[pl.ds(j * part, part)], tiles_ref.at[pl.ds(j * part, part)], sems.at[6 + j]
+        )
+        for j in range(PULLS)
+    ]
+    for copy in copies + pulls:
+        copy.start()
+    for copy in copies:
+        copy.wait()
     sub, lane = sub_iota(), lane_iota()
     receivers = receiver_ref[...]
     weight = jnp.zeros((RT, RAY_TILE), F32)
@@ -209,15 +237,20 @@
     start_ref[...] = start
     names = jnp.zeros((8, LAT), jnp.int32)
     for k in range(slots):
-        live = jnp.where(k < count_ref[0], scale_ref[k], 0.0)
+        live = jnp.where(k < count_ref[0, 0], scale_ref[k], 0.0)
         pick_ref[k] = jnp.where(sub == row_ref[k], live, 0.0)
         own_ref[pl.ds(k, 1), :] = jnp.full((1, LAT), col_ref[k], jnp.int32)
         names = jnp.where(lane == k, col_ref[k], names)
-    pull_lines(weight * start, tiles_ref, pick_ref, packet_ref, slots)
     square = total(start * start)
     packet_ref[slots:, :] = jnp.where(
         sub == 0, names.astype(F32), jnp.where(sub == 1, square, 0.0)
     )
+    rays = (weight * start).astype(BF16)
+    for j in range(PULLS):
+        pulls[j].wait()
+        for k in range(j * part, (j + 1) * part):
+            product = jnp.dot(rays, tiles_ref[k], preferred_element_type=F32)
+            packet_ref[pl.ds(k, 1), :] = jnp.sum(pick_ref[k] * product, axis=0, keepdims=True)
 
 
 def names_of(ref, slots):
@@ -239,15 +272,17 @@
     return [ref[b * (slots + 8) : b * (slots + 8) + slots, :] for b in range(blocks)]
 
 
-def padded_lines(ref_a, ref_b, slots):
+def padded_lines(ref, slots):
     per = LAT // slots
-    rows = []
-    for ref in (ref_a, ref_b):
-        lines = lines_in(ref, slots)
-        rows += lines
-        if len(lines) % per:
-            rows.append(jnp.zeros(((per - len(lines) % per) * slots, LAT), F32))
+    rows = lines_in(ref, slots)
+    if len(rows) % per:
+        rows.append(jnp.zeros(((per - len(rows) % per) * slots, LAT), F32))
     return jnp.concatenate(rows, axis=0)
+
+
+def found_lines(onehot, parts):
+    found = jnp.dot(onehot, parts, preferred_element_type=F32)
+    return found[:, :LAT] + found[:, LAT:]
 
 
 def rows_sum(ref, slots, at):
@@ -268,38 +303,46 @@
 
 
 def edge_of(field_ref, at):
-    return field_ref[PAD : PAIRS + PAD, at, :]
-
-
-def first_body(slots, mine_ref, other_ref, own_ref, pick_ref, tiles_ref,
-               field_ref, lines_ref, out_ref, left_ref, names_ref):
-    names = names_of(mine_ref, slots) + names_of(other_ref, slots)
+    flat = field_ref.reshape((PAIRS + 2 * PAD) * LON_DEV, LAT)
+    return flat[pl.ds(PAD * LON_DEV + at, PAIRS, stride=LON_DEV), :]
+
+
+def first_half_body(slots, mine_ref, own_ref, field_ref, lines_ref, names_ref):
+    names = names_of(mine_ref, slots)
     for j, piece in enumerate(names):
         names_ref[pl.ds(j, 1), :] = piece
-    parts = both_parts(padded_lines(mine_ref, other_ref, slots))
-
-    def take(ids):
-        found = jnp.dot(onehot_of(names, ids), parts, preferred_element_type=F32)
-        return found[:, :LAT] + found[:, LAT:]
-
-    lines = take(own_ref[...])
+    parts = both_parts(padded_lines(mine_ref, slots))
+    lines_ref[...] = found_lines(onehot_of(names, own_ref[...]), parts)
+    for first in range(0, LINES, CHUNK):
+        onehot = onehot_of(names, sub_iota((CHUNK, LAT)) + first)
+        piece = found_lines(onehot, parts).reshape(CHUNK // LON_DEV, LON_DEV, LAT)
+        field_ref[first // LON_DEV : (first + CHUNK) // LON_DEV] = piece
+
+
+def first_body(slots, other_ref, half_ref, half_lines_ref, mine_ref, own_ref, pick_ref, tiles_ref,
+               field_ref, lines_ref, out_ref, left_ref, names_ref, turned_ref):
+    names = names_of(other_ref, slots)
+    for j, piece in enumerate(names):
+        names_ref[pl.ds(j, 1), :] = piece
+    parts = both_parts(padded_lines(other_ref, slots))
+    lines = half_lines_ref[...] + found_lines(onehot_of(names, own_ref[...]), parts)
     lines_ref[...] = lines
-    rays = push_lines(lines, tiles_ref, pick_ref, slots)
+    rays = push_lines(lines, tiles_ref, pick_ref, turned_ref, slots)
     zeros = jnp.zeros((PAD, LON_DEV, LAT), F32)
     field_ref[:PAD] = zeros
     field_ref[PAIRS + PAD :] = zeros
     square = jnp.zeros((8, LAT), F32)
     for first in range(0, LINES, CHUNK):
-        piece = take(sub_iota((CHUNK, LAT)) + first).reshape(CHUNK // LON_DEV, LON_DEV, LAT)
-        at = first // LON_DEV + PAD
-        field_ref[at : at + CHUNK // LON_DEV] = piece
+        onehot = onehot_of(names, sub_iota((CHUNK, LAT)) + first)
+        count, pair = CHUNK // LON_DEV, first // LON_DEV
+        piece = found_lines(onehot, parts).reshape(count, LON_DEV, LAT) + half_ref[pair : pair + count]
+        field_ref[pair + PAD : pair + PAD + count] = piece
         square = square + jnp.sum(piece * piece, axis=0)
     out_ref[:RT, :] = rays
     out_ref[RT : RT + 8, :] = jnp.broadcast_to(total(square), (8, LAT))
-    odd = lax.axis_index("ray") % 2 == 1
-    high = jnp.where(odd, edge_of(field_ref, LON_DEV - 2), edge_of(field_ref, LON_DEV - 1))
-    low = jnp.where(odd, edge_of(field_ref, 1), edge_of(field_ref, 0))
-    out_ref[RT + 8 :, :] = jnp.where(lax.axis_index("vox") == 0, high, low)
+    odd = lax.axis_index("ray") % 2
+    at = jnp.where(lax.axis_index("vox") == 0, LON_DEV - 1 - odd, odd)
+    out_ref[RT + 8 :, :] = edge_of(field_ref, at)
     left_ref[...] = jnp.broadcast_to(rows_sum(mine_ref, slots, 1) + rows_sum(other_ref, slots, 1), (8, LAT))
 
 
@@ -358,10 +401,12 @@
     square_ref[...] = jnp.broadcast_to(total(square), (8, LAT))
 
 
-def onehot_body(names_ref, onehot_ref):
-    pieces = [names_ref[pl.ds(j, 1), :] for j in range(onehot_ref.shape[1] // LAT)]
-    for first in range(0, LINES, CHUNK):
-        onehot_ref[first : first + CHUNK, :] = onehot_of(pieces, sub_iota((CHUNK, LAT)) + first)
+def onehot_body(*refs):
+    names_refs, onehot_refs = refs[: len(refs) // 2], refs[len(refs) // 2 :]
+    for names_ref, onehot_ref in zip(names_refs, onehot_refs):
+        pieces = [names_ref[pl.ds(j, 1), :] for j in range(onehot_ref.shape[1] // LAT)]
+        for first in range(0, LINES, CHUNK):
+            onehot_ref[first : first + CHUNK, :] = onehot_of(pieces, sub_iota((CHUNK, LAT)) + first)
 
 
 def again_body(slots, col_ref, scaled_ref, far_ref, again_ref, lines_ref):
@@ -377,22 +422,28 @@
         lines_ref[pl.ds(k, 1), :] = again_ref[col // LON_DEV, pl.ds(col % LON_DEV, 1), :]
 
 
-def third_body(slots, mine_ref, other_ref, square_ref, onehot_ref, names_ref, own_ref, lines_ref,
-               again_lines_ref, again_ref, field_ref, norm_ref, pick_ref, tiles_ref,
-               next_ref, out_ref, shift_ref):
+def third_half_body(slots, mine_ref, onehot_ref, names_ref, own_ref, again_lines_ref, again_ref,
+                    half_ref, lines_ref):
+    parts = both_parts(padded_lines(mine_ref, slots))
+    names = [names_ref[pl.ds(j, 1), :] for j in range(onehot_ref.shape[1] // LAT)]
+    lines_ref[...] = found_lines(onehot_of(names, own_ref[...]), parts) + again_lines_ref[...]
+    for first in range(0, LINES, CHUNK):
+        count, pair = CHUNK // LON_DEV, first // LON_DEV
+        piece = found_lines(onehot_ref[first : first + CHUNK, :], parts).reshape(count, LON_DEV, LAT)
+        half_ref[pair : pair + count] = piece + again_ref[pair : pair + count]
+
+
+def third_body(slots, other_ref, half_ref, half_lines_ref, mine_ref, square_ref, onehot_ref, names_ref, own_ref,
+               lines_ref, field_ref, norm_ref, pick_ref, tiles_ref,
+               next_ref, out_ref, shift_ref, turned_ref):
     shift = jnp.broadcast_to(rows_sum(mine_ref, slots, 0) + rows_sum(other_ref, slots, 0), (8, LAT))
     shift_ref[...] = shift
     inverse = 1.0 / norm_ref[...]
     back = shift * inverse
-    parts = both_parts(padded_lines(mine_ref, other_ref, slots))
+    parts = both_parts(padded_lines(other_ref, slots))
     names = [names_ref[pl.ds(j, 1), :] for j in range(onehot_ref.shape[1] // LAT)]
-
-    def take(onehot):
-        found = jnp.dot(onehot, parts, preferred_element_type=F32)
-        return found[:, :LAT] + found[:, LAT:]
-
-    lines = take(onehot_of(names, own_ref[...])) + again_lines_ref[...] - lines_ref[...] * back[:1]
-    rays = push_lines(lines, tiles_ref, pick_ref, slots)
+    lines = found_lines(onehot_of(names, own_ref[...]), parts) + half_lines_ref[...] - lines_ref[...] * back[:1]
+    rays = push_lines(lines, tiles_ref, pick_ref, turned_ref, slots)
     zeros = jnp.zeros((PAD, LON_DEV, LAT), F32)
     next_ref[:PAD] = zeros
     next_ref[PAIRS + PAD :] = zeros
@@ -400,9 +451,9 @@
     cross = jnp.zeros((8, LAT), F32)
     for first in range(0, LINES, CHUNK):
         count, pair = CHUNK // LON_DEV, first // LON_DEV
-        piece = take(onehot_ref[first : first + CHUNK, :]).reshape(count, LON_DEV, LAT)
+        piece = found_lines(onehot_ref[first : first + CHUNK, :], parts).reshape(count, LON_DEV, LAT)
         base = field_ref[pair + PAD : pair + PAD + count]
-        piece = piece + again_ref[pair : pair + count] - base * back
+        piece = piece + half_ref[pair : pair + count] - base * back
         next_ref[pair + PAD : pair + PAD + count] = piece
         square = square + jnp.sum(piece * piece, axis=0)
         cross = cross + jnp.sum(piece * base, axis=0)
@@ -411,9 +462,9 @@
     out_ref[RT : RT + 8, :] = jnp.where(
         sub == 0, total(square), jnp.where(sub == 1, total(cross) * inverse, square_ref[...])
     )
-    out_ref[RT + 8 :, :] = jnp.where(
-        lax.axis_index("vox") == 0, edge_of(next_ref, LON_DEV - 1), edge_of(next_ref, 0)
-    )
+    edge = edge_of(next_ref, jnp.where(lax.axis_index("vox") == 0, LON_DEV - 1, 0))
+    half = PAIRS // 2
+    out_ref[RT + 8 :, :] = jnp.where(lax.axis_index("ray") % 2 == 0, edge[:half], edge[half:])
 
 
 def fourth_body(mine_ref, other_ref, shift_ref, weight_ref, rays_ref, image_ref,
@@ -434,12 +485,18 @@
     sum_ref[...] = jnp.broadcast_to(total(rays * rays), (8, LAT))
 
 
-def last_smooth_body(next_ref, low_ref, high_ref, damp_ref, smooth_ref, norm_ref, left_ref, rest_ref,
+def last_smooth_body(halves, next_ref, low_ref, high_ref, damp_ref, smooth_ref, norm_ref, left_ref, rest_ref,
                      square_ref, near_ref):
     sub, lane = sub_iota(), lane_iota()
     has_low, has_high = flags()
-    near_ref[0] = low_ref[...] * has_low
-    near_ref[1] = high_ref[...] * has_high
+    if halves:
+        odd, half = lax.axis_index("ray") % 2, PAIRS // 2
+        for ref, at in ((low_ref, odd), (high_ref, 1 - odd)):
+            near_ref[0, pl.ds(at * half, half), :] = ref[...] * has_low
+            near_ref[1, pl.ds(at * half, half), :] = ref[...] * has_high
+    else:
+        near_ref[0] = low_ref[...] * has_low
+        near_ref[1] = high_ref[...] * has_high
     norm, per_left = norm_ref[...], lax.rsqrt(left_ref[...])
     inverse = per_left / norm
     back = rest_ref[...] * inverse + norm * per_left
@@ -501,22 +558,37 @@
     packet = ((slots + 8, LAT), F32)
     damp = jnp.broadcast_to(jnp.repeat(smooth_scale, EPOCHS)[:, None], (PAIRS, LAT))
 
-    mine, weight, start, pick, own = local_call(
-        functools.partial(start_body, slots), "start", [SM] * 5 + [VM] * 3,
-        [packet, (held, F32), (held, F32), ((slots, RT, LAT), F32), ((slots, LAT), jnp.int32)],
-    )(tile_row[0, 0], col_index, tile_scale[0, 0], tile_count[0], receiver_weight,
-      ray_receiver.reshape(held), delays.reshape(held), block)
+    hbm = pl.BlockSpec(memory_space=pl.ANY)
+    table = receiver_weight.shape[0]
+    mine, weight, start, pick, own, block = local_call(
+        functools.partial(start_body, slots), "start", [SM] + [hbm] * 7,
+        [packet, (held, F32), (held, F32), ((slots, RT, LAT), F32), ((slots, LAT), jnp.int32),
+         (block.shape, BF16)],
+        [pltpu.SMEM((slots,), jnp.int32), pltpu.SMEM((slots,), jnp.int32), pltpu.SMEM((slots,), F32),
+         pltpu.SMEM((table,), F32), pltpu.VMEM(held, jnp.int32),
+         pltpu.VMEM(held, F32), pltpu.SemaphoreType.DMA((6 + PULLS,))],
+    )(tile_count, *(pltpu.with_memory_space_constraint(x, pltpu.MemorySpace.HBM) for x in (
+        tile_row[0, 0], col_index, tile_scale[0, 0], receiver_weight,
+        ray_receiver.reshape(held), delays.reshape(held), block)))
     near, far, damp = gather_rays(mine, (lambda _: damp,))
     per = LAT // slots
-    names_n = 2 * -(-(near.shape[0] // (slots + 8)) // per)
-
-    field, lines, sums, left0, names = local_call(
-        functools.partial(first_body, slots), "first", [VM] * 5,
-        [padded, ((slots, LAT), F32), ((RT + 8 + PAIRS, LAT), F32), row, ((names_n, LAT), jnp.int32)],
-    )(near, far, own, pick, block)
+    names_n = -(-(near.shape[0] // (slots + 8)) // per)
+    named = ((names_n, LAT), jnp.int32)
+    turned = pltpu.VMEM((RAY_TILE, LAT), F32)
+
+    half, half_lines, names_a = local_call(
+        functools.partial(first_half_body, slots), "first_half", [VM] * 2,
+        [slab, ((slots, LAT), F32), named],
+    )(near, own)
+    field, lines, sums, left0, names_b = local_call(
+        functools.partial(first_body, slots), "first", [VM] * 7,
+        [padded, ((slots, LAT), F32), ((RT + 8 + PAIRS, LAT), F32), row, named], [turned],
+    )(far, half, half_lines, near, own, pick, block)
     others, columns, swapped = first_halo(sums, field)
-    onehot = local_call(onehot_body, "onehot", [VM], [((LINES, names_n * LAT), BF16)])(names)[0]
-    others, onehot = lax.optimization_barrier((others, onehot))
+    onehots = local_call(
+        onehot_body, "onehot", [VM] * 2, [((LINES, names_n * LAT), BF16)] * 2,
+    )(names_a, names_b)
+    others, (onehot_a, onehot_b) = lax.optimization_barrier((others, onehots))
 
     mine, rays, image, norm0 = local_call(
         functools.partial(second_body, slots), "second", [VM] * 7, [packet, (held, F32), (held, F32), row],
@@ -537,21 +609,24 @@
     near, far, given = gather_rays(mine, (lambda _: columns, smooth_step, again_step))
     smooth, square, again, again_lines = given
 
+    half, half_lines = local_call(
+        functools.partial(third_half_body, slots), "third_half", [VM] * 6, [slab, ((slots, LAT), F32)],
+    )(near, onehot_a, names_a, own, again_lines, again)
     following, sums, shift = local_call(
         functools.partial(third_body, slots), "third", [VM] * 13,
-        [padded, ((RT + 8 + PAIRS, LAT), F32), row],
-    )(near, far, square, onehot, names, own, lines, again_lines, again, field, norm0, pick, block)
-    others, beside = next_halo(sums, following)
+        [padded, ((RT + 8 + PAIRS // 2, LAT), F32), row], [turned],
+    )(far, half, half_lines, near, square, onehot_b, names_b, own, lines, field, norm0, pick, block)
+    others, beside, halves = next_halo(sums, following)
     last_rays, left1, rest, norm1, ray_square = local_call(
         fourth_body, "fourth", [VM] * 6, [(held, F32), row, row, row, row],
     )(sums, others, shift, weight, rays, image)
 
-    def last_step(_):
+    def last_step(beside):
         return local_call(
-            last_smooth_body, "last_smooth", [VM] * 8, [row], [pltpu.VMEM((2, PAIRS, LAT), F32)],
+            functools.partial(last_smooth_body, halves), "last_smooth", [VM] * 8, [row], [pltpu.VMEM((2, PAIRS, LAT), F32)],
         )(following, *beside, damp, smooth, norm1, left1, rest)[0]
 
-    shares = last_sums(ray_square, last_step)
+    shares = last_sums(ray_square, beside, last_step)
 
     share = PAIRS // rays_n
     density, rays_out = local_call(

time: 62 us -> 59.5 us (0.960)
  local copies, waits for them, and re-layouts: 2.23 us -> 0.32 us
  waiting for transfers between devices: 21.8 us -> 20.6 us
    unnamed x20 -> x6, local copies, waits for them, and re-layouts: 1.93 us -> 0.02 us
    pallas_call x4 -> x6, Pallas kernels: 4.24 us -> 5.18 us  [the longest x1 1.72 us: on_device(): local_call(functools.partial(start_body, slots), 'start', [SM] + [hbm] *...]
    ppermute x8, waiting for transfers between devices: 11.8 us -> 11.1 us  [gather_rays(): other = lax.ppermute(block, 'ray', pairs_of(count, step))]
  transfers between devices with their start and end apart: 15 -> 16, of which waited for: 14 -> 14; matrix products, arithmetic and copies ran while one was open for 0% -> 0% of each run, Pallas kernels for 9% -> 11%
where the time goes in v3:
time: 59.5 us; the launch traced here: 59.4 us
  starting transfers between devices  25.7 us (43%)
  waiting for transfers between devices  20.6 us (35%)
  Pallas kernels  11.3 us (19%)
  between operations  1.41 us (2%)
    ppermute x8, starting transfers between devices, gather_rays(): other = lax.ppermute(block, 'ray', pairs_of(count, step))  14.5 us
    ppermute x8, waiting for transfers between devices, gather_rays(): other = lax.ppermute(block, 'ray', pairs_of(count, step))  11.1 us
    ppermute x2, starting transfers between devices, last_sums(): value = value + lax.ppermute(value, 'ray', pairs_of(count, step))  4.58 us
    ppermute x1, starting transfers between devices, last_sums(): lax.ppermute(both, ('ray', 'vox'), [(i, i ^ 5) for i in range(2 * count)])  2.71 us
    ppermute x1, waiting for transfers between devices, first_halo(): other = lax.ppermute(sums, 'vox', [(0, 1), (1, 0)])  2.34 us
    ppermute x1, waiting for transfers between devices, next_halo(): other = lax.ppermute(sums, 'vox', [(0, 1), (1, 0)])  2.21 us
    pallas_call x1, Pallas kernels, again_step(): local_call(functools.partial(again_body, slots), 'again', [SM] + [VM] * 2...  2.17 us
    ppermute x1, starting transfers between devices, first_halo(): other = lax.ppermute(sums, 'vox', [(0, 1), (1, 0)])  2.02 us
  transfers between devices with their start and end apart: 16, of which 14 were waited for; matrix products, arithmetic and copies ran while one was open for 0% of the time, Pallas kernels for 11%

profile of v3, /device:TPU:0, one launch (start us, length us, event | category | flops | bytes accessed | tf_op | source)
XLA Modules:
  0.0 59.4 jit_solution(13567875506270686333)
XLA Ops:
  1.3 1.7 %start.1 = (f32[40,128]{1,0:T(8,128)S(1)}, f32[8,128]{1,0:T(8,128)S(1)}, f32[8,128]{1,0:T(8,128)S(1)}, f32[32,8,128]{2,1,0:T(8,128)S(1)}, s32[32,128]{1,0:T(8,128)S(1)}, /*index=5*/bf16[32,128,128]{2,1,0:T(8,128)(2,1)S(1)}) custom-call(s32[1,1]{1,0:T(1,128)S(6)} %copy.13.count_ref, s32[32]{0:T(128)} %bitcast.13, s32[32]{0:T(128)} %bitcast.8, f32[32]{0:T(128)} %bitcast.14, ...), custom_call_target="tpu_custom_call" | custom-call | tf_op jit(solution)/shard_map/start/pallas_call | solution.py:563
  3.0 0.0 copy-start.1
  3.0 4.1 %collective-permute-start = (f32[40,128]{1,0:T(8,128)S(1)}, f32[40,128]{1,0:T(8,128)S(1)}, u32[]{:S(2)}, u32[]{:S(2)}) collective-permute-start(f32[40,128]{1,0:T(8,128)S(1)} %get-tuple-element.65), channel_id=1, source_target_pairs={{0,16},{2,18},{4,20},{6,22},{8,24},{10,26},{12,28},{14,30},{16,0},... | collective-permute-start | bytes 61448 | tf_op jit(solution)/shard_map/ppermute | solution.py:65
  7.1 0.1 broadcast_in_dim.10
  7.2 0.1 broadcast_in_dim.11
  7.3 1.6 %collective-permute-done = f32[40,128]{1,0:T(8,128)S(1)} collective-permute-done((f32[40,128]{1,0:T(8,128)S(1)}, f32[40,128]{1,0:T(8,128)S(1)}, u32[]{:S(2)}, u32[]{:S(2)}) %collective-permute-start) | collective-permute-done | bytes 20512 | tf_op jit(solution)/shard_map/ppermute | solution.py:65
  8.9 0.1 broadcast_in_dim.12.damp_ref
  9.0 1.9 %collective-permute-start.1 = (f32[80,128]{1,0:T(8,128)S(1)}, f32[80,128]{1,0:T(8,128)S(1)}, u32[]{:S(2)}, u32[]{:S(2)}) collective-permute-start(f32[80,128]{1,0:T(8,128)S(1)} %pad_maximum_fusion.3), channel_id=1, source_target_pairs={{0,8},{2,10},{4,12},{6,14},{8,0},{10,2},{12,4},{14,6},{16,24},{18,... | collective-permute-start | bytes 122888 | tf_op jit(solution)/shard_map/ppermute | solution.py:65
  10.9 2.1 %collective-permute-done.1 = f32[80,128]{1,0:T(8,128)S(1)} collective-permute-done((f32[80,128]{1,0:T(8,128)S(1)}, f32[80,128]{1,0:T(8,128)S(1)}, u32[]{:S(2)}, u32[]{:S(2)}) %collective-permute-start.1) | collective-permute-done | bytes 40992 | tf_op jit(solution)/shard_map/ppermute | solution.py:65
  13.0 1.9 %collective-permute-start.2 = (f32[160,128]{1,0:T(8,128)S(1)}, f32[160,128]{1,0:T(8,128)S(1)}, u32[]{:S(2)}, u32[]{:S(2)}) collective-permute-start(f32[160,128]{1,0:T(8,128)S(1)} %pad_maximum_fusion.1), channel_id=1, source_target_pairs={{0,4},{2,6},{4,0},{6,2},{8,12},{10,14},{12,8},{14,10},{16,20},{18,... | collective-permute-start | bytes 245768 | tf_op jit(solution)/shard_map/ppermute | solution.py:65
  14.9 2.5 %collective-permute-done.2 = f32[160,128]{1,0:T(8,128)S(1)} collective-permute-done((f32[160,128]{1,0:T(8,128)S(1)}, f32[160,128]{1,0:T(8,128)S(1)}, u32[]{:S(2)}, u32[]{:S(2)}) %collective-permute-start.2) | collective-permute-done | bytes 81952 | tf_op jit(solution)/shard_map/ppermute | solution.py:65
  17.5 0.1 collective-permute-start.3
  17.5 0.4 first_half.1
  17.9 1.0 %collective-permute-done.3.other_ref = f32[320,128]{1,0:T(8,128)S(1)} collective-permute-done((f32[320,128]{1,0:T(8,128)S(1)}, f32[320,128]{1,0:T(8,128)S(1)}, u32[]{:S(2)}, u32[]{:S(2)}) %collective-permute-start.3) | collective-permute-done | bytes 163872 | tf_op jit(solution)/shard_map/ppermute | solution.py:65
  18.9 0.9 %first.1 = (f32[132,8,128]{2,1,0:T(8,128)S(1)}, f32[32,128]{1,0:T(8,128)S(1)}, f32[144,128]{1,0:T(8,128)S(1)}, f32[8,128]{1,0:T(8,128)S(1)}, s32[2,128]{1,0:T(2,128)S(1)}) custom-call(f32[320,128]{1,0:T(8,128)S(1)} %collective-permute-done.3.other_ref, f32[128,8,128]{2,1,0:T(8,128)S(1)} %get-tuple-element.68.half_ref, ...), custom_call_target="tpu_custom_call" | custom-call | tf_op jit(solution)/shard_map/first/pallas_call | solution.py:583
  19.8 2.0 %collective-permute-start.4 = (f32[144,128]{1,0:T(8,128)S(1)}, f32[144,128]{1,0:T(8,128)S(1)}, u32[]{:S(2)}, u32[]{:S(2)}) collective-permute-start(f32[144,128]{1,0:T(8,128)S(1)} %get-tuple-element.72.mine_ref), channel_id=1, source_target_pairs={{0,1},{1,0},{2,3},{3,2},{4,5},{5,4},{6,7},{7,6},{8,9},{9,8},{10,11... | collective-permute-start | bytes 221192 | tf_op jit(solution)/shard_map/ppermute | solution.py:115
  21.9 0.2 onehot.1
  22.1 2.3 %collective-permute-done.4.other_ref = f32[144,128]{1,0:T(8,128)S(1)} collective-permute-done((f32[144,128]{1,0:T(8,128)S(1)}, f32[144,128]{1,0:T(8,128)S(1)}, u32[]{:S(2)}, u32[]{:S(2)}) %collective-permute-start.4) | collective-permute-done | bytes 73760 | tf_op jit(solution)/shard_map/ppermute | solution.py:115
  24.4 0.4 second.1
  24.8 2.8 %collective-permute-start.5 = (f32[40,128]{1,0:T(8,128)S(1)}, f32[40,128]{1,0:T(8,128)S(1)}, u32[]{:S(2)}, u32[]{:S(2)}) collective-permute-start(f32[40,128]{1,0:T(8,128)S(1)} %get-tuple-element.81), channel_id=1, source_target_pairs={{0,16},{2,18},{4,20},{6,22},{8,24},{10,26},{12,28},{14,30},{16,0},... | collective-permute-start | bytes 61448 | tf_op jit(solution)/shard_map/ppermute | solution.py:65
  27.6 0.0 collective-permute-start.6
  27.7 1.9 %collective-permute-done.5 = f32[40,128]{1,0:T(8,128)S(1)} collective-permute-done((f32[40,128]{1,0:T(8,128)S(1)}, f32[40,128]{1,0:T(8,128)S(1)}, u32[]{:S(2)}, u32[]{:S(2)}) %collective-permute-start.5) | collective-permute-done | bytes 20512 | tf_op jit(solution)/shard_map/ppermute | solution.py:65
  29.6 0.0 collective-permute-done.6.low2_ref.high2_ref
  29.6 1.8 %collective-permute-start.7 = (f32[80,128]{1,0:T(8,128)S(1)}, f32[80,128]{1,0:T(8,128)S(1)}, u32[]{:S(2)}, u32[]{:S(2)}) collective-permute-start(f32[80,128]{1,0:T(8,128)S(1)} %pad_maximum_fusion.4), channel_id=1, source_target_pairs={{0,8},{2,10},{4,12},{6,14},{8,0},{10,2},{12,4},{14,6},{16,24},{18,... | collective-permute-start | bytes 122888 | tf_op jit(solution)/shard_map/ppermute | solution.py:65
  31.4 1.8 %smooth.1 = (f32[128,8,128]{2,1,0:T(8,128)S(1)}, f32[132,8,128]{2,1,0:T(8,128)S(1)}, f32[2,128,128]{2,1,0:T(8,128)S(1)}, f32[8,128]{1,0:T(8,128)S(1)}) custom-call(f32[132,8,128]{2,1,0:T(8,128)S(1)} %get-tuple-element.83.field_ref.refs_10_, f32[128,128]{1,0:T(8,128)S(1)} %slice.16.low_ref.high_ref, f32[128,128]{1,0:T(8,128)S(1)} %collective-permute-done.6.low2_ref.high2_ref, ...), custom_call_target="tpu_custom_call" | custom-call | tf_op jit(solution)/shard_map/smooth/pallas_call | solution.py:597
  33.2 0.5 collective-permute-done.7
  33.6 1.8 %collective-permute-start.8 = (f32[160,128]{1,0:T(8,128)S(1)}, f32[160,128]{1,0:T(8,128)S(1)}, u32[]{:S(2)}, u32[]{:S(2)}) collective-permute-start(f32[160,128]{1,0:T(8,128)S(1)} %pad_maximum_fusion.2), channel_id=1, source_target_pairs={{0,4},{2,6},{4,0},{6,2},{8,12},{10,14},{12,8},{14,10},{16,20},{18,... | collective-permute-start | bytes 245768 | tf_op jit(solution)/shard_map/ppermute | solution.py:65
  35.5 2.2 %again.1 = (f32[128,8,128]{2,1,0:T(8,128)S(1)}, f32[32,128]{1,0:T(8,128)S(1)}) custom-call(s32[32]{0:T(128)S(1)} %bitcast.9, f32[132,8,128]{2,1,0:T(8,128)S(1)} %get-tuple-element.97.scaled_ref, f32[2,128,128]{2,1,0:T(8,128)S(1)} %get-tuple-element.98.far_ref), custom_call_target="tpu_custom_call" | custom-call | tf_op jit(solution)/shard_map/again/pallas_call | solution.py:604
  37.6 0.5 collective-permute-done.8
  38.2 0.1 collective-permute-start.9
  38.2 0.3 third_half.1
  38.6 1.1 %collective-permute-done.9.other_ref = f32[320,128]{1,0:T(8,128)S(1)} collective-permute-done((f32[320,128]{1,0:T(8,128)S(1)}, f32[320,128]{1,0:T(8,128)S(1)}, u32[]{:S(2)}, u32[]{:S(2)}) %collective-permute-start.9) | collective-permute-done | bytes 163872 | tf_op jit(solution)/shard_map/ppermute | solution.py:65
  39.6 0.9 %third.1 = (f32[132,8,128]{2,1,0:T(8,128)S(1)}, f32[80,128]{1,0:T(8,128)S(1)}, f32[8,128]{1,0:T(8,128)S(1)}) custom-call(f32[320,128]{1,0:T(8,128)S(1)} %collective-permute-done.9.other_ref, f32[128,8,128]{2,1,0:T(8,128)S(1)} %get-tuple-element.105.half_ref, f32[32,128]{1,0:T(8,128)S(1)} %get-tuple-element.106.half_lines_ref, ...), custom_call_target="tpu_custom_call" | custom-call | tf_op jit(solution)/shard_map/third/pallas_call | solution.py:615
  40.5 1.9 %collective-permute-start.10 = (f32[80,128]{1,0:T(8,128)S(1)}, f32[80,128]{1,0:T(8,128)S(1)}, u32[]{:S(2)}, u32[]{:S(2)}) collective-permute-start(f32[80,128]{1,0:T(8,128)S(1)} %get-tuple-element.110.mine_ref), channel_id=1, source_target_pairs={{0,1},{1,0},{2,3},{3,2},{4,5},{5,4},{6,7},{7,6},{8,9},{9,8},{10,11... | collective-permute-start | bytes 122888 | tf_op jit(solution)/shard_map/ppermute | solution.py:126
  42.4 2.2 %collective-permute-done.10.other_ref = f32[80,128]{1,0:T(8,128)S(1)} collective-permute-done((f32[80,128]{1,0:T(8,128)S(1)}, f32[80,128]{1,0:T(8,128)S(1)}, u32[]{:S(2)}, u32[]{:S(2)}) %collective-permute-start.10) | collective-permute-done | bytes 40992 | tf_op jit(solution)/shard_map/ppermute | solution.py:126
  44.6 0.0 collective-permute-start.12
  44.6 0.1 fourth.1
  44.8 2.8 %collective-permute-start.11 = (f32[8,128]{1,0:T(8,128)S(1)}, f32[8,128]{1,0:T(8,128)S(1)}, u32[]{:S(2)}, u32[]{:S(2)}) collective-permute-start(f32[8,128]{1,0:T(8,128)S(1)} %get-tuple-element.114), channel_id=1, source_target_pairs={{0,16},{2,18},{4,20},{6,22},{8,24},{10,26},{12,28},{14,30},{16,0},... | collective-permute-start | bytes 12296 | tf_op jit(solution)/shard_map/ppermute | solution.py:93
  47.6 1.7 %collective-permute-done.11 = f32[8,128]{1,0:T(8,128)S(1)} collective-permute-done((f32[8,128]{1,0:T(8,128)S(1)}, f32[8,128]{1,0:T(8,128)S(1)}, u32[]{:S(2)}, u32[]{:S(2)}) %collective-permute-start.11) | collective-permute-done | bytes 4128 | tf_op jit(solution)/shard_map/ppermute | solution.py:93
  49.3 0.0 collective-permute-done.12.high_ref
  49.3 1.7 %collective-permute-start.13 = (f32[8,128]{1,0:T(8,128)S(1)}, f32[8,128]{1,0:T(8,128)S(1)}, u32[]{:S(2)}, u32[]{:S(2)}) collective-permute-start(f32[8,128]{1,0:T(8,128)S(1)} %add.9), channel_id=1, source_target_pairs={{0,8},{2,10},{4,12},{6,14},{8,0},{10,2},{12,4},{14,6},{16,24},{18,... | collective-permute-start | bytes 12296 | tf_op jit(solution)/shard_map/ppermute | solution.py:93
  51.1 1.7 %last_smooth.1.refs_2_ = f32[8,128]{1,0:T(8,128)S(1)} custom-call(f32[132,8,128]{2,1,0:T(8,128)S(1)} %get-tuple-element.116.next_ref.refs_11_, f32[64,128]{1,0:T(8,128)S(1)} %slice.17.low_ref, f32[64,128]{1,0:T(8,128)S(1)} %collective-permute-done.12.high_ref, f32[128,128]{1,0:T(8,128)S(1)} %broadcast_in_dim.12.damp_ref, ...), custom_call_target="tpu_custom_call" | custom-call | tf_op jit(solution)/shard_map/last_smooth/pallas_call | solution.py:625
  52.8 0.2 collective-permute-done.13
  53.0 2.7 %collective-permute-start.14 = (f32[16,128]{1,0:T(8,128)S(1)}, f32[16,128]{1,0:T(8,128)S(1)}, u32[]{:S(2)}, u32[]{:S(2)}) collective-permute-start(f32[16,128]{1,0:T(8,128)S(1)} %pad_maximum_fusion.5), channel_id=1, source_target_pairs={{0,5},{1,4},{2,7},{3,6},{4,1},{5,0},{6,3},{7,2},{8,13},{9,12},{10,... | collective-permute-start | bytes 24584 | tf_op jit(solution)/shard_map/ppermute | solution.py:99
  55.7 1.8 %collective-permute-done.14 = f32[16,128]{1,0:T(8,128)S(1)} collective-permute-done((f32[16,128]{1,0:T(8,128)S(1)}, f32[16,128]{1,0:T(8,128)S(1)}, u32[]{:S(2)}, u32[]{:S(2)}) %collective-permute-start.14) | collective-permute-done | bytes 8224 | tf_op jit(solution)/shard_map/ppermute | solution.py:99
  57.5 0.0 collective-permute-start.15
  57.5 1.2 %collective-permute-done.15.refs_1_ = f32[8,128]{1,0:T(8,128)S(1)} collective-permute-done((f32[8,128]{1,0:T(8,128)S(1)}, f32[8,128]{1,0:T(8,128)S(1)}, u32[]{:S(2)}, u32[]{:S(2)}) %collective-permute-start.15) | collective-permute-done | bytes 4128 | tf_op jit(solution)/shard_map/ppermute | solution.py:101
  58.7 0.7 %end.1 = (f32[8,8,128]{2,1,0:T(8,128)}, f32[8,128]{1,0:T(8,128)}) custom-call(f32[8,128]{1,0:T(8,128)S(1)} %get-tuple-element.129.refs_0_, f32[8,128]{1,0:T(8,128)S(1)} %collective-permute-done.15.refs_1_, f32[8,128]{1,0:T(8,128)S(1)} %last_smooth.1.refs_2_, f32[8,128]{1,0:T(8,128)S(1)} %get-tuple-element.128.refs_3_, ...), custom_call_target="tpu_custom_call" | custom-call | tf_op jit(solution)/shard_map/end/pallas_call | solution.py:632
  (17 shorter events, 0.1 us)
Async XLA Ops:
  3.0 4.1 %copy-start.1 = (f32[64]{0:T(128)S(1)}, f32[64]{0:T(128)}, u32[]{:S(2)}) copy-start(f32[64]{0:T(128)} %param.17) | copy-start | bytes 772
  3.0 5.9 %collective-permute-start = (f32[40,128]{1,0:T(8,128)S(1)}, f32[40,128]{1,0:T(8,128)S(1)}, u32[]{:S(2)}, u32[]{:S(2)}) collective-permute-start(f32[40,128]{1,0:T(8,128)S(1)} %get-tuple-element.65), channel_id=1, source_target_pairs={{0,16},{2,18},{4,20},{6,22},{8,24},{10,26},{12,28},{14,30},{16,0},... | collective-permute-start | bytes 61448 | tf_op jit(solution)/shard_map/ppermute | solution.py:65
  9.0 4.0 %collective-permute-start.1 = (f32[80,128]{1,0:T(8,128)S(1)}, f32[80,128]{1,0:T(8,128)S(1)}, u32[]{:S(2)}, u32[]{:S(2)}) collective-permute-start(f32[80,128]{1,0:T(8,128)S(1)} %pad_maximum_fusion.3), channel_id=1, source_target_pairs={{0,8},{2,10},{4,12},{6,14},{8,0},{10,2},{12,4},{14,6},{16,24},{18,... | collective-permute-start | bytes 122888 | tf_op jit(solution)/shard_map/ppermute | solution.py:65
  13.0 4.4 %collective-permute-start.2 = (f32[160,128]{1,0:T(8,128)S(1)}, f32[160,128]{1,0:T(8,128)S(1)}, u32[]{:S(2)}, u32[]{:S(2)}) collective-permute-start(f32[160,128]{1,0:T(8,128)S(1)} %pad_maximum_fusion.1), channel_id=1, source_target_pairs={{0,4},{2,6},{4,0},{6,2},{8,12},{10,14},{12,8},{14,10},{16,20},{18,... | collective-permute-start | bytes 245768 | tf_op jit(solution)/shard_map/ppermute | solution.py:65
  17.5 1.5 %collective-permute-start.3 = (f32[320,128]{1,0:T(8,128)S(1)}, f32[320,128]{1,0:T(8,128)S(1)}, u32[]{:S(2)}, u32[]{:S(2)}) collective-permute-start(f32[320,128]{1,0:T(8,128)S(1)} %constant_dynamic-update-slice_fusion.mine_ref), channel_id=1, source_target_pairs={{0,2},{2,0},{4,6},{6,4},{8,10},{10,8},{12,14},{14,12},{16,18},{18,... | collective-permute-start | bytes 491528 | tf_op jit(solution)/shard_map/ppermute | solution.py:65
  19.8 4.6 %collective-permute-start.4 = (f32[144,128]{1,0:T(8,128)S(1)}, f32[144,128]{1,0:T(8,128)S(1)}, u32[]{:S(2)}, u32[]{:S(2)}) collective-permute-start(f32[144,128]{1,0:T(8,128)S(1)} %get-tuple-element.72.mine_ref), channel_id=1, source_target_pairs={{0,1},{1,0},{2,3},{3,2},{4,5},{5,4},{6,7},{7,6},{8,9},{9,8},{10,11... | collective-permute-start | bytes 221192 | tf_op jit(solution)/shard_map/ppermute | solution.py:115
  24.8 4.7 %collective-permute-start.5 = (f32[40,128]{1,0:T(8,128)S(1)}, f32[40,128]{1,0:T(8,128)S(1)}, u32[]{:S(2)}, u32[]{:S(2)}) collective-permute-start(f32[40,128]{1,0:T(8,128)S(1)} %get-tuple-element.81), channel_id=1, source_target_pairs={{0,16},{2,18},{4,20},{6,22},{8,24},{10,26},{12,28},{14,30},{16,0},... | collective-permute-start | bytes 61448 | tf_op jit(solution)/shard_map/ppermute | solution.py:65
  27.6 1.9 %collective-permute-start.6 = (f32[128,128]{1,0:T(8,128)S(1)}, f32[128,128]{1,0:T(8,128)S(1)}, u32[]{:S(2)}, u32[]{:S(2)}) collective-permute-start(f32[128,128]{1,0:T(8,128)S(1)} %slice.16.low_ref.high_ref), channel_id=1, source_target_pairs={{0,2},{2,0},{4,6},{6,4},{8,10},{10,8},{12,14},{14,12},{16,18},{18,... | collective-permute-start | bytes 196616 | tf_op jit(solution)/shard_map/ppermute | solution.py:117
  29.6 4.1 %collective-permute-start.7 = (f32[80,128]{1,0:T(8,128)S(1)}, f32[80,128]{1,0:T(8,128)S(1)}, u32[]{:S(2)}, u32[]{:S(2)}) collective-permute-start(f32[80,128]{1,0:T(8,128)S(1)} %pad_maximum_fusion.4), channel_id=1, source_target_pairs={{0,8},{2,10},{4,12},{6,14},{8,0},{10,2},{12,4},{14,6},{16,24},{18,... | collective-permute-start | bytes 122888 | tf_op jit(solution)/shard_map/ppermute | solution.py:65
  33.6 1.8 %copy-start = (s32[1,1,32]{2,1,0:T(1,128)S(1)}, s32[1,1,32]{2,1,0:T(1,128)}, u32[]{:S(2)}) copy-start(s32[1,1,32]{2,1,0:T(1,128)} %param.12) | copy-start | bytes 388
  33.6 4.5 %collective-permute-start.8 = (f32[160,128]{1,0:T(8,128)S(1)}, f32[160,128]{1,0:T(8,128)S(1)}, u32[]{:S(2)}, u32[]{:S(2)}) collective-permute-start(f32[160,128]{1,0:T(8,128)S(1)} %pad_maximum_fusion.2), channel_id=1, source_target_pairs={{0,4},{2,6},{4,0},{6,2},{8,12},{10,14},{12,8},{14,10},{16,20},{18,... | collective-permute-start | bytes 245768 | tf_op jit(solution)/shard_map/ppermute | solution.py:65
  38.2 1.5 %collective-permute-start.9 = (f32[320,128]{1,0:T(8,128)S(1)}, f32[320,128]{1,0:T(8,128)S(1)}, u32[]{:S(2)}, u32[]{:S(2)}) collective-permute-start(f32[320,128]{1,0:T(8,128)S(1)} %pad_maximum_fusion.mine_ref), channel_id=1, source_target_pairs={{0,2},{2,0},{4,6},{6,4},{8,10},{10,8},{12,14},{14,12},{16,18},{18,... | collective-permute-start | bytes 491528 | tf_op jit(solution)/shard_map/ppermute | solution.py:65
  40.5 4.1 %collective-permute-start.10 = (f32[80,128]{1,0:T(8,128)S(1)}, f32[80,128]{1,0:T(8,128)S(1)}, u32[]{:S(2)}, u32[]{:S(2)}) collective-permute-start(f32[80,128]{1,0:T(8,128)S(1)} %get-tuple-element.110.mine_ref), channel_id=1, source_target_pairs={{0,1},{1,0},{2,3},{3,2},{4,5},{5,4},{6,7},{7,6},{8,9},{9,8},{10,11... | collective-permute-start | bytes 122888 | tf_op jit(solution)/shard_map/ppermute | solution.py:126
  44.6 4.7 %collective-permute-start.12 = (f32[64,128]{1,0:T(8,128)S(1)}, f32[64,128]{1,0:T(8,128)S(1)}, u32[]{:S(2)}, u32[]{:S(2)}) collective-permute-start(f32[64,128]{1,0:T(8,128)S(1)} %slice.17.low_ref), channel_id=1, source_target_pairs={{0,2},{2,0},{4,6},{6,4},{8,10},{10,8},{12,14},{14,12},{16,18},{18,... | collective-permute-start | bytes 98312 | tf_op jit(solution)/shard_map/ppermute | solution.py:128
  44.8 4.6 %collective-permute-start.11 = (f32[8,128]{1,0:T(8,128)S(1)}, f32[8,128]{1,0:T(8,128)S(1)}, u32[]{:S(2)}, u32[]{:S(2)}) collective-permute-start(f32[8,128]{1,0:T(8,128)S(1)} %get-tuple-element.114), channel_id=1, source_target_pairs={{0,16},{2,18},{4,20},{6,22},{8,24},{10,26},{12,28},{14,30},{16,0},... | collective-permute-start | bytes 12296 | tf_op jit(solution)/shard_map/ppermute | solution.py:93
  49.3 3.6 %collective-permute-start.13 = (f32[8,128]{1,0:T(8,128)S(1)}, f32[8,128]{1,0:T(8,128)S(1)}, u32[]{:S(2)}, u32[]{:S(2)}) collective-permute-start(f32[8,128]{1,0:T(8,128)S(1)} %add.9), channel_id=1, source_target_pairs={{0,8},{2,10},{4,12},{6,14},{8,0},{10,2},{12,4},{14,6},{16,24},{18,... | collective-permute-start | bytes 12296 | tf_op jit(solution)/shard_map/ppermute | solution.py:93
  53.0 4.5 %collective-permute-start.14 = (f32[16,128]{1,0:T(8,128)S(1)}, f32[16,128]{1,0:T(8,128)S(1)}, u32[]{:S(2)}, u32[]{:S(2)}) collective-permute-start(f32[16,128]{1,0:T(8,128)S(1)} %pad_maximum_fusion.5), channel_id=1, source_target_pairs={{0,5},{1,4},{2,7},{3,6},{4,1},{5,0},{6,3},{7,2},{8,13},{9,12},{10,... | collective-permute-start | bytes 24584 | tf_op jit(solution)/shard_map/ppermute | solution.py:99
  57.5 1.2 %collective-permute-start.15 = (f32[8,128]{1,0:T(8,128)S(1)}, f32[8,128]{1,0:T(8,128)S(1)}, u32[]{:S(2)}, u32[]{:S(2)}) collective-permute-start(f32[8,128]{1,0:T(8,128)S(1)} %get-tuple-element.129.refs_0_), channel_id=1, source_target_pairs={{0,2},{2,0},{4,6},{6,4},{8,10},{10,8},{12,14},{14,12},{16,18},{18,... | collective-permute-start | bytes 12296 | tf_op jit(solution)/shard_map/ppermute | solution.py:101

commit v4 on v3

--- a/solution.py
+++ b/solution.py
@@ -49,7 +49,7 @@
     steps = []
     while count > 1:
         count //= 2
-        steps.append(count)
+        steps.append(count | 1)
     return steps
 
 
@@ -91,12 +91,12 @@
         return lax.psum(value, "ray"), mine, vox_others(mine)
     for step in hops(count)[:-2]:
         value = value + lax.ppermute(value, "ray", pairs_of(count, step))
-        if step == count // 4:
+        if step == count // 4 | 1:
             given = step_of(given)
         value, given = lax.optimization_barrier((value, given))
     mine = given
     both = jnp.concatenate([value, mine], axis=0)
-    both = lax.ppermute(both, ("ray", "vox"), [(i, i ^ 5) for i in range(2 * count)])
+    both = lax.ppermute(both, ("ray", "vox"), [(i, i ^ 7) for i in range(2 * count)])
     value = value + both[:8]
     return value, lax.ppermute(value, "ray", pairs_of(count, 1)), mine, both[8:]
 
@@ -143,24 +143,24 @@
 
 def pull_lines(weighted, tiles_ref, pick_ref, out_ref, slots):
     rays = weighted.astype(BF16)
-    for k in range(slots):
-        product = jnp.dot(rays, tiles_ref[k], preferred_element_type=F32)
-        out_ref[pl.ds(k, 1), :] = jnp.sum(pick_ref[k] * product, axis=0, keepdims=True)
-
-
-def push_lines(lines, tiles_ref, pick_ref, turned_ref, slots):
-    lane = lane_iota((RAY_TILE, LAT))
-    wide = jnp.concatenate([lines.astype(BF16), jnp.zeros((LAT - slots, LAT), BF16)], axis=0)
-    turned = jnp.zeros((RAY_TILE, LAT), F32)
-    for k in range(slots):
+    for k in range(0, slots, 2):
+        pair = jnp.concatenate([tiles_ref[k], tiles_ref[k + 1]], axis=1)
+        product = jnp.dot(rays, pair, preferred_element_type=F32)
+        out_ref[pl.ds(k, 1), :] = jnp.sum(pick_ref[k] * product[:, :LAT], axis=0, keepdims=True)
+        out_ref[pl.ds(k + 1, 1), :] = jnp.sum(pick_ref[k + 1] * product[:, LAT:], axis=0, keepdims=True)
+
+
+def push_lines(rays, lines, tiles_ref, pick_ref, first, last):
+    for k in range(first, last, 2):
+        both = [jnp.broadcast_to(lines[j : j + 1], (RT, LAT)) for j in (k, k + 1)]
         product = lax.dot_general(
-            tiles_ref[k], wide, (((1,), (1,)), ((), ())), preferred_element_type=F32
+            jnp.concatenate(both, axis=0).astype(BF16),
+            tiles_ref[pl.ds(k, 2)].reshape(2 * RAY_TILE, LAT),
+            (((1,), (1,)), ((), ())),
+            preferred_element_type=F32,
         )
-        turned = jnp.where(lane == k, product, turned)
-    turned_ref[...] = turned.T
-    rays = jnp.zeros((RT, RAY_TILE), F32)
-    for k in range(slots):
-        rays = rays + pick_ref[k] * turned_ref[pl.ds(k, 1), :]
+        rays = rays + pick_ref[k] * product[:RT, :RAY_TILE]
+        rays = rays + pick_ref[k + 1] * product[RT:, RAY_TILE:]
     return rays
 
 
@@ -203,13 +203,9 @@
     )
 
 
-PULLS = 1
-
-
 def start_body(slots, count_ref, row_in, col_in, scale_in, table_in, receiver_in, delays_in, tiles_in,
                packet_ref, weight_ref, start_ref, pick_ref, own_ref, tiles_ref,
                row_ref, col_ref, scale_ref, table_ref, receiver_ref, delays_ref, sems):
-    part = slots // PULLS
     copies = [
         pltpu.make_async_copy(source, target, sems.at[j])
         for j, (source, target) in enumerate([
@@ -217,13 +213,9 @@
             (scale_in, scale_ref), (row_in, row_ref), (col_in, col_ref),
         ])
     ]
-    pulls = [
-        pltpu.make_async_copy(
-            tiles_in.at[pl.ds(j * part, part)], tiles_ref.at[pl.ds(j * part, part)], sems.at[6 + j]
-        )
-        for j in range(PULLS)
-    ]
-    for copy in copies + pulls:
+    pull = pltpu.make_async_copy(tiles_in, tiles_ref, sems.at[6])
+    pull.start()
+    for copy in copies:
         copy.start()
     for copy in copies:
         copy.wait()
@@ -245,12 +237,8 @@
     packet_ref[slots:, :] = jnp.where(
         sub == 0, names.astype(F32), jnp.where(sub == 1, square, 0.0)
     )
-    rays = (weight * start).astype(BF16)
-    for j in range(PULLS):
-        pulls[j].wait()
-        for k in range(j * part, (j + 1) * part):
-            product = jnp.dot(rays, tiles_ref[k], preferred_element_type=F32)
-            packet_ref[pl.ds(k, 1), :] = jnp.sum(pick_ref[k] * product, axis=0, keepdims=True)
+    pull.wait()
+    pull_lines(weight * start, tiles_ref, pick_ref, packet_ref, slots)
 
 
 def names_of(ref, slots):
@@ -320,14 +308,14 @@
 
 
 def first_body(slots, other_ref, half_ref, half_lines_ref, mine_ref, own_ref, pick_ref, tiles_ref,
-               field_ref, lines_ref, out_ref, left_ref, names_ref, turned_ref):
+               field_ref, lines_ref, out_ref, left_ref, names_ref):
     names = names_of(other_ref, slots)
     for j, piece in enumerate(names):
         names_ref[pl.ds(j, 1), :] = piece
     parts = both_parts(padded_lines(other_ref, slots))
     lines = half_lines_ref[...] + found_lines(onehot_of(names, own_ref[...]), parts)
     lines_ref[...] = lines
-    rays = push_lines(lines, tiles_ref, pick_ref, turned_ref, slots)
+    rays, part = jnp.zeros((RT, RAY_TILE), F32), slots * CHUNK // LINES
     zeros = jnp.zeros((PAD, LON_DEV, LAT), F32)
     field_ref[:PAD] = zeros
     field_ref[PAIRS + PAD :] = zeros
@@ -338,6 +326,7 @@
         piece = found_lines(onehot, parts).reshape(count, LON_DEV, LAT) + half_ref[pair : pair + count]
         field_ref[pair + PAD : pair + PAD + count] = piece
         square = square + jnp.sum(piece * piece, axis=0)
+        rays = push_lines(rays, lines, tiles_ref, pick_ref, first // CHUNK * part, (first // CHUNK + 1) * part)
     out_ref[:RT, :] = rays
     out_ref[RT : RT + 8, :] = jnp.broadcast_to(total(square), (8, LAT))
     odd = lax.axis_index("ray") % 2
@@ -435,7 +424,7 @@
 
 def third_body(slots, other_ref, half_ref, half_lines_ref, mine_ref, square_ref, onehot_ref, names_ref, own_ref,
                lines_ref, field_ref, norm_ref, pick_ref, tiles_ref,
-               next_ref, out_ref, shift_ref, turned_ref):
+               next_ref, out_ref, shift_ref):
     shift = jnp.broadcast_to(rows_sum(mine_ref, slots, 0) + rows_sum(other_ref, slots, 0), (8, LAT))
     shift_ref[...] = shift
     inverse = 1.0 / norm_ref[...]
@@ -443,7 +432,7 @@
     parts = both_parts(padded_lines(other_ref, slots))
     names = [names_ref[pl.ds(j, 1), :] for j in range(onehot_ref.shape[1] // LAT)]
     lines = found_lines(onehot_of(names, own_ref[...]), parts) + half_lines_ref[...] - lines_ref[...] * back[:1]
-    rays = push_lines(lines, tiles_ref, pick_ref, turned_ref, slots)
+    rays, part = jnp.zeros((RT, RAY_TILE), F32), slots * CHUNK // LINES
     zeros = jnp.zeros((PAD, LON_DEV, LAT), F32)
     next_ref[:PAD] = zeros
     next_ref[PAIRS + PAD :] = zeros
@@ -457,6 +446,7 @@
         next_ref[pair + PAD : pair + PAD + count] = piece
         square = square + jnp.sum(piece * piece, axis=0)
         cross = cross + jnp.sum(piece * base, axis=0)
+        rays = push_lines(rays, lines, tiles_ref, pick_ref, first // CHUNK * part, (first // CHUNK + 1) * part)
     sub = sub_iota()
     out_ref[:RT, :] = rays
     out_ref[RT : RT + 8, :] = jnp.where(
@@ -566,7 +556,7 @@
          (block.shape, BF16)],
         [pltpu.SMEM((slots,), jnp.int32), pltpu.SMEM((slots,), jnp.int32), pltpu.SMEM((slots,), F32),
          pltpu.SMEM((table,), F32), pltpu.VMEM(held, jnp.int32),
-         pltpu.VMEM(held, F32), pltpu.SemaphoreType.DMA((6 + PULLS,))],
+         pltpu.VMEM(held, F32), pltpu.SemaphoreType.DMA((7,))],
     )(tile_count, *(pltpu.with_memory_space_constraint(x, pltpu.MemorySpace.HBM) for x in (
         tile_row[0, 0], col_index, tile_scale[0, 0], receiver_weight,
         ray_receiver.reshape(held), delays.reshape(held), block)))
@@ -574,7 +564,6 @@
     per = LAT // slots
     names_n = -(-(near.shape[0] // (slots + 8)) // per)
     named = ((names_n, LAT), jnp.int32)
-    turned = pltpu.VMEM((RAY_TILE, LAT), F32)
 
     half, half_lines, names_a = local_call(
         functools.partial(first_half_body, slots), "first_half", [VM] * 2,
@@ -582,7 +571,7 @@
     )(near, own)
     field, lines, sums, left0, names_b = local_call(
         functools.partial(first_body, slots), "first", [VM] * 7,
-        [padded, ((slots, LAT), F32), ((RT + 8 + PAIRS, LAT), F32), row, named], [turned],
+        [padded, ((slots, LAT), F32), ((RT + 8 + PAIRS, LAT), F32), row, named],
     )(far, half, half_lines, near, own, pick, block)
     others, columns, swapped = first_halo(sums, field)
     onehots = local_call(
@@ -614,7 +603,7 @@
     )(near, onehot_a, names_a, own, again_lines, again)
     following, sums, shift = local_call(
         functools.partial(third_body, slots), "third", [VM] * 13,
-        [padded, ((RT + 8 + PAIRS // 2, LAT), F32), row], [turned],
+        [padded, ((RT + 8 + PAIRS // 2, LAT), F32), row],
     )(far, half, half_lines, near, square, onehot_b, names_b, own, lines, field, norm0, pick, block)
     others, beside, halves = next_halo(sums, following)
     last_rays, left1, rest, norm1, ray_square = local_call(

time: 59.5 us -> 56.4 us (0.948)
  waiting for transfers between devices: 20.6 us -> 18.9 us
  starting transfers between devices: 25.7 us -> 24.7 us
    ppermute x8, starting transfers between devices: 14.5 us -> 12.7 us  [gather_rays(): other = lax.ppermute(block, 'ray', pairs_of(count, step))]
    ppermute x8, waiting for transfers between devices: 11.1 us -> 9.46 us  [gather_rays(): other = lax.ppermute(block, 'ray', pairs_of(count, step))]
    ppermute x1, starting transfers between devices: 0.01 us -> 1.48 us  [first_halo(): partner = lax.ppermute(column, 'ray', pairs_of(lax.axis_size('ray'), 1))]
    ppermute x1, starting transfers between devices: 2.71 us -> 2 us  [last_sums(): lax.ppermute(both, ('ray', 'vox'), [(i, i ^ 7) for i in range(2 * count)])]
  transfers between devices with their start and end apart: 16 -> 16, of which waited for: 14 -> 13; matrix products, arithmetic and copies ran while one was open for 0% -> 0% of each run, Pallas kernels for 11% -> 12%
where the time goes in v4:
time: 56.4 us; the launch traced here: 56.2 us
  starting transfers between devices  24.7 us (44%)
  waiting for transfers between devices  18.9 us (34%)
  Pallas kernels  10.8 us (19%)
  between operations  1.41 us (2%)
    ppermute x8, starting transfers between devices, gather_rays(): other = lax.ppermute(block, 'ray', pairs_of(count, step))  12.7 us
    ppermute x8, waiting for transfers between devices, gather_rays(): other = lax.ppermute(block, 'ray', pairs_of(count, step))  9.46 us
    ppermute x2, starting transfers between devices, last_sums(): value = value + lax.ppermute(value, 'ray', pairs_of(count, step))  4.19 us
    ppermute x1, waiting for transfers between devices, next_halo(): other = lax.ppermute(sums, 'vox', [(0, 1), (1, 0)])  2.5 us
    ppermute x1, waiting for transfers between devices, first_halo(): other = lax.ppermute(sums, 'vox', [(0, 1), (1, 0)])  2.36 us
    ppermute x1, starting transfers between devices, first_halo(): other = lax.ppermute(sums, 'vox', [(0, 1), (1, 0)])  2.33 us
    pallas_call x1, Pallas kernels, again_step(): local_call(functools.partial(again_body, slots), 'again', [SM] + [VM] * 2...  2.17 us
    ppermute x1, waiting for transfers between devices, last_sums(): lax.ppermute(both, ('ray', 'vox'), [(i, i ^ 7) for i in range(2 * count)])  2.04 us
  transfers between devices with their start and end apart: 16, of which 13 were waited for; matrix products, arithmetic and copies ran while one was open for 0% of the time, Pallas kernels for 12%

profile of v4, /device:TPU:0, one launch (start us, length us, event | category | flops | bytes accessed | tf_op | source)
XLA Modules:
  0.0 56.2 jit_solution(13367402892355357856)
XLA Ops:
  1.3 1.6 %start.1 = (f32[40,128]{1,0:T(8,128)S(1)}, f32[8,128]{1,0:T(8,128)S(1)}, f32[8,128]{1,0:T(8,128)S(1)}, f32[32,8,128]{2,1,0:T(8,128)S(1)}, s32[32,128]{1,0:T(8,128)S(1)}, /*index=5*/bf16[32,128,128]{2,1,0:T(8,128)(2,1)S(1)}) custom-call(s32[1,1]{1,0:T(1,128)S(6)} %copy.13.count_ref, s32[32]{0:T(128)} %bitcast.13, s32[32]{0:T(128)} %bitcast.8, f32[32]{0:T(128)} %bitcast.14, ...), custom_call_target="tpu_custom_call" | custom-call | tf_op jit(solution)/shard_map/start/pallas_call | solution.py:553
  2.9 0.0 copy-start.1
  2.9 3.5 %collective-permute-start = (f32[40,128]{1,0:T(8,128)S(1)}, f32[40,128]{1,0:T(8,128)S(1)}, u32[]{:S(2)}, u32[]{:S(2)}) collective-permute-start(f32[40,128]{1,0:T(8,128)S(1)} %get-tuple-element.65), channel_id=1, source_target_pairs={{0,18},{2,16},{4,22},{6,20},{8,26},{10,24},{12,30},{14,28},{16,2},... | collective-permute-start | bytes 61448 | tf_op jit(solution)/shard_map/ppermute | solution.py:65
  6.4 0.1 broadcast_in_dim.10
  6.5 0.1 broadcast_in_dim.11
  6.6 1.3 %collective-permute-done = f32[40,128]{1,0:T(8,128)S(1)} collective-permute-done((f32[40,128]{1,0:T(8,128)S(1)}, f32[40,128]{1,0:T(8,128)S(1)}, u32[]{:S(2)}, u32[]{:S(2)}) %collective-permute-start) | collective-permute-done | bytes 20512 | tf_op jit(solution)/shard_map/ppermute | solution.py:65
  7.9 0.1 broadcast_in_dim.12.damp_ref
  8.0 1.9 %collective-permute-start.1 = (f32[80,128]{1,0:T(8,128)S(1)}, f32[80,128]{1,0:T(8,128)S(1)}, u32[]{:S(2)}, u32[]{:S(2)}) collective-permute-start(f32[80,128]{1,0:T(8,128)S(1)} %pad_maximum_fusion.3), channel_id=1, source_target_pairs={{0,10},{2,8},{4,14},{6,12},{8,2},{10,0},{12,6},{14,4},{16,26},{18,... | collective-permute-start | bytes 122888 | tf_op jit(solution)/shard_map/ppermute | solution.py:65
  9.9 1.7 %collective-permute-done.1 = f32[80,128]{1,0:T(8,128)S(1)} collective-permute-done((f32[80,128]{1,0:T(8,128)S(1)}, f32[80,128]{1,0:T(8,128)S(1)}, u32[]{:S(2)}, u32[]{:S(2)}) %collective-permute-start.1) | collective-permute-done | bytes 40992 | tf_op jit(solution)/shard_map/ppermute | solution.py:65
  11.6 1.8 %collective-permute-start.2 = (f32[160,128]{1,0:T(8,128)S(1)}, f32[160,128]{1,0:T(8,128)S(1)}, u32[]{:S(2)}, u32[]{:S(2)}) collective-permute-start(f32[160,128]{1,0:T(8,128)S(1)} %pad_maximum_fusion.1), channel_id=1, source_target_pairs={{0,6},{2,4},{4,2},{6,0},{8,14},{10,12},{12,10},{14,8},{16,22},{18,... | collective-permute-start | bytes 245768 | tf_op jit(solution)/shard_map/ppermute | solution.py:65
  13.4 2.5 %collective-permute-done.2 = f32[160,128]{1,0:T(8,128)S(1)} collective-permute-done((f32[160,128]{1,0:T(8,128)S(1)}, f32[160,128]{1,0:T(8,128)S(1)}, u32[]{:S(2)}, u32[]{:S(2)}) %collective-permute-start.2) | collective-permute-done | bytes 81952 | tf_op jit(solution)/shard_map/ppermute | solution.py:65
  16.0 0.3 collective-permute-start.3
  16.3 0.4 first_half.1
  16.7 0.7 %collective-permute-done.3.other_ref = f32[320,128]{1,0:T(8,128)S(1)} collective-permute-done((f32[320,128]{1,0:T(8,128)S(1)}, f32[320,128]{1,0:T(8,128)S(1)}, u32[]{:S(2)}, u32[]{:S(2)}) %collective-permute-start.3) | collective-permute-done | bytes 163872 | tf_op jit(solution)/shard_map/ppermute | solution.py:65
  17.4 0.8 %first.1 = (f32[132,8,128]{2,1,0:T(8,128)S(1)}, f32[32,128]{1,0:T(8,128)S(1)}, f32[144,128]{1,0:T(8,128)S(1)}, f32[8,128]{1,0:T(8,128)S(1)}, s32[2,128]{1,0:T(2,128)S(1)}) custom-call(f32[320,128]{1,0:T(8,128)S(1)} %collective-permute-done.3.other_ref, f32[128,8,128]{2,1,0:T(8,128)S(1)} %get-tuple-element.68.half_ref, ...), custom_call_target="tpu_custom_call" | custom-call | tf_op jit(solution)/shard_map/first/pallas_call | solution.py:572
  18.2 2.3 %collective-permute-start.4 = (f32[144,128]{1,0:T(8,128)S(1)}, f32[144,128]{1,0:T(8,128)S(1)}, u32[]{:S(2)}, u32[]{:S(2)}) collective-permute-start(f32[144,128]{1,0:T(8,128)S(1)} %get-tuple-element.72.mine_ref), channel_id=1, source_target_pairs={{0,1},{1,0},{2,3},{3,2},{4,5},{5,4},{6,7},{7,6},{8,9},{9,8},{10,11... | collective-permute-start | bytes 221192 | tf_op jit(solution)/shard_map/ppermute | solution.py:115
  20.5 0.2 onehot.1
  20.8 2.4 %collective-permute-done.4.other_ref = f32[144,128]{1,0:T(8,128)S(1)} collective-permute-done((f32[144,128]{1,0:T(8,128)S(1)}, f32[144,128]{1,0:T(8,128)S(1)}, u32[]{:S(2)}, u32[]{:S(2)}) %collective-permute-start.4) | collective-permute-done | bytes 73760 | tf_op jit(solution)/shard_map/ppermute | solution.py:115
  23.1 0.3 second.1
  23.4 1.6 %collective-permute-start.5 = (f32[40,128]{1,0:T(8,128)S(1)}, f32[40,128]{1,0:T(8,128)S(1)}, u32[]{:S(2)}, u32[]{:S(2)}) collective-permute-start(f32[40,128]{1,0:T(8,128)S(1)} %get-tuple-element.81), channel_id=1, source_target_pairs={{0,18},{2,16},{4,22},{6,20},{8,26},{10,24},{12,30},{14,28},{16,2},... | collective-permute-start | bytes 61448 | tf_op jit(solution)/shard_map/ppermute | solution.py:65
  25.0 1.5 %collective-permute-start.6 = (f32[128,128]{1,0:T(8,128)S(1)}, f32[128,128]{1,0:T(8,128)S(1)}, u32[]{:S(2)}, u32[]{:S(2)}) collective-permute-start(f32[128,128]{1,0:T(8,128)S(1)} %slice.16.low_ref.high_ref), channel_id=1, source_target_pairs={{0,2},{2,0},{4,6},{6,4},{8,10},{10,8},{12,14},{14,12},{16,18},{18,... | collective-permute-start | bytes 196616 | tf_op jit(solution)/shard_map/ppermute | solution.py:117
  26.4 1.1 %collective-permute-done.5 = f32[40,128]{1,0:T(8,128)S(1)} collective-permute-done((f32[40,128]{1,0:T(8,128)S(1)}, f32[40,128]{1,0:T(8,128)S(1)}, u32[]{:S(2)}, u32[]{:S(2)}) %collective-permute-start.5) | collective-permute-done | bytes 20512 | tf_op jit(solution)/shard_map/ppermute | solution.py:65
  27.6 0.0 collective-permute-done.6.low2_ref.high2_ref
  27.6 2.1 %collective-permute-start.7 = (f32[80,128]{1,0:T(8,128)S(1)}, f32[80,128]{1,0:T(8,128)S(1)}, u32[]{:S(2)}, u32[]{:S(2)}) collective-permute-start(f32[80,128]{1,0:T(8,128)S(1)} %pad_maximum_fusion.4), channel_id=1, source_target_pairs={{0,10},{2,8},{4,14},{6,12},{8,2},{10,0},{12,6},{14,4},{16,26},{18,... | collective-permute-start | bytes 122888 | tf_op jit(solution)/shard_map/ppermute | solution.py:65
  29.7 1.8 %smooth.1 = (f32[128,8,128]{2,1,0:T(8,128)S(1)}, f32[132,8,128]{2,1,0:T(8,128)S(1)}, f32[2,128,128]{2,1,0:T(8,128)S(1)}, f32[8,128]{1,0:T(8,128)S(1)}) custom-call(f32[132,8,128]{2,1,0:T(8,128)S(1)} %get-tuple-element.83.field_ref.refs_10_, f32[128,128]{1,0:T(8,128)S(1)} %slice.16.low_ref.high_ref, f32[128,128]{1,0:T(8,128)S(1)} %collective-permute-done.6.low2_ref.high2_ref, ...), custom_call_target="tpu_custom_call" | custom-call | tf_op jit(solution)/shard_map/smooth/pallas_call | solution.py:586
  31.5 0.1 collective-permute-done.7
  31.6 1.3 %collective-permute-start.8 = (f32[160,128]{1,0:T(8,128)S(1)}, f32[160,128]{1,0:T(8,128)S(1)}, u32[]{:S(2)}, u32[]{:S(2)}) collective-permute-start(f32[160,128]{1,0:T(8,128)S(1)} %pad_maximum_fusion.2), channel_id=1, source_target_pairs={{0,6},{2,4},{4,2},{6,0},{8,14},{10,12},{12,10},{14,8},{16,22},{18,... | collective-permute-start | bytes 245768 | tf_op jit(solution)/shard_map/ppermute | solution.py:65
  32.9 2.2 %again.1 = (f32[128,8,128]{2,1,0:T(8,128)S(1)}, f32[32,128]{1,0:T(8,128)S(1)}) custom-call(s32[32]{0:T(128)S(1)} %bitcast.9, f32[132,8,128]{2,1,0:T(8,128)S(1)} %get-tuple-element.97.scaled_ref, f32[2,128,128]{2,1,0:T(8,128)S(1)} %get-tuple-element.98.far_ref), custom_call_target="tpu_custom_call" | custom-call | tf_op jit(solution)/shard_map/again/pallas_call | solution.py:593
  35.0 1.1 %collective-permute-done.8 = f32[160,128]{1,0:T(8,128)S(1)} collective-permute-done((f32[160,128]{1,0:T(8,128)S(1)}, f32[160,128]{1,0:T(8,128)S(1)}, u32[]{:S(2)}, u32[]{:S(2)}) %collective-permute-start.8) | collective-permute-done | bytes 81952 | tf_op jit(solution)/shard_map/ppermute | solution.py:65
  36.1 0.2 collective-permute-start.9
  36.3 0.3 third_half.1
  36.6 1.0 %collective-permute-done.9.other_ref = f32[320,128]{1,0:T(8,128)S(1)} collective-permute-done((f32[320,128]{1,0:T(8,128)S(1)}, f32[320,128]{1,0:T(8,128)S(1)}, u32[]{:S(2)}, u32[]{:S(2)}) %collective-permute-start.9) | collective-permute-done | bytes 163872 | tf_op jit(solution)/shard_map/ppermute | solution.py:65
  37.6 0.8 %third.1 = (f32[132,8,128]{2,1,0:T(8,128)S(1)}, f32[80,128]{1,0:T(8,128)S(1)}, f32[8,128]{1,0:T(8,128)S(1)}) custom-call(f32[320,128]{1,0:T(8,128)S(1)} %collective-permute-done.9.other_ref, f32[128,8,128]{2,1,0:T(8,128)S(1)} %get-tuple-element.105.half_ref, f32[32,128]{1,0:T(8,128)S(1)} %get-tuple-element.106.half_lines_ref, ...), custom_call_target="tpu_custom_call" | custom-call | tf_op jit(solution)/shard_map/third/pallas_call | solution.py:604
  38.4 1.6 %collective-permute-start.10 = (f32[80,128]{1,0:T(8,128)S(1)}, f32[80,128]{1,0:T(8,128)S(1)}, u32[]{:S(2)}, u32[]{:S(2)}) collective-permute-start(f32[80,128]{1,0:T(8,128)S(1)} %get-tuple-element.110.mine_ref), channel_id=1, source_target_pairs={{0,1},{1,0},{2,3},{3,2},{4,5},{5,4},{6,7},{7,6},{8,9},{9,8},{10,11... | collective-permute-start | bytes 122888 | tf_op jit(solution)/shard_map/ppermute | solution.py:126
  40.0 2.5 %collective-permute-done.10.other_ref = f32[80,128]{1,0:T(8,128)S(1)} collective-permute-done((f32[80,128]{1,0:T(8,128)S(1)}, f32[80,128]{1,0:T(8,128)S(1)}, u32[]{:S(2)}, u32[]{:S(2)}) %collective-permute-start.10) | collective-permute-done | bytes 40992 | tf_op jit(solution)/shard_map/ppermute | solution.py:126
  42.5 0.0 collective-permute-start.12
  42.5 0.1 fourth.1
  42.7 2.3 %collective-permute-start.11 = (f32[8,128]{1,0:T(8,128)S(1)}, f32[8,128]{1,0:T(8,128)S(1)}, u32[]{:S(2)}, u32[]{:S(2)}) collective-permute-start(f32[8,128]{1,0:T(8,128)S(1)} %get-tuple-element.114), channel_id=1, source_target_pairs={{0,18},{2,16},{4,22},{6,20},{8,26},{10,24},{12,30},{14,28},{16,2},... | collective-permute-start | bytes 12296 | tf_op jit(solution)/shard_map/ppermute | solution.py:93
  45.0 1.7 %collective-permute-done.11 = f32[8,128]{1,0:T(8,128)S(1)} collective-permute-done((f32[8,128]{1,0:T(8,128)S(1)}, f32[8,128]{1,0:T(8,128)S(1)}, u32[]{:S(2)}, u32[]{:S(2)}) %collective-permute-start.11) | collective-permute-done | bytes 4128 | tf_op jit(solution)/shard_map/ppermute | solution.py:93
  46.7 0.0 collective-permute-done.12.high_ref
  46.7 1.9 %collective-permute-start.13 = (f32[8,128]{1,0:T(8,128)S(1)}, f32[8,128]{1,0:T(8,128)S(1)}, u32[]{:S(2)}, u32[]{:S(2)}) collective-permute-start(f32[8,128]{1,0:T(8,128)S(1)} %add.9), channel_id=1, source_target_pairs={{0,10},{2,8},{4,14},{6,12},{8,2},{10,0},{12,6},{14,4},{16,26},{18,... | collective-permute-start | bytes 12296 | tf_op jit(solution)/shard_map/ppermute | solution.py:93
  48.5 1.7 %last_smooth.1.refs_2_ = f32[8,128]{1,0:T(8,128)S(1)} custom-call(f32[132,8,128]{2,1,0:T(8,128)S(1)} %get-tuple-element.116.next_ref.refs_11_, f32[64,128]{1,0:T(8,128)S(1)} %slice.17.low_ref, f32[64,128]{1,0:T(8,128)S(1)} %collective-permute-done.12.high_ref, f32[128,128]{1,0:T(8,128)S(1)} %broadcast_in_dim.12.damp_ref, ...), custom_call_target="tpu_custom_call" | custom-call | tf_op jit(solution)/shard_map/last_smooth/pallas_call | solution.py:614
  50.2 0.0 collective-permute-done.13
  50.2 2.0 %collective-permute-start.14 = (f32[16,128]{1,0:T(8,128)S(1)}, f32[16,128]{1,0:T(8,128)S(1)}, u32[]{:S(2)}, u32[]{:S(2)}) collective-permute-start(f32[16,128]{1,0:T(8,128)S(1)} %pad_maximum_fusion.5), channel_id=1, source_target_pairs={{0,7},{1,6},{2,5},{3,4},{4,3},{5,2},{6,1},{7,0},{8,15},{9,14},{10,... | collective-permute-start | bytes 24584 | tf_op jit(solution)/shard_map/ppermute | solution.py:99
  52.2 2.0 %collective-permute-done.14 = f32[16,128]{1,0:T(8,128)S(1)} collective-permute-done((f32[16,128]{1,0:T(8,128)S(1)}, f32[16,128]{1,0:T(8,128)S(1)}, u32[]{:S(2)}, u32[]{:S(2)}) %collective-permute-start.14) | collective-permute-done | bytes 8224 | tf_op jit(solution)/shard_map/ppermute | solution.py:99
  54.3 0.4 collective-permute-start.15
  54.7 0.8 %collective-permute-done.15.refs_1_ = f32[8,128]{1,0:T(8,128)S(1)} collective-permute-done((f32[8,128]{1,0:T(8,128)S(1)}, f32[8,128]{1,0:T(8,128)S(1)}, u32[]{:S(2)}, u32[]{:S(2)}) %collective-permute-start.15) | collective-permute-done | bytes 4128 | tf_op jit(solution)/shard_map/ppermute | solution.py:101
  55.6 0.7 %end.1 = (f32[8,8,128]{2,1,0:T(8,128)}, f32[8,128]{1,0:T(8,128)}) custom-call(f32[8,128]{1,0:T(8,128)S(1)} %get-tuple-element.129.refs_0_, f32[8,128]{1,0:T(8,128)S(1)} %collective-permute-done.15.refs_1_, f32[8,128]{1,0:T(8,128)S(1)} %last_smooth.1.refs_2_, f32[8,128]{1,0:T(8,128)S(1)} %get-tuple-element.128.refs_3_, ...), custom_call_target="tpu_custom_call" | custom-call | tf_op jit(solution)/shard_map/end/pallas_call | solution.py:621
  (17 shorter events, 0.1 us)
Async XLA Ops:
  2.9 3.6 %copy-start.1 = (f32[64]{0:T(128)S(1)}, f32[64]{0:T(128)}, u32[]{:S(2)}) copy-start(f32[64]{0:T(128)} %param.17) | copy-start | bytes 772
  2.9 5.1 %collective-permute-start = (f32[40,128]{1,0:T(8,128)S(1)}, f32[40,128]{1,0:T(8,128)S(1)}, u32[]{:S(2)}, u32[]{:S(2)}) collective-permute-start(f32[40,128]{1,0:T(8,128)S(1)} %get-tuple-element.65), channel_id=1, source_target_pairs={{0,18},{2,16},{4,22},{6,20},{8,26},{10,24},{12,30},{14,28},{16,2},... | collective-permute-start | bytes 61448 | tf_op jit(solution)/shard_map/ppermute | solution.py:65
  8.0 3.6 %collective-permute-start.1 = (f32[80,128]{1,0:T(8,128)S(1)}, f32[80,128]{1,0:T(8,128)S(1)}, u32[]{:S(2)}, u32[]{:S(2)}) collective-permute-start(f32[80,128]{1,0:T(8,128)S(1)} %pad_maximum_fusion.3), channel_id=1, source_target_pairs={{0,10},{2,8},{4,14},{6,12},{8,2},{10,0},{12,6},{14,4},{16,26},{18,... | collective-permute-start | bytes 122888 | tf_op jit(solution)/shard_map/ppermute | solution.py:65
  11.6 4.3 %collective-permute-start.2 = (f32[160,128]{1,0:T(8,128)S(1)}, f32[160,128]{1,0:T(8,128)S(1)}, u32[]{:S(2)}, u32[]{:S(2)}) collective-permute-start(f32[160,128]{1,0:T(8,128)S(1)} %pad_maximum_fusion.1), channel_id=1, source_target_pairs={{0,6},{2,4},{4,2},{6,0},{8,14},{10,12},{12,10},{14,8},{16,22},{18,... | collective-permute-start | bytes 245768 | tf_op jit(solution)/shard_map/ppermute | solution.py:65
  16.0 1.4 %collective-permute-start.3 = (f32[320,128]{1,0:T(8,128)S(1)}, f32[320,128]{1,0:T(8,128)S(1)}, u32[]{:S(2)}, u32[]{:S(2)}) collective-permute-start(f32[320,128]{1,0:T(8,128)S(1)} %constant_dynamic-update-slice_fusion.mine_ref), channel_id=1, source_target_pairs={{0,2},{2,0},{4,6},{6,4},{8,10},{10,8},{12,14},{14,12},{16,18},{18,... | collective-permute-start | bytes 491528 | tf_op jit(solution)/shard_map/ppermute | solution.py:65
  18.2 4.9 %collective-permute-start.4 = (f32[144,128]{1,0:T(8,128)S(1)}, f32[144,128]{1,0:T(8,128)S(1)}, u32[]{:S(2)}, u32[]{:S(2)}) collective-permute-start(f32[144,128]{1,0:T(8,128)S(1)} %get-tuple-element.72.mine_ref), channel_id=1, source_target_pairs={{0,1},{1,0},{2,3},{3,2},{4,5},{5,4},{6,7},{7,6},{8,9},{9,8},{10,11... | collective-permute-start | bytes 221192 | tf_op jit(solution)/shard_map/ppermute | solution.py:115
  23.4 4.2 %collective-permute-start.5 = (f32[40,128]{1,0:T(8,128)S(1)}, f32[40,128]{1,0:T(8,128)S(1)}, u32[]{:S(2)}, u32[]{:S(2)}) collective-permute-start(f32[40,128]{1,0:T(8,128)S(1)} %get-tuple-element.81), channel_id=1, source_target_pairs={{0,18},{2,16},{4,22},{6,20},{8,26},{10,24},{12,30},{14,28},{16,2},... | collective-permute-start | bytes 61448 | tf_op jit(solution)/shard_map/ppermute | solution.py:65
  25.0 2.6 %collective-permute-start.6 = (f32[128,128]{1,0:T(8,128)S(1)}, f32[128,128]{1,0:T(8,128)S(1)}, u32[]{:S(2)}, u32[]{:S(2)}) collective-permute-start(f32[128,128]{1,0:T(8,128)S(1)} %slice.16.low_ref.high_ref), channel_id=1, source_target_pairs={{0,2},{2,0},{4,6},{6,4},{8,10},{10,8},{12,14},{14,12},{16,18},{18,... | collective-permute-start | bytes 196616 | tf_op jit(solution)/shard_map/ppermute | solution.py:117
  27.6 4.0 %collective-permute-start.7 = (f32[80,128]{1,0:T(8,128)S(1)}, f32[80,128]{1,0:T(8,128)S(1)}, u32[]{:S(2)}, u32[]{:S(2)}) collective-permute-start(f32[80,128]{1,0:T(8,128)S(1)} %pad_maximum_fusion.4), channel_id=1, source_target_pairs={{0,10},{2,8},{4,14},{6,12},{8,2},{10,0},{12,6},{14,4},{16,26},{18,... | collective-permute-start | bytes 122888 | tf_op jit(solution)/shard_map/ppermute | solution.py:65
  31.6 1.3 %copy-start = (s32[1,1,32]{2,1,0:T(1,128)S(1)}, s32[1,1,32]{2,1,0:T(1,128)}, u32[]{:S(2)}) copy-start(s32[1,1,32]{2,1,0:T(1,128)} %param.12) | copy-start | bytes 388
  31.6 4.5 %collective-permute-start.8 = (f32[160,128]{1,0:T(8,128)S(1)}, f32[160,128]{1,0:T(8,128)S(1)}, u32[]{:S(2)}, u32[]{:S(2)}) collective-permute-start(f32[160,128]{1,0:T(8,128)S(1)} %pad_maximum_fusion.2), channel_id=1, source_target_pairs={{0,6},{2,4},{4,2},{6,0},{8,14},{10,12},{12,10},{14,8},{16,22},{18,... | collective-permute-start | bytes 245768 | tf_op jit(solution)/shard_map/ppermute | solution.py:65
  36.1 1.5 %collective-permute-start.9 = (f32[320,128]{1,0:T(8,128)S(1)}, f32[320,128]{1,0:T(8,128)S(1)}, u32[]{:S(2)}, u32[]{:S(2)}) collective-permute-start(f32[320,128]{1,0:T(8,128)S(1)} %pad_maximum_fusion.mine_ref), channel_id=1, source_target_pairs={{0,2},{2,0},{4,6},{6,4},{8,10},{10,8},{12,14},{14,12},{16,18},{18,... | collective-permute-start | bytes 491528 | tf_op jit(solution)/shard_map/ppermute | solution.py:65
  38.4 4.1 %collective-permute-start.10 = (f32[80,128]{1,0:T(8,128)S(1)}, f32[80,128]{1,0:T(8,128)S(1)}, u32[]{:S(2)}, u32[]{:S(2)}) collective-permute-start(f32[80,128]{1,0:T(8,128)S(1)} %get-tuple-element.110.mine_ref), channel_id=1, source_target_pairs={{0,1},{1,0},{2,3},{3,2},{4,5},{5,4},{6,7},{7,6},{8,9},{9,8},{10,11... | collective-permute-start | bytes 122888 | tf_op jit(solution)/shard_map/ppermute | solution.py:126
  42.5 4.2 %collective-permute-start.12 = (f32[64,128]{1,0:T(8,128)S(1)}, f32[64,128]{1,0:T(8,128)S(1)}, u32[]{:S(2)}, u32[]{:S(2)}) collective-permute-start(f32[64,128]{1,0:T(8,128)S(1)} %slice.17.low_ref), channel_id=1, source_target_pairs={{0,2},{2,0},{4,6},{6,4},{8,10},{10,8},{12,14},{14,12},{16,18},{18,... | collective-permute-start | bytes 98312 | tf_op jit(solution)/shard_map/ppermute | solution.py:128
  42.7 4.0 %collective-permute-start.11 = (f32[8,128]{1,0:T(8,128)S(1)}, f32[8,128]{1,0:T(8,128)S(1)}, u32[]{:S(2)}, u32[]{:S(2)}) collective-permute-start(f32[8,128]{1,0:T(8,128)S(1)} %get-tuple-element.114), channel_id=1, source_target_pairs={{0,18},{2,16},{4,22},{6,20},{8,26},{10,24},{12,30},{14,28},{16,2},... | collective-permute-start | bytes 12296 | tf_op jit(solution)/shard_map/ppermute | solution.py:93
  46.7 3.6 %collective-permute-start.13 = (f32[8,128]{1,0:T(8,128)S(1)}, f32[8,128]{1,0:T(8,128)S(1)}, u32[]{:S(2)}, u32[]{:S(2)}) collective-permute-start(f32[8,128]{1,0:T(8,128)S(1)} %add.9), channel_id=1, source_target_pairs={{0,10},{2,8},{4,14},{6,12},{8,2},{10,0},{12,6},{14,4},{16,26},{18,... | collective-permute-start | bytes 12296 | tf_op jit(solution)/shard_map/ppermute | solution.py:93
  50.2 4.0 %collective-permute-start.14 = (f32[16,128]{1,0:T(8,128)S(1)}, f32[16,128]{1,0:T(8,128)S(1)}, u32[]{:S(2)}, u32[]{:S(2)}) collective-permute-start(f32[16,128]{1,0:T(8,128)S(1)} %pad_maximum_fusion.5), channel_id=1, source_target_pairs={{0,7},{1,6},{2,5},{3,4},{4,3},{5,2},{6,1},{7,0},{8,15},{9,14},{10,... | collective-permute-start | bytes 24584 | tf_op jit(solution)/shard_map/ppermute | solution.py:99
  54.3 1.3 %collective-permute-start.15 = (f32[8,128]{1,0:T(8,128)S(1)}, f32[8,128]{1,0:T(8,128)S(1)}, u32[]{:S(2)}, u32[]{:S(2)}) collective-permute-start(f32[8,128]{1,0:T(8,128)S(1)} %get-tuple-element.129.refs_0_), channel_id=1, source_target_pairs={{0,2},{2,0},{4,6},{6,4},{8,10},{10,8},{12,14},{14,12},{16,18},{18,... | collective-permute-start | bytes 12296 | tf_op jit(solution)/shard_map/ppermute | solution.py:101

commit v5 on v4

--- a/solution.py
+++ b/solution.py
@@ -13,10 +13,11 @@
 LON_DEV = 8
 RAY_TILE = 128
 RT = 8
+CORES = 2
 PAIRS = ALT * EPOCHS
 LINES = PAIRS * LON_DEV
 PAD = EPOCHS
-UNROLL = 8
+UNROLL = 32
 
 LATERAL = 1.0
 VERTICAL = 4.0
@@ -53,26 +54,25 @@
     return steps
 
 
-def gather_rays(block, during=()):
+def gather_rays(packet, extra, during=()):
     count = lax.axis_size("ray")
+    if count < 2 or count & (count - 1):
+        raise ValueError("ray size")
     done, given = list(during), None
-    if count & (count - 1) or count == 1:
-        whole = lax.all_gather(block, "ray", tiled=True)
-        half = whole.shape[0] // 2
-        block, other = whole[:half], whole[half:]
-    else:
-        for step in hops(count):
-            other = lax.ppermute(block, "ray", pairs_of(count, step))
-            if step == 1:
-                break
-            joined = jnp.concatenate([block, other], axis=0)
-            if done:
-                given = done.pop(0)(given)
-                joined, given = lax.optimization_barrier((joined, given))
-            block = joined
+    for step in hops(count):
+        other = lax.ppermute(packet, "ray", pairs_of(count, step))
+        if step == 1:
+            break
+        joined = jnp.concatenate(
+            [packet[:-extra], other[:-extra], packet[-extra:] + other[-extra:]], axis=0
+        )
+        if done:
+            given = done.pop(0)(given)
+            joined, given = lax.optimization_barrier((joined, given))
+        packet = joined
     while done:
         given = done.pop(0)(given)
-    return block, other, given
+    return packet, other, given
 
 
 def vox_others(value):
@@ -227,45 +227,62 @@
     weight_ref[...] = weight
     start = weight * delays_ref[...]
     start_ref[...] = start
-    names = jnp.zeros((8, LAT), jnp.int32)
+    extra = packet_ref.shape[0] - slots
+    sub_x, lane_x = sub_iota((extra, LAT)), lane_iota((extra, LAT))
+    side, place = own_place()
+    rows, per = names_rows(slots), LAT // slots
+    first = place % per * slots
+    names = jnp.zeros((1, LAT), jnp.int32)
     for k in range(slots):
         live = jnp.where(k < count_ref[0, 0], scale_ref[k], 0.0)
         pick_ref[k] = jnp.where(sub == row_ref[k], live, 0.0)
         own_ref[pl.ds(k, 1), :] = jnp.full((1, LAT), col_ref[k], jnp.int32)
-        names = jnp.where(lane == k, col_ref[k], names)
+        names = jnp.where(lane[:1] == first + k, col_ref[k], names)
     square = total(start * start)
     packet_ref[slots:, :] = jnp.where(
-        sub == 0, names.astype(F32), jnp.where(sub == 1, square, 0.0)
+        sub_x == side * rows + place // per,
+        jnp.broadcast_to(names.astype(F32), (extra, LAT)),
+        jnp.where(sub_x == CORES * rows, square, 0.0),
     )
     pull.wait()
     pull_lines(weight * start, tiles_ref, pick_ref, packet_ref, slots)
 
 
-def names_of(ref, slots):
-    blocks = ref.shape[0] // (slots + 8)
-    per = LAT // slots
-    pieces = []
-    for first in range(0, blocks, per):
-        row = ref[pl.ds(first * (slots + 8) + slots, 1), :]
-        for j in range(1, min(per, blocks - first)):
-            row = row + pltpu.roll(ref[pl.ds((first + j) * (slots + 8) + slots, 1), :], j * slots, 1)
-        if blocks - first < per:
-            row = jnp.where(lane_iota((1, LAT)) < (blocks - first) * slots, row, -1.0)
-        pieces.append(row.astype(jnp.int32))
-    return pieces
-
-
-def lines_in(ref, slots):
-    blocks = ref.shape[0] // (slots + 8)
-    return [ref[b * (slots + 8) : b * (slots + 8) + slots, :] for b in range(blocks)]
-
-
-def padded_lines(ref, slots):
-    per = LAT // slots
-    rows = lines_in(ref, slots)
-    if len(rows) % per:
-        rows.append(jnp.zeros(((per - len(rows) % per) * slots, LAT), F32))
-    return jnp.concatenate(rows, axis=0)
+def own_place():
+    count, at = lax.axis_size("ray"), lax.axis_index("ray")
+    side, place, bit = at % 2, 0, 1
+    for step in hops(count)[:-1]:
+        digit = at // (step - 1) % 2
+        side = (side + digit) % 2
+        place = place + bit * digit
+        bit *= 2
+    return side, place
+
+
+def names_rows(slots):
+    return lax.axis_size("ray") // CORES * slots // LAT
+
+
+def names_of(ref, side, slots):
+    rows = names_rows(slots)
+    first = lax.axis_size("ray") // CORES * slots + side * rows
+    return [ref[pl.ds(first + j, 1), :].astype(jnp.int32) for j in range(rows)]
+
+
+def placed_lines(ref, slots):
+    place = own_place()[1]
+    return jnp.concatenate(
+        [
+            ref[pl.ds(pl.multiple_of((j ^ place) * slots, slots), slots), :]
+            for j in range(lax.axis_size("ray") // CORES)
+        ],
+        axis=0,
+    )
+
+
+def extra_row(ref, slots, at):
+    first = lax.axis_size("ray") // CORES * slots
+    return ref[first + at : first + at + 1, :]
 
 
 def found_lines(onehot, parts):
@@ -273,14 +290,6 @@
     return found[:, :LAT] + found[:, LAT:]
 
 
-def rows_sum(ref, slots, at):
-    blocks = ref.shape[0] // (slots + 8)
-    out = ref[pl.ds(slots + at, 1), :]
-    for b in range(1, blocks):
-        out = out + ref[pl.ds(b * (slots + 8) + slots + at, 1), :]
-    return out
-
-
 CHUNK = 128
 
 
@@ -296,10 +305,10 @@
 
 
 def first_half_body(slots, mine_ref, own_ref, field_ref, lines_ref, names_ref):
-    names = names_of(mine_ref, slots)
+    names = names_of(mine_ref, own_place()[0], slots)
     for j, piece in enumerate(names):
         names_ref[pl.ds(j, 1), :] = piece
-    parts = both_parts(padded_lines(mine_ref, slots))
+    parts = both_parts(placed_lines(mine_ref, slots))
     lines_ref[...] = found_lines(onehot_of(names, own_ref[...]), parts)
     for first in range(0, LINES, CHUNK):
         onehot = onehot_of(names, sub_iota((CHUNK, LAT)) + first)
@@ -309,10 +318,10 @@
 
 def first_body(slots, other_ref, half_ref, half_lines_ref, mine_ref, own_ref, pick_ref, tiles_ref,
                field_ref, lines_ref, out_ref, left_ref, names_ref):
-    names = names_of(other_ref, slots)
+    names = names_of(other_ref, 1 - own_place()[0], slots)
     for j, piece in enumerate(names):
         names_ref[pl.ds(j, 1), :] = piece
-    parts = both_parts(padded_lines(other_ref, slots))
+    parts = both_parts(placed_lines(other_ref, slots))
     lines = half_lines_ref[...] + found_lines(onehot_of(names, own_ref[...]), parts)
     lines_ref[...] = lines
     rays, part = jnp.zeros((RT, RAY_TILE), F32), slots * CHUNK // LINES
@@ -332,7 +341,9 @@
     odd = lax.axis_index("ray") % 2
     at = jnp.where(lax.axis_index("vox") == 0, LON_DEV - 1 - odd, odd)
     out_ref[RT + 8 :, :] = edge_of(field_ref, at)
-    left_ref[...] = jnp.broadcast_to(rows_sum(mine_ref, slots, 1) + rows_sum(other_ref, slots, 1), (8, LAT))
+    at = CORES * names_rows(slots)
+    left = extra_row(mine_ref, slots, at) + extra_row(other_ref, slots, at)
+    left_ref[...] = jnp.broadcast_to(left, (8, LAT))
 
 
 def second_body(slots, mine_ref, other_ref, left_ref, weight_ref, start_ref, pick_ref, tiles_ref,
@@ -413,7 +424,7 @@
 
 def third_half_body(slots, mine_ref, onehot_ref, names_ref, own_ref, again_lines_ref, again_ref,
                     half_ref, lines_ref):
-    parts = both_parts(padded_lines(mine_ref, slots))
+    parts = both_parts(placed_lines(mine_ref, slots))
     names = [names_ref[pl.ds(j, 1), :] for j in range(onehot_ref.shape[1] // LAT)]
     lines_ref[...] = found_lines(onehot_of(names, own_ref[...]), parts) + again_lines_ref[...]
     for first in range(0, LINES, CHUNK):
@@ -425,11 +436,11 @@
 def third_body(slots, other_ref, half_ref, half_lines_ref, mine_ref, square_ref, onehot_ref, names_ref, own_ref,
                lines_ref, field_ref, norm_ref, pick_ref, tiles_ref,
                next_ref, out_ref, shift_ref):
-    shift = jnp.broadcast_to(rows_sum(mine_ref, slots, 0) + rows_sum(other_ref, slots, 0), (8, LAT))
+    shift = jnp.broadcast_to(extra_row(mine_ref, slots, 0) + extra_row(other_ref, slots, 0), (8, LAT))
     shift_ref[...] = shift
     inverse = 1.0 / norm_ref[...]
     back = shift * inverse
-    parts = both_parts(padded_lines(other_ref, slots))
+    parts = both_parts(placed_lines(other_ref, slots))
     names = [names_ref[pl.ds(j, 1), :] for j in range(onehot_ref.shape[1] // LAT)]
     lines = found_lines(onehot_of(names, own_ref[...]), parts) + half_lines_ref[...] - lines_ref[...] * back[:1]
     rays, part = jnp.zeros((RT, RAY_TILE), F32), slots * CHUNK // LINES
@@ -546,13 +557,15 @@
     slab = ((PAIRS, LON_DEV, LAT), F32)
     padded = ((PAIRS + 2 * PAD, LON_DEV, LAT), F32)
     packet = ((slots + 8, LAT), F32)
+    names_n = rays_n // CORES * slots // LAT
+    extra = -(-(CORES * names_n + 1) // 8) * 8
     damp = jnp.broadcast_to(jnp.repeat(smooth_scale, EPOCHS)[:, None], (PAIRS, LAT))
 
     hbm = pl.BlockSpec(memory_space=pl.ANY)
     table = receiver_weight.shape[0]
     mine, weight, start, pick, own, block = local_call(
         functools.partial(start_body, slots), "start", [SM] + [hbm] * 7,
-        [packet, (held, F32), (held, F32), ((slots, RT, LAT), F32), ((slots, LAT), jnp.int32),
+        [((slots + extra, LAT), F32), (held, F32), (held, F32), ((slots, RT, LAT), F32), ((slots, LAT), jnp.int32),
          (block.shape, BF16)],
         [pltpu.SMEM((slots,), jnp.int32), pltpu.SMEM((slots,), jnp.int32), pltpu.SMEM((slots,), F32),
          pltpu.SMEM((table,), F32), pltpu.VMEM(held, jnp.int32),
@@ -560,9 +573,7 @@
     )(tile_count, *(pltpu.with_memory_space_constraint(x, pltpu.MemorySpace.HBM) for x in (
         tile_row[0, 0], col_index, tile_scale[0, 0], receiver_weight,
         ray_receiver.reshape(held), delays.reshape(held), block)))
-    near, far, damp = gather_rays(mine, (lambda _: damp,))
-    per = LAT // slots
-    names_n = -(-(near.shape[0] // (slots + 8)) // per)
+    near, far, damp = gather_rays(mine, extra, (lambda _: damp,))
     named = ((names_n, LAT), jnp.int32)
 
     half, half_lines, names_a = local_call(
@@ -595,7 +606,7 @@
         )(col_index, scaled, beside)
         return smooth, square, again, again_lines
 
-    near, far, given = gather_rays(mine, (lambda _: columns, smooth_step, again_step))
+    near, far, given = gather_rays(mine, 8, (lambda _: columns, smooth_step, again_step))
     smooth, square, again, again_lines = given
 
     half, half_lines = local_call(

time: 56.4 us -> 55.3 us (0.980)
  Pallas kernels: 10.8 us -> 8.1 us
  waiting for transfers between devices: 18.9 us -> 19.9 us
  starting transfers between devices: 24.7 us -> 25.3 us
    ppermute x8, waiting for transfers between devices: 9.46 us -> 10.4 us  [gather_rays(): other = lax.ppermute(packet, 'ray', pairs_of(count, step))]
    pallas_call x1, Pallas kernels: 1.78 us -> 0.88 us  [smooth_step(): local_call(functools.partial(smooth_body, swapped), 'smooth', [VM] * 7, [...]
    pallas_call x1, Pallas kernels: 2.17 us -> 1.29 us  [again_step(): local_call(functools.partial(again_body, slots), 'again', [SM] + [VM] * 2...]
    pallas_call x1, Pallas kernels: 1.67 us -> 0.8 us  [last_step(): local_call(functools.partial(last_smooth_body, halves), 'last_smooth', [V...]
  transfers between devices with their start and end apart: 16 -> 16, of which waited for: 13 -> 14; matrix products, arithmetic and copies ran while one was open for 0% -> 0% of each run, Pallas kernels for 12% -> 7%
where the time goes in v5:
time: 55.3 us; the launch traced here: 55.1 us
  starting transfers between devices  25.3 us (46%)
  waiting for transfers between devices  19.9 us (36%)
  Pallas kernels  8.1 us (15%)
  between operations  1.43 us (3%)
    ppermute x8, starting transfers between devices, gather_rays(): other = lax.ppermute(packet, 'ray', pairs_of(count, step))  12.8 us
    ppermute x8, waiting for transfers between devices, gather_rays(): other = lax.ppermute(packet, 'ray', pairs_of(count, step))  10.4 us
    ppermute x2, starting transfers between devices, last_sums(): value = value + lax.ppermute(value, 'ray', pairs_of(count, step))  4.39 us
    ppermute x1, waiting for transfers between devices, next_halo(): other = lax.ppermute(sums, 'vox', [(0, 1), (1, 0)])  2.48 us
    ppermute x1, waiting for transfers between devices, first_halo(): other = lax.ppermute(sums, 'vox', [(0, 1), (1, 0)])  2.37 us
    ppermute x1, starting transfers between devices, last_sums(): lax.ppermute(both, ('ray', 'vox'), [(i, i ^ 7) for i in range(2 * count)])  2.3 us
    ppermute x1, starting transfers between devices, first_halo(): other = lax.ppermute(sums, 'vox', [(0, 1), (1, 0)])  2.28 us
    ppermute x2, waiting for transfers between devices, last_sums(): value = value + lax.ppermute(value, 'ray', pairs_of(count, step))  2.1 us
  transfers between devices with their start and end apart: 16, of which 14 were waited for; matrix products, arithmetic and copies ran while one was open for 0% of the time, Pallas kernels for 7%

profile of v5, /device:TPU:0, one launch (start us, length us, event | category | flops | bytes accessed | tf_op | source)
XLA Modules:
  0.0 55.1 jit_solution(12621277804957171803)
XLA Ops:
  1.3 1.6 %start.1 = (f32[40,128]{1,0:T(8,128)S(1)}, f32[8,128]{1,0:T(8,128)S(1)}, f32[8,128]{1,0:T(8,128)S(1)}, f32[32,8,128]{2,1,0:T(8,128)S(1)}, s32[32,128]{1,0:T(8,128)S(1)}, /*index=5*/bf16[32,128,128]{2,1,0:T(8,128)(2,1)S(1)}) custom-call(s32[1,1]{1,0:T(1,128)S(6)} %copy.11.count_ref, s32[32]{0:T(128)} %bitcast.13, s32[32]{0:T(128)} %bitcast.8, f32[32]{0:T(128)} %bitcast.14, ...), custom_call_target="tpu_custom_call" | custom-call | tf_op jit(solution)/shard_map/start/pallas_call | solution.py:566
  2.9 0.0 copy-start.1
  2.9 3.5 %collective-permute-start = (f32[40,128]{1,0:T(8,128)S(1)}, f32[40,128]{1,0:T(8,128)S(1)}, u32[]{:S(2)}, u32[]{:S(2)}) collective-permute-start(f32[40,128]{1,0:T(8,128)S(1)} %get-tuple-element.65), channel_id=1, source_target_pairs={{0,18},{2,16},{4,22},{6,20},{8,26},{10,24},{12,30},{14,28},{16,2},... | collective-permute-start | bytes 61448 | tf_op jit(solution)/shard_map/ppermute | solution.py:63
  6.4 0.1 broadcast_in_dim.10
  6.5 0.1 broadcast_in_dim.11
  6.6 1.3 %collective-permute-done = f32[40,128]{1,0:T(8,128)S(1)} collective-permute-done((f32[40,128]{1,0:T(8,128)S(1)}, f32[40,128]{1,0:T(8,128)S(1)}, u32[]{:S(2)}, u32[]{:S(2)}) %collective-permute-start) | collective-permute-done | bytes 20512 | tf_op jit(solution)/shard_map/ppermute | solution.py:63
  8.0 0.1 broadcast_in_dim.12.damp_ref
  8.0 1.9 %collective-permute-start.1 = (f32[72,128]{1,0:T(8,128)S(1)}, f32[72,128]{1,0:T(8,128)S(1)}, u32[]{:S(2)}, u32[]{:S(2)}) collective-permute-start(f32[72,128]{1,0:T(8,128)S(1)} %pad_maximum_fusion.4), channel_id=1, source_target_pairs={{0,10},{2,8},{4,14},{6,12},{8,2},{10,0},{12,6},{14,4},{16,26},{18,... | collective-permute-start | bytes 110600 | tf_op jit(solution)/shard_map/ppermute | solution.py:63
  9.9 1.6 %collective-permute-done.1 = f32[72,128]{1,0:T(8,128)S(1)} collective-permute-done((f32[72,128]{1,0:T(8,128)S(1)}, f32[72,128]{1,0:T(8,128)S(1)}, u32[]{:S(2)}, u32[]{:S(2)}) %collective-permute-start.1) | collective-permute-done | bytes 36896 | tf_op jit(solution)/shard_map/ppermute | solution.py:63
  11.6 1.8 %collective-permute-start.2 = (f32[136,128]{1,0:T(8,128)S(1)}, f32[136,128]{1,0:T(8,128)S(1)}, u32[]{:S(2)}, u32[]{:S(2)}) collective-permute-start(f32[136,128]{1,0:T(8,128)S(1)} %pad_maximum_fusion.2), channel_id=1, source_target_pairs={{0,6},{2,4},{4,2},{6,0},{8,14},{10,12},{12,10},{14,8},{16,22},{18,... | collective-permute-start | bytes 208904 | tf_op jit(solution)/shard_map/ppermute | solution.py:63
  13.4 2.3 %collective-permute-done.2 = f32[136,128]{1,0:T(8,128)S(1)} collective-permute-done((f32[136,128]{1,0:T(8,128)S(1)}, f32[136,128]{1,0:T(8,128)S(1)}, u32[]{:S(2)}, u32[]{:S(2)}) %collective-permute-start.2) | collective-permute-done | bytes 69664 | tf_op jit(solution)/shard_map/ppermute | solution.py:63
  15.7 0.3 collective-permute-start.3
  16.1 0.3 first_half.1
  16.4 0.8 %collective-permute-done.3.other_ref = f32[264,128]{1,0:T(8,128)S(1)} collective-permute-done((f32[264,128]{1,0:T(8,128)S(1)}, f32[264,128]{1,0:T(8,128)S(1)}, u32[]{:S(2)}, u32[]{:S(2)}) %collective-permute-start.3) | collective-permute-done | bytes 135200 | tf_op jit(solution)/shard_map/ppermute | solution.py:63
  17.1 0.8 %first.1 = (f32[132,8,128]{2,1,0:T(8,128)S(1)}, f32[32,128]{1,0:T(8,128)S(1)}, f32[144,128]{1,0:T(8,128)S(1)}, f32[8,128]{1,0:T(8,128)S(1)}, s32[2,128]{1,0:T(2,128)S(1)}) custom-call(f32[264,128]{1,0:T(8,128)S(1)} %collective-permute-done.3.other_ref, f32[128,8,128]{2,1,0:T(8,128)S(1)} %get-tuple-element.68.half_ref, ...), custom_call_target="tpu_custom_call" | custom-call | tf_op jit(solution)/shard_map/first/pallas_call | solution.py:583
  17.9 2.3 %collective-permute-start.4 = (f32[144,128]{1,0:T(8,128)S(1)}, f32[144,128]{1,0:T(8,128)S(1)}, u32[]{:S(2)}, u32[]{:S(2)}) collective-permute-start(f32[144,128]{1,0:T(8,128)S(1)} %get-tuple-element.72.mine_ref), channel_id=1, source_target_pairs={{0,1},{1,0},{2,3},{3,2},{4,5},{5,4},{6,7},{7,6},{8,9},{9,8},{10,11... | collective-permute-start | bytes 221192 | tf_op jit(solution)/shard_map/ppermute | solution.py:115
  20.2 0.2 onehot.1
  20.4 2.4 %collective-permute-done.4.other_ref = f32[144,128]{1,0:T(8,128)S(1)} collective-permute-done((f32[144,128]{1,0:T(8,128)S(1)}, f32[144,128]{1,0:T(8,128)S(1)}, u32[]{:S(2)}, u32[]{:S(2)}) %collective-permute-start.4) | collective-permute-done | bytes 73760 | tf_op jit(solution)/shard_map/ppermute | solution.py:115
  22.8 0.3 second.1
  23.1 1.6 %collective-permute-start.5 = (f32[40,128]{1,0:T(8,128)S(1)}, f32[40,128]{1,0:T(8,128)S(1)}, u32[]{:S(2)}, u32[]{:S(2)}) collective-permute-start(f32[40,128]{1,0:T(8,128)S(1)} %get-tuple-element.81), channel_id=1, source_target_pairs={{0,18},{2,16},{4,22},{6,20},{8,26},{10,24},{12,30},{14,28},{16,2},... | collective-permute-start | bytes 61448 | tf_op jit(solution)/shard_map/ppermute | solution.py:63
  24.7 1.5 %collective-permute-start.6 = (f32[128,128]{1,0:T(8,128)S(1)}, f32[128,128]{1,0:T(8,128)S(1)}, u32[]{:S(2)}, u32[]{:S(2)}) collective-permute-start(f32[128,128]{1,0:T(8,128)S(1)} %slice.114.low_ref.high_ref), channel_id=1, source_target_pairs={{0,2},{2,0},{4,6},{6,4},{8,10},{10,8},{12,14},{14,12},{16,18},{18,... | collective-permute-start | bytes 196616 | tf_op jit(solution)/shard_map/ppermute | solution.py:117
  26.2 1.0 %collective-permute-done.5 = f32[40,128]{1,0:T(8,128)S(1)} collective-permute-done((f32[40,128]{1,0:T(8,128)S(1)}, f32[40,128]{1,0:T(8,128)S(1)}, u32[]{:S(2)}, u32[]{:S(2)}) %collective-permute-start.5) | collective-permute-done | bytes 20512 | tf_op jit(solution)/shard_map/ppermute | solution.py:63
  27.3 2.1 %collective-permute-start.7 = (f32[72,128]{1,0:T(8,128)S(1)}, f32[72,128]{1,0:T(8,128)S(1)}, u32[]{:S(2)}, u32[]{:S(2)}) collective-permute-start(f32[72,128]{1,0:T(8,128)S(1)} %pad_maximum_fusion.5), channel_id=1, source_target_pairs={{0,10},{2,8},{4,14},{6,12},{8,2},{10,0},{12,6},{14,4},{16,26},{18,... | collective-permute-start | bytes 110600 | tf_op jit(solution)/shard_map/ppermute | solution.py:63
  29.4 0.9 %smooth.1 = (f32[128,8,128]{2,1,0:T(8,128)S(1)}, f32[132,8,128]{2,1,0:T(8,128)S(1)}, f32[2,128,128]{2,1,0:T(8,128)S(1)}, f32[8,128]{1,0:T(8,128)S(1)}) custom-call(f32[132,8,128]{2,1,0:T(8,128)S(1)} %get-tuple-element.83.field_ref.refs_10_, f32[128,128]{1,0:T(8,128)S(1)} %slice.114.low_ref.high_ref, ...), custom_call_target="tpu_custom_call" | custom-call | tf_op jit(solution)/shard_map/smooth/pallas_call | solution.py:597
  30.3 0.9 %collective-permute-done.7 = f32[72,128]{1,0:T(8,128)S(1)} collective-permute-done((f32[72,128]{1,0:T(8,128)S(1)}, f32[72,128]{1,0:T(8,128)S(1)}, u32[]{:S(2)}, u32[]{:S(2)}) %collective-permute-start.7) | collective-permute-done | bytes 36896 | tf_op jit(solution)/shard_map/ppermute | solution.py:63
  31.2 0.0 copy-start
  31.2 1.3 %collective-permute-start.8 = (f32[136,128]{1,0:T(8,128)S(1)}, f32[136,128]{1,0:T(8,128)S(1)}, u32[]{:S(2)}, u32[]{:S(2)}) collective-permute-start(f32[136,128]{1,0:T(8,128)S(1)} %pad_maximum_fusion.3), channel_id=1, source_target_pairs={{0,6},{2,4},{4,2},{6,0},{8,14},{10,12},{12,10},{14,8},{16,22},{18,... | collective-permute-start | bytes 208904 | tf_op jit(solution)/shard_map/ppermute | solution.py:63
  32.5 1.3 %again.1 = (f32[128,8,128]{2,1,0:T(8,128)S(1)}, f32[32,128]{1,0:T(8,128)S(1)}) custom-call(s32[32]{0:T(128)S(1)} %bitcast.9, f32[132,8,128]{2,1,0:T(8,128)S(1)} %get-tuple-element.97.scaled_ref, f32[2,128,128]{2,1,0:T(8,128)S(1)} %get-tuple-element.98.far_ref), custom_call_target="tpu_custom_call" | custom-call | tf_op jit(solution)/shard_map/again/pallas_call | solution.py:604
  33.8 1.7 %collective-permute-done.8 = f32[136,128]{1,0:T(8,128)S(1)} collective-permute-done((f32[136,128]{1,0:T(8,128)S(1)}, f32[136,128]{1,0:T(8,128)S(1)}, u32[]{:S(2)}, u32[]{:S(2)}) %collective-permute-start.8) | collective-permute-done | bytes 69664 | tf_op jit(solution)/shard_map/ppermute | solution.py:63
  35.5 0.2 collective-permute-start.9
  35.6 0.3 third_half.1
  36.0 0.9 %collective-permute-done.9.other_ref = f32[264,128]{1,0:T(8,128)S(1)} collective-permute-done((f32[264,128]{1,0:T(8,128)S(1)}, f32[264,128]{1,0:T(8,128)S(1)}, u32[]{:S(2)}, u32[]{:S(2)}) %collective-permute-start.9) | collective-permute-done | bytes 135200 | tf_op jit(solution)/shard_map/ppermute | solution.py:63
  36.9 0.8 %third.1 = (f32[132,8,128]{2,1,0:T(8,128)S(1)}, f32[80,128]{1,0:T(8,128)S(1)}, f32[8,128]{1,0:T(8,128)S(1)}) custom-call(f32[264,128]{1,0:T(8,128)S(1)} %collective-permute-done.9.other_ref, f32[128,8,128]{2,1,0:T(8,128)S(1)} %get-tuple-element.105.half_ref, f32[32,128]{1,0:T(8,128)S(1)} %get-tuple-element.106.half_lines_ref, ...), custom_call_target="tpu_custom_call" | custom-call | tf_op jit(solution)/shard_map/third/pallas_call | solution.py:615
  37.7 1.6 %collective-permute-start.10 = (f32[80,128]{1,0:T(8,128)S(1)}, f32[80,128]{1,0:T(8,128)S(1)}, u32[]{:S(2)}, u32[]{:S(2)}) collective-permute-start(f32[80,128]{1,0:T(8,128)S(1)} %get-tuple-element.110.mine_ref), channel_id=1, source_target_pairs={{0,1},{1,0},{2,3},{3,2},{4,5},{5,4},{6,7},{7,6},{8,9},{9,8},{10,11... | collective-permute-start | bytes 122888 | tf_op jit(solution)/shard_map/ppermute | solution.py:126
  39.3 2.5 %collective-permute-done.10.other_ref = f32[80,128]{1,0:T(8,128)S(1)} collective-permute-done((f32[80,128]{1,0:T(8,128)S(1)}, f32[80,128]{1,0:T(8,128)S(1)}, u32[]{:S(2)}, u32[]{:S(2)}) %collective-permute-start.10) | collective-permute-done | bytes 40992 | tf_op jit(solution)/shard_map/ppermute | solution.py:126
  41.8 0.0 collective-permute-start.12
  41.8 0.1 fourth.1
  41.9 2.4 %collective-permute-start.11 = (f32[8,128]{1,0:T(8,128)S(1)}, f32[8,128]{1,0:T(8,128)S(1)}, u32[]{:S(2)}, u32[]{:S(2)}) collective-permute-start(f32[8,128]{1,0:T(8,128)S(1)} %get-tuple-element.114), channel_id=1, source_target_pairs={{0,18},{2,16},{4,22},{6,20},{8,26},{10,24},{12,30},{14,28},{16,2},... | collective-permute-start | bytes 12296 | tf_op jit(solution)/shard_map/ppermute | solution.py:93
  44.4 1.6 %collective-permute-done.11 = f32[8,128]{1,0:T(8,128)S(1)} collective-permute-done((f32[8,128]{1,0:T(8,128)S(1)}, f32[8,128]{1,0:T(8,128)S(1)}, u32[]{:S(2)}, u32[]{:S(2)}) %collective-permute-start.11) | collective-permute-done | bytes 4128 | tf_op jit(solution)/shard_map/ppermute | solution.py:93
  45.9 0.0 collective-permute-done.12.high_ref
  45.9 2.0 %collective-permute-start.13 = (f32[8,128]{1,0:T(8,128)S(1)}, f32[8,128]{1,0:T(8,128)S(1)}, u32[]{:S(2)}, u32[]{:S(2)}) collective-permute-start(f32[8,128]{1,0:T(8,128)S(1)} %add.33), channel_id=1, source_target_pairs={{0,10},{2,8},{4,14},{6,12},{8,2},{10,0},{12,6},{14,4},{16,26},{18,... | collective-permute-start | bytes 12296 | tf_op jit(solution)/shard_map/ppermute | solution.py:93
  47.9 0.8 %last_smooth.1.refs_2_ = f32[8,128]{1,0:T(8,128)S(1)} custom-call(f32[132,8,128]{2,1,0:T(8,128)S(1)} %get-tuple-element.116.next_ref.refs_11_, f32[64,128]{1,0:T(8,128)S(1)} %slice.119.low_ref, f32[64,128]{1,0:T(8,128)S(1)} %collective-permute-done.12.high_ref, f32[128,128]{1,0:T(8,128)S(1)} %broadcast_in_dim.12.damp_ref, ...), custom_call_target="tpu_custom_call" | custom-call | tf_op jit(solution)/shard_map/last_smooth/pallas_call | solution.py:625
  48.7 0.5 collective-permute-done.13
  49.3 2.3 %collective-permute-start.14 = (f32[16,128]{1,0:T(8,128)S(1)}, f32[16,128]{1,0:T(8,128)S(1)}, u32[]{:S(2)}, u32[]{:S(2)}) collective-permute-start(f32[16,128]{1,0:T(8,128)S(1)} %pad_maximum_fusion.6), channel_id=1, source_target_pairs={{0,7},{1,6},{2,5},{3,4},{4,3},{5,2},{6,1},{7,0},{8,15},{9,14},{10,... | collective-permute-start | bytes 24584 | tf_op jit(solution)/shard_map/ppermute | solution.py:99
  51.5 1.7 %collective-permute-done.14 = f32[16,128]{1,0:T(8,128)S(1)} collective-permute-done((f32[16,128]{1,0:T(8,128)S(1)}, f32[16,128]{1,0:T(8,128)S(1)}, u32[]{:S(2)}, u32[]{:S(2)}) %collective-permute-start.14) | collective-permute-done | bytes 8224 | tf_op jit(solution)/shard_map/ppermute | solution.py:99
  53.3 0.4 collective-permute-start.15
  53.6 0.8 %collective-permute-done.15.refs_1_ = f32[8,128]{1,0:T(8,128)S(1)} collective-permute-done((f32[8,128]{1,0:T(8,128)S(1)}, f32[8,128]{1,0:T(8,128)S(1)}, u32[]{:S(2)}, u32[]{:S(2)}) %collective-permute-start.15) | collective-permute-done | bytes 4128 | tf_op jit(solution)/shard_map/ppermute | solution.py:101
  54.4 0.7 %end.1 = (f32[8,8,128]{2,1,0:T(8,128)}, f32[8,128]{1,0:T(8,128)}) custom-call(f32[8,128]{1,0:T(8,128)S(1)} %get-tuple-element.129.refs_0_, f32[8,128]{1,0:T(8,128)S(1)} %collective-permute-done.15.refs_1_, f32[8,128]{1,0:T(8,128)S(1)} %last_smooth.1.refs_2_, f32[8,128]{1,0:T(8,128)S(1)} %get-tuple-element.128.refs_3_, ...), custom_call_target="tpu_custom_call" | custom-call | tf_op jit(solution)/shard_map/end/pallas_call | solution.py:632
  (32 shorter events, 0.1 us)
Async XLA Ops:
  2.9 3.6 %copy-start.1 = (f32[64]{0:T(128)S(1)}, f32[64]{0:T(128)}, u32[]{:S(2)}) copy-start(f32[64]{0:T(128)} %param.17) | copy-start | bytes 772
  2.9 5.1 %collective-permute-start = (f32[40,128]{1,0:T(8,128)S(1)}, f32[40,128]{1,0:T(8,128)S(1)}, u32[]{:S(2)}, u32[]{:S(2)}) collective-permute-start(f32[40,128]{1,0:T(8,128)S(1)} %get-tuple-element.65), channel_id=1, source_target_pairs={{0,18},{2,16},{4,22},{6,20},{8,26},{10,24},{12,30},{14,28},{16,2},... | collective-permute-start | bytes 61448 | tf_op jit(solution)/shard_map/ppermute | solution.py:63
  8.0 3.5 %collective-permute-start.1 = (f32[72,128]{1,0:T(8,128)S(1)}, f32[72,128]{1,0:T(8,128)S(1)}, u32[]{:S(2)}, u32[]{:S(2)}) collective-permute-start(f32[72,128]{1,0:T(8,128)S(1)} %pad_maximum_fusion.4), channel_id=1, source_target_pairs={{0,10},{2,8},{4,14},{6,12},{8,2},{10,0},{12,6},{14,4},{16,26},{18,... | collective-permute-start | bytes 110600 | tf_op jit(solution)/shard_map/ppermute | solution.py:63
  11.6 4.1 %collective-permute-start.2 = (f32[136,128]{1,0:T(8,128)S(1)}, f32[136,128]{1,0:T(8,128)S(1)}, u32[]{:S(2)}, u32[]{:S(2)}) collective-permute-start(f32[136,128]{1,0:T(8,128)S(1)} %pad_maximum_fusion.2), channel_id=1, source_target_pairs={{0,6},{2,4},{4,2},{6,0},{8,14},{10,12},{12,10},{14,8},{16,22},{18,... | collective-permute-start | bytes 208904 | tf_op jit(solution)/shard_map/ppermute | solution.py:63
  15.7 1.4 %collective-permute-start.3 = (f32[264,128]{1,0:T(8,128)S(1)}, f32[264,128]{1,0:T(8,128)S(1)}, u32[]{:S(2)}, u32[]{:S(2)}) collective-permute-start(f32[264,128]{1,0:T(8,128)S(1)} %pad_maximum_fusion.mine_ref), channel_id=1, source_target_pairs={{0,2},{2,0},{4,6},{6,4},{8,10},{10,8},{12,14},{14,12},{16,18},{18,... | collective-permute-start | bytes 405512 | tf_op jit(solution)/shard_map/ppermute | solution.py:63
  17.9 4.9 %collective-permute-start.4 = (f32[144,128]{1,0:T(8,128)S(1)}, f32[144,128]{1,0:T(8,128)S(1)}, u32[]{:S(2)}, u32[]{:S(2)}) collective-permute-start(f32[144,128]{1,0:T(8,128)S(1)} %get-tuple-element.72.mine_ref), channel_id=1, source_target_pairs={{0,1},{1,0},{2,3},{3,2},{4,5},{5,4},{6,7},{7,6},{8,9},{9,8},{10,11... | collective-permute-start | bytes 221192 | tf_op jit(solution)/shard_map/ppermute | solution.py:115
  23.1 4.2 %collective-permute-start.5 = (f32[40,128]{1,0:T(8,128)S(1)}, f32[40,128]{1,0:T(8,128)S(1)}, u32[]{:S(2)}, u32[]{:S(2)}) collective-permute-start(f32[40,128]{1,0:T(8,128)S(1)} %get-tuple-element.81), channel_id=1, source_target_pairs={{0,18},{2,16},{4,22},{6,20},{8,26},{10,24},{12,30},{14,28},{16,2},... | collective-permute-start | bytes 61448 | tf_op jit(solution)/shard_map/ppermute | solution.py:63
  24.7 2.6 %collective-permute-start.6 = (f32[128,128]{1,0:T(8,128)S(1)}, f32[128,128]{1,0:T(8,128)S(1)}, u32[]{:S(2)}, u32[]{:S(2)}) collective-permute-start(f32[128,128]{1,0:T(8,128)S(1)} %slice.114.low_ref.high_ref), channel_id=1, source_target_pairs={{0,2},{2,0},{4,6},{6,4},{8,10},{10,8},{12,14},{14,12},{16,18},{18,... | collective-permute-start | bytes 196616 | tf_op jit(solution)/shard_map/ppermute | solution.py:117
  27.3 3.9 %collective-permute-start.7 = (f32[72,128]{1,0:T(8,128)S(1)}, f32[72,128]{1,0:T(8,128)S(1)}, u32[]{:S(2)}, u32[]{:S(2)}) collective-permute-start(f32[72,128]{1,0:T(8,128)S(1)} %pad_maximum_fusion.5), channel_id=1, source_target_pairs={{0,10},{2,8},{4,14},{6,12},{8,2},{10,0},{12,6},{14,4},{16,26},{18,... | collective-permute-start | bytes 110600 | tf_op jit(solution)/shard_map/ppermute | solution.py:63
  31.2 1.3 %copy-start = (s32[1,1,32]{2,1,0:T(1,128)S(1)}, s32[1,1,32]{2,1,0:T(1,128)}, u32[]{:S(2)}) copy-start(s32[1,1,32]{2,1,0:T(1,128)} %param.12) | copy-start | bytes 388
  31.2 4.2 %collective-permute-start.8 = (f32[136,128]{1,0:T(8,128)S(1)}, f32[136,128]{1,0:T(8,128)S(1)}, u32[]{:S(2)}, u32[]{:S(2)}) collective-permute-start(f32[136,128]{1,0:T(8,128)S(1)} %pad_maximum_fusion.3), channel_id=1, source_target_pairs={{0,6},{2,4},{4,2},{6,0},{8,14},{10,12},{12,10},{14,8},{16,22},{18,... | collective-permute-start | bytes 208904 | tf_op jit(solution)/shard_map/ppermute | solution.py:63
  35.5 1.4 %collective-permute-start.9 = (f32[264,128]{1,0:T(8,128)S(1)}, f32[264,128]{1,0:T(8,128)S(1)}, u32[]{:S(2)}, u32[]{:S(2)}) collective-permute-start(f32[264,128]{1,0:T(8,128)S(1)} %pad_maximum_fusion.1.mine_ref), channel_id=1, source_target_pairs={{0,2},{2,0},{4,6},{6,4},{8,10},{10,8},{12,14},{14,12},{16,18},{18,... | collective-permute-start | bytes 405512 | tf_op jit(solution)/shard_map/ppermute | solution.py:63
  37.7 4.1 %collective-permute-start.10 = (f32[80,128]{1,0:T(8,128)S(1)}, f32[80,128]{1,0:T(8,128)S(1)}, u32[]{:S(2)}, u32[]{:S(2)}) collective-permute-start(f32[80,128]{1,0:T(8,128)S(1)} %get-tuple-element.110.mine_ref), channel_id=1, source_target_pairs={{0,1},{1,0},{2,3},{3,2},{4,5},{5,4},{6,7},{7,6},{8,9},{9,8},{10,11... | collective-permute-start | bytes 122888 | tf_op jit(solution)/shard_map/ppermute | solution.py:126
  41.8 4.2 %collective-permute-start.12 = (f32[64,128]{1,0:T(8,128)S(1)}, f32[64,128]{1,0:T(8,128)S(1)}, u32[]{:S(2)}, u32[]{:S(2)}) collective-permute-start(f32[64,128]{1,0:T(8,128)S(1)} %slice.119.low_ref), channel_id=1, source_target_pairs={{0,2},{2,0},{4,6},{6,4},{8,10},{10,8},{12,14},{14,12},{16,18},{18,... | collective-permute-start | bytes 98312 | tf_op jit(solution)/shard_map/ppermute | solution.py:128
  41.9 4.0 %collective-permute-start.11 = (f32[8,128]{1,0:T(8,128)S(1)}, f32[8,128]{1,0:T(8,128)S(1)}, u32[]{:S(2)}, u32[]{:S(2)}) collective-permute-start(f32[8,128]{1,0:T(8,128)S(1)} %get-tuple-element.114), channel_id=1, source_target_pairs={{0,18},{2,16},{4,22},{6,20},{8,26},{10,24},{12,30},{14,28},{16,2},... | collective-permute-start | bytes 12296 | tf_op jit(solution)/shard_map/ppermute | solution.py:93
  45.9 3.3 %collective-permute-start.13 = (f32[8,128]{1,0:T(8,128)S(1)}, f32[8,128]{1,0:T(8,128)S(1)}, u32[]{:S(2)}, u32[]{:S(2)}) collective-permute-start(f32[8,128]{1,0:T(8,128)S(1)} %add.33), channel_id=1, source_target_pairs={{0,10},{2,8},{4,14},{6,12},{8,2},{10,0},{12,6},{14,4},{16,26},{18,... | collective-permute-start | bytes 12296 | tf_op jit(solution)/shard_map/ppermute | solution.py:93
  49.3 4.0 %collective-permute-start.14 = (f32[16,128]{1,0:T(8,128)S(1)}, f32[16,128]{1,0:T(8,128)S(1)}, u32[]{:S(2)}, u32[]{:S(2)}) collective-permute-start(f32[16,128]{1,0:T(8,128)S(1)} %pad_maximum_fusion.6), channel_id=1, source_target_pairs={{0,7},{1,6},{2,5},{3,4},{4,3},{5,2},{6,1},{7,0},{8,15},{9,14},{10,... | collective-permute-start | bytes 24584 | tf_op jit(solution)/shard_map/ppermute | solution.py:99
  53.3 1.2 %collective-permute-start.15 = (f32[8,128]{1,0:T(8,128)S(1)}, f32[8,128]{1,0:T(8,128)S(1)}, u32[]{:S(2)}, u32[]{:S(2)}) collective-permute-start(f32[8,128]{1,0:T(8,128)S(1)} %get-tuple-element.129.refs_0_), channel_id=1, source_target_pairs={{0,2},{2,0},{4,6},{6,4},{8,10},{10,8},{12,14},{14,12},{16,18},{18,... | collective-permute-start | bytes 12296 | tf_op jit(solution)/shard_map/ppermute | solution.py:101

commit v6 on v5

--- a/solution.py
+++ b/solution.py
@@ -150,14 +150,12 @@
         out_ref[pl.ds(k + 1, 1), :] = jnp.sum(pick_ref[k + 1] * product[:, LAT:], axis=0, keepdims=True)
 
 
-def push_lines(rays, lines, tiles_ref, pick_ref, first, last):
+def push_lines(rays, lines, turned_ref, pick_ref, first, last):
     for k in range(first, last, 2):
         both = [jnp.broadcast_to(lines[j : j + 1], (RT, LAT)) for j in (k, k + 1)]
-        product = lax.dot_general(
-            jnp.concatenate(both, axis=0).astype(BF16),
-            tiles_ref[pl.ds(k, 2)].reshape(2 * RAY_TILE, LAT),
-            (((1,), (1,)), ((), ())),
-            preferred_element_type=F32,
+        pair = jnp.concatenate([turned_ref[k], turned_ref[k + 1]], axis=1)
+        product = jnp.dot(
+            jnp.concatenate(both, axis=0).astype(BF16), pair, preferred_element_type=F32
         )
         rays = rays + pick_ref[k] * product[:RT, :RAY_TILE]
         rays = rays + pick_ref[k + 1] * product[RT:, RAY_TILE:]
@@ -248,6 +246,11 @@
     pull_lines(weight * start, tiles_ref, pick_ref, packet_ref, slots)
 
 
+def turn_body(tiles_ref, turned_ref):
+    for k in range(tiles_ref.shape[0]):
+        turned_ref[k] = tiles_ref[k].T
+
+
 def own_place():
     count, at = lax.axis_size("ray"), lax.axis_index("ray")
     side, place, bit = at % 2, 0, 1
@@ -290,7 +293,7 @@
     return found[:, :LAT] + found[:, LAT:]
 
 
-CHUNK = 128
+CHUNK = 256
 
 
 def onehot_of(names, ids):
@@ -316,7 +319,7 @@
         field_ref[first // LON_DEV : (first + CHUNK) // LON_DEV] = piece
 
 
-def first_body(slots, other_ref, half_ref, half_lines_ref, mine_ref, own_ref, pick_ref, tiles_ref,
+def first_body(slots, other_ref, half_ref, half_lines_ref, mine_ref, own_ref, pick_ref, turned_ref,
                field_ref, lines_ref, out_ref, left_ref, names_ref):
     names = names_of(other_ref, 1 - own_place()[0], slots)
     for j, piece in enumerate(names):
@@ -335,7 +338,7 @@
         piece = found_lines(onehot, parts).reshape(count, LON_DEV, LAT) + half_ref[pair : pair + count]
         field_ref[pair + PAD : pair + PAD + count] = piece
         square = square + jnp.sum(piece * piece, axis=0)
-        rays = push_lines(rays, lines, tiles_ref, pick_ref, first // CHUNK * part, (first // CHUNK + 1) * part)
+        rays = push_lines(rays, lines, turned_ref, pick_ref, first // CHUNK * part, (first // CHUNK + 1) * part)
     out_ref[:RT, :] = rays
     out_ref[RT : RT + 8, :] = jnp.broadcast_to(total(square), (8, LAT))
     odd = lax.axis_index("ray") % 2
@@ -434,7 +437,7 @@
 
 
 def third_body(slots, other_ref, half_ref, half_lines_ref, mine_ref, square_ref, onehot_ref, names_ref, own_ref,
-               lines_ref, field_ref, norm_ref, pick_ref, tiles_ref,
+               lines_ref, field_ref, norm_ref, pick_ref, turned_ref,
                next_ref, out_ref, shift_ref):
     shift = jnp.broadcast_to(extra_row(mine_ref, slots, 0) + extra_row(other_ref, slots, 0), (8, LAT))
     shift_ref[...] = shift
@@ -457,7 +460,7 @@
         next_ref[pair + PAD : pair + PAD + count] = piece
         square = square + jnp.sum(piece * piece, axis=0)
         cross = cross + jnp.sum(piece * base, axis=0)
-        rays = push_lines(rays, lines, tiles_ref, pick_ref, first // CHUNK * part, (first // CHUNK + 1) * part)
+        rays = push_lines(rays, lines, turned_ref, pick_ref, first // CHUNK * part, (first // CHUNK + 1) * part)
     sub = sub_iota()
     out_ref[:RT, :] = rays
     out_ref[RT : RT + 8, :] = jnp.where(
@@ -573,7 +576,8 @@
     )(tile_count, *(pltpu.with_memory_space_constraint(x, pltpu.MemorySpace.HBM) for x in (
         tile_row[0, 0], col_index, tile_scale[0, 0], receiver_weight,
         ray_receiver.reshape(held), delays.reshape(held), block)))
-    near, far, damp = gather_rays(mine, extra, (lambda _: damp,))
+    turn = lambda given: (given, *local_call(turn_body, "turn", [VM], [(block.shape, BF16)])(block))
+    near, far, (damp, turned) = gather_rays(mine, extra, (lambda _: damp, turn))
     named = ((names_n, LAT), jnp.int32)
 
     half, half_lines, names_a = local_call(
@@ -583,7 +587,7 @@
     field, lines, sums, left0, names_b = local_call(
         functools.partial(first_body, slots), "first", [VM] * 7,
         [padded, ((slots, LAT), F32), ((RT + 8 + PAIRS, LAT), F32), row, named],
-    )(far, half, half_lines, near, own, pick, block)
+    )(far, half, half_lines, near, own, pick, turned)
     others, columns, swapped = first_halo(sums, field)
     onehots = local_call(
         onehot_body, "onehot", [VM] * 2, [((LINES, names_n * LAT), BF16)] * 2,
@@ -615,7 +619,7 @@
     following, sums, shift = local_call(
         functools.partial(third_body, slots), "third", [VM] * 13,
         [padded, ((RT + 8 + PAIRS // 2, LAT), F32), row],
-    )(far, half, half_lines, near, square, onehot_b, names_b, own, lines, field, norm0, pick, block)
+    )(far, half, half_lines, near, square, onehot_b, names_b, own, lines, field, norm0, pick, turned)
     others, beside, halves = next_halo(sums, following)
     last_rays, left1, rest, norm1, ray_square = local_call(
         fourth_body, "fourth", [VM] * 6, [(held, F32), row, row, row, row],

time: 55.3 us -> 54.8 us (level)
  transfers between devices with their start and end apart: 16 -> 16, of which waited for: 14 -> 14; matrix products, arithmetic and copies ran while one was open for 0% -> 0% of each run, Pallas kernels for 7% -> 8%
where the time goes in v6:
time: 54.8 us; the launch traced here: 54.6 us
  starting transfers between devices  25.3 us (46%)
  waiting for transfers between devices  19.6 us (36%)
  Pallas kernels  7.93 us (14%)
  between operations  1.45 us (3%)
    ppermute x8, starting transfers between devices, gather_rays(): other = lax.ppermute(packet, 'ray', pairs_of(count, step))  12.8 us
    ppermute x8, waiting for transfers between devices, gather_rays(): other = lax.ppermute(packet, 'ray', pairs_of(count, step))  10.1 us
    ppermute x2, starting transfers between devices, last_sums(): value = value + lax.ppermute(value, 'ray', pairs_of(count, step))  4.39 us
    ppermute x1, waiting for transfers between devices, next_halo(): other = lax.ppermute(sums, 'vox', [(0, 1), (1, 0)])  2.48 us
    ppermute x1, waiting for transfers between devices, first_halo(): other = lax.ppermute(sums, 'vox', [(0, 1), (1, 0)])  2.37 us
    ppermute x1, starting transfers between devices, last_sums(): lax.ppermute(both, ('ray', 'vox'), [(i, i ^ 7) for i in range(2 * count)])  2.3 us
    ppermute x1, starting transfers between devices, first_halo(): other = lax.ppermute(sums, 'vox', [(0, 1), (1, 0)])  2.28 us
    ppermute x2, waiting for transfers between devices, last_sums(): value = value + lax.ppermute(value, 'ray', pairs_of(count, step))  2.1 us
  transfers between devices with their start and end apart: 16, of which 14 were waited for; matrix products, arithmetic and copies ran while one was open for 0% of the time, Pallas kernels for 8%

profile of v6, /device:TPU:0, one launch (start us, length us, event | category | flops | bytes accessed | tf_op | source)
XLA Modules:
  0.0 54.6 jit_solution(18432577278946188411)
XLA Ops:
  1.3 1.6 %start.1 = (f32[40,128]{1,0:T(8,128)S(1)}, f32[8,128]{1,0:T(8,128)S(1)}, f32[8,128]{1,0:T(8,128)S(1)}, f32[32,8,128]{2,1,0:T(8,128)S(1)}, s32[32,128]{1,0:T(8,128)S(1)}, /*index=5*/bf16[32,128,128]{2,1,0:T(8,128)(2,1)S(1)}) custom-call(s32[1,1]{1,0:T(1,128)S(6)} %copy.11.count_ref, s32[32]{0:T(128)} %bitcast.13, s32[32]{0:T(128)} %bitcast.8, f32[32]{0:T(128)} %bitcast.14, ...), custom_call_target="tpu_custom_call" | custom-call | tf_op jit(solution)/shard_map/start/pallas_call | solution.py:569
  2.9 0.0 copy-start.1
  2.9 3.5 %collective-permute-start = (f32[40,128]{1,0:T(8,128)S(1)}, f32[40,128]{1,0:T(8,128)S(1)}, u32[]{:S(2)}, u32[]{:S(2)}) collective-permute-start(f32[40,128]{1,0:T(8,128)S(1)} %get-tuple-element.68), channel_id=1, source_target_pairs={{0,18},{2,16},{4,22},{6,20},{8,26},{10,24},{12,30},{14,28},{16,2},... | collective-permute-start | bytes 61448 | tf_op jit(solution)/shard_map/ppermute | solution.py:63
  6.4 0.1 broadcast_in_dim.10
  6.5 0.1 broadcast_in_dim.11
  6.6 1.3 %collective-permute-done = f32[40,128]{1,0:T(8,128)S(1)} collective-permute-done((f32[40,128]{1,0:T(8,128)S(1)}, f32[40,128]{1,0:T(8,128)S(1)}, u32[]{:S(2)}, u32[]{:S(2)}) %collective-permute-start) | collective-permute-done | bytes 20512 | tf_op jit(solution)/shard_map/ppermute | solution.py:63
  8.0 0.1 broadcast_in_dim.12.damp_ref
  8.0 1.9 %collective-permute-start.1 = (f32[72,128]{1,0:T(8,128)S(1)}, f32[72,128]{1,0:T(8,128)S(1)}, u32[]{:S(2)}, u32[]{:S(2)}) collective-permute-start(f32[72,128]{1,0:T(8,128)S(1)} %pad_maximum_fusion.4), channel_id=1, source_target_pairs={{0,10},{2,8},{4,14},{6,12},{8,2},{10,0},{12,6},{14,4},{16,26},{18,... | collective-permute-start | bytes 110600 | tf_op jit(solution)/shard_map/ppermute | solution.py:63
  9.9 0.3 turn.1.turned_ref
  10.3 1.3 %collective-permute-done.1 = f32[72,128]{1,0:T(8,128)S(1)} collective-permute-done((f32[72,128]{1,0:T(8,128)S(1)}, f32[72,128]{1,0:T(8,128)S(1)}, u32[]{:S(2)}, u32[]{:S(2)}) %collective-permute-start.1) | collective-permute-done | bytes 36896 | tf_op jit(solution)/shard_map/ppermute | solution.py:63
  11.6 1.8 %collective-permute-start.2 = (f32[136,128]{1,0:T(8,128)S(1)}, f32[136,128]{1,0:T(8,128)S(1)}, u32[]{:S(2)}, u32[]{:S(2)}) collective-permute-start(f32[136,128]{1,0:T(8,128)S(1)} %pad_maximum_fusion.2), channel_id=1, source_target_pairs={{0,6},{2,4},{4,2},{6,0},{8,14},{10,12},{12,10},{14,8},{16,22},{18,... | collective-permute-start | bytes 208904 | tf_op jit(solution)/shard_map/ppermute | solution.py:63
  13.4 2.3 %collective-permute-done.2 = f32[136,128]{1,0:T(8,128)S(1)} collective-permute-done((f32[136,128]{1,0:T(8,128)S(1)}, f32[136,128]{1,0:T(8,128)S(1)}, u32[]{:S(2)}, u32[]{:S(2)}) %collective-permute-start.2) | collective-permute-done | bytes 69664 | tf_op jit(solution)/shard_map/ppermute | solution.py:63
  15.7 0.3 collective-permute-start.3
  16.1 0.3 first_half.1
  16.4 0.8 %collective-permute-done.3.other_ref = f32[264,128]{1,0:T(8,128)S(1)} collective-permute-done((f32[264,128]{1,0:T(8,128)S(1)}, f32[264,128]{1,0:T(8,128)S(1)}, u32[]{:S(2)}, u32[]{:S(2)}) %collective-permute-start.3) | collective-permute-done | bytes 135200 | tf_op jit(solution)/shard_map/ppermute | solution.py:63
  17.1 0.6 %first.1 = (f32[132,8,128]{2,1,0:T(8,128)S(1)}, f32[32,128]{1,0:T(8,128)S(1)}, f32[144,128]{1,0:T(8,128)S(1)}, f32[8,128]{1,0:T(8,128)S(1)}, s32[2,128]{1,0:T(2,128)S(1)}) custom-call(f32[264,128]{1,0:T(8,128)S(1)} %collective-permute-done.3.other_ref, f32[128,8,128]{2,1,0:T(8,128)S(1)} %get-tuple-element.74.half_ref, ...), custom_call_target="tpu_custom_call" | custom-call | tf_op jit(solution)/shard_map/first/pallas_call | solution.py:587
  17.7 2.3 %collective-permute-start.4 = (f32[144,128]{1,0:T(8,128)S(1)}, f32[144,128]{1,0:T(8,128)S(1)}, u32[]{:S(2)}, u32[]{:S(2)}) collective-permute-start(f32[144,128]{1,0:T(8,128)S(1)} %get-tuple-element.78.mine_ref), channel_id=1, source_target_pairs={{0,1},{1,0},{2,3},{3,2},{4,5},{5,4},{6,7},{7,6},{8,9},{9,8},{10,11... | collective-permute-start | bytes 221192 | tf_op jit(solution)/shard_map/ppermute | solution.py:115
  20.0 0.2 onehot.1
  20.2 2.4 %collective-permute-done.4.other_ref = f32[144,128]{1,0:T(8,128)S(1)} collective-permute-done((f32[144,128]{1,0:T(8,128)S(1)}, f32[144,128]{1,0:T(8,128)S(1)}, u32[]{:S(2)}, u32[]{:S(2)}) %collective-permute-start.4) | collective-permute-done | bytes 73760 | tf_op jit(solution)/shard_map/ppermute | solution.py:115
  22.6 0.3 second.1
  22.8 1.6 %collective-permute-start.5 = (f32[40,128]{1,0:T(8,128)S(1)}, f32[40,128]{1,0:T(8,128)S(1)}, u32[]{:S(2)}, u32[]{:S(2)}) collective-permute-start(f32[40,128]{1,0:T(8,128)S(1)} %get-tuple-element.87), channel_id=1, source_target_pairs={{0,18},{2,16},{4,22},{6,20},{8,26},{10,24},{12,30},{14,28},{16,2},... | collective-permute-start | bytes 61448 | tf_op jit(solution)/shard_map/ppermute | solution.py:63
  24.4 1.5 %collective-permute-start.6 = (f32[128,128]{1,0:T(8,128)S(1)}, f32[128,128]{1,0:T(8,128)S(1)}, u32[]{:S(2)}, u32[]{:S(2)}) collective-permute-start(f32[128,128]{1,0:T(8,128)S(1)} %slice.120.low_ref.high_ref), channel_id=1, source_target_pairs={{0,2},{2,0},{4,6},{6,4},{8,10},{10,8},{12,14},{14,12},{16,18},{18,... | collective-permute-start | bytes 196616 | tf_op jit(solution)/shard_map/ppermute | solution.py:117
  26.0 1.0 %collective-permute-done.5 = f32[40,128]{1,0:T(8,128)S(1)} collective-permute-done((f32[40,128]{1,0:T(8,128)S(1)}, f32[40,128]{1,0:T(8,128)S(1)}, u32[]{:S(2)}, u32[]{:S(2)}) %collective-permute-start.5) | collective-permute-done | bytes 20512 | tf_op jit(solution)/shard_map/ppermute | solution.py:63
  27.0 2.1 %collective-permute-start.7 = (f32[72,128]{1,0:T(8,128)S(1)}, f32[72,128]{1,0:T(8,128)S(1)}, u32[]{:S(2)}, u32[]{:S(2)}) collective-permute-start(f32[72,128]{1,0:T(8,128)S(1)} %pad_maximum_fusion.5), channel_id=1, source_target_pairs={{0,10},{2,8},{4,14},{6,12},{8,2},{10,0},{12,6},{14,4},{16,26},{18,... | collective-permute-start | bytes 110600 | tf_op jit(solution)/shard_map/ppermute | solution.py:63
  29.1 0.9 %smooth.1 = (f32[128,8,128]{2,1,0:T(8,128)S(1)}, f32[132,8,128]{2,1,0:T(8,128)S(1)}, f32[2,128,128]{2,1,0:T(8,128)S(1)}, f32[8,128]{1,0:T(8,128)S(1)}) custom-call(f32[132,8,128]{2,1,0:T(8,128)S(1)} %get-tuple-element.89.field_ref.refs_10_, f32[128,128]{1,0:T(8,128)S(1)} %slice.120.low_ref.high_ref, ...), custom_call_target="tpu_custom_call" | custom-call | tf_op jit(solution)/shard_map/smooth/pallas_call | solution.py:601
  30.0 0.9 %collective-permute-done.7 = f32[72,128]{1,0:T(8,128)S(1)} collective-permute-done((f32[72,128]{1,0:T(8,128)S(1)}, f32[72,128]{1,0:T(8,128)S(1)}, u32[]{:S(2)}, u32[]{:S(2)}) %collective-permute-start.7) | collective-permute-done | bytes 36896 | tf_op jit(solution)/shard_map/ppermute | solution.py:63
  30.9 0.0 copy-start
  30.9 1.3 %collective-permute-start.8 = (f32[136,128]{1,0:T(8,128)S(1)}, f32[136,128]{1,0:T(8,128)S(1)}, u32[]{:S(2)}, u32[]{:S(2)}) collective-permute-start(f32[136,128]{1,0:T(8,128)S(1)} %pad_maximum_fusion.3), channel_id=1, source_target_pairs={{0,6},{2,4},{4,2},{6,0},{8,14},{10,12},{12,10},{14,8},{16,22},{18,... | collective-permute-start | bytes 208904 | tf_op jit(solution)/shard_map/ppermute | solution.py:63
  32.2 1.3 %again.1 = (f32[128,8,128]{2,1,0:T(8,128)S(1)}, f32[32,128]{1,0:T(8,128)S(1)}) custom-call(s32[32]{0:T(128)S(1)} %bitcast.9, f32[132,8,128]{2,1,0:T(8,128)S(1)} %get-tuple-element.103.scaled_ref, f32[2,128,128]{2,1,0:T(8,128)S(1)} %get-tuple-element.104.far_ref), custom_call_target="tpu_custom_call" | custom-call | tf_op jit(solution)/shard_map/again/pallas_call | solution.py:608
  33.5 1.7 %collective-permute-done.8 = f32[136,128]{1,0:T(8,128)S(1)} collective-permute-done((f32[136,128]{1,0:T(8,128)S(1)}, f32[136,128]{1,0:T(8,128)S(1)}, u32[]{:S(2)}, u32[]{:S(2)}) %collective-permute-start.8) | collective-permute-done | bytes 69664 | tf_op jit(solution)/shard_map/ppermute | solution.py:63
  35.2 0.2 collective-permute-start.9
  35.4 0.3 third_half.1
  35.7 0.9 %collective-permute-done.9.other_ref = f32[264,128]{1,0:T(8,128)S(1)} collective-permute-done((f32[264,128]{1,0:T(8,128)S(1)}, f32[264,128]{1,0:T(8,128)S(1)}, u32[]{:S(2)}, u32[]{:S(2)}) %collective-permute-start.9) | collective-permute-done | bytes 135200 | tf_op jit(solution)/shard_map/ppermute | solution.py:63
  36.6 0.6 %third.1 = (f32[132,8,128]{2,1,0:T(8,128)S(1)}, f32[80,128]{1,0:T(8,128)S(1)}, f32[8,128]{1,0:T(8,128)S(1)}) custom-call(f32[264,128]{1,0:T(8,128)S(1)} %collective-permute-done.9.other_ref, f32[128,8,128]{2,1,0:T(8,128)S(1)} %get-tuple-element.111.half_ref, f32[32,128]{1,0:T(8,128)S(1)} %get-tuple-element.112.half_lines_ref, ...), custom_call_target="tpu_custom_call" | custom-call | tf_op jit(solution)/shard_map/third/pallas_call | solution.py:619
  37.2 1.6 %collective-permute-start.10 = (f32[80,128]{1,0:T(8,128)S(1)}, f32[80,128]{1,0:T(8,128)S(1)}, u32[]{:S(2)}, u32[]{:S(2)}) collective-permute-start(f32[80,128]{1,0:T(8,128)S(1)} %get-tuple-element.116.mine_ref), channel_id=1, source_target_pairs={{0,1},{1,0},{2,3},{3,2},{4,5},{5,4},{6,7},{7,6},{8,9},{9,8},{10,11... | collective-permute-start | bytes 122888 | tf_op jit(solution)/shard_map/ppermute | solution.py:126
  38.8 2.5 %collective-permute-done.10.other_ref = f32[80,128]{1,0:T(8,128)S(1)} collective-permute-done((f32[80,128]{1,0:T(8,128)S(1)}, f32[80,128]{1,0:T(8,128)S(1)}, u32[]{:S(2)}, u32[]{:S(2)}) %collective-permute-start.10) | collective-permute-done | bytes 40992 | tf_op jit(solution)/shard_map/ppermute | solution.py:126
  41.3 0.0 collective-permute-start.12
  41.3 0.1 fourth.1
  41.4 2.4 %collective-permute-start.11 = (f32[8,128]{1,0:T(8,128)S(1)}, f32[8,128]{1,0:T(8,128)S(1)}, u32[]{:S(2)}, u32[]{:S(2)}) collective-permute-start(f32[8,128]{1,0:T(8,128)S(1)} %get-tuple-element.120), channel_id=1, source_target_pairs={{0,18},{2,16},{4,22},{6,20},{8,26},{10,24},{12,30},{14,28},{16,2},... | collective-permute-start | bytes 12296 | tf_op jit(solution)/shard_map/ppermute | solution.py:93
  43.9 1.6 %collective-permute-done.11 = f32[8,128]{1,0:T(8,128)S(1)} collective-permute-done((f32[8,128]{1,0:T(8,128)S(1)}, f32[8,128]{1,0:T(8,128)S(1)}, u32[]{:S(2)}, u32[]{:S(2)}) %collective-permute-start.11) | collective-permute-done | bytes 4128 | tf_op jit(solution)/shard_map/ppermute | solution.py:93
  45.4 2.0 %collective-permute-start.13 = (f32[8,128]{1,0:T(8,128)S(1)}, f32[8,128]{1,0:T(8,128)S(1)}, u32[]{:S(2)}, u32[]{:S(2)}) collective-permute-start(f32[8,128]{1,0:T(8,128)S(1)} %add.33), channel_id=1, source_target_pairs={{0,10},{2,8},{4,14},{6,12},{8,2},{10,0},{12,6},{14,4},{16,26},{18,... | collective-permute-start | bytes 12296 | tf_op jit(solution)/shard_map/ppermute | solution.py:93
  47.4 0.8 %last_smooth.1.refs_2_ = f32[8,128]{1,0:T(8,128)S(1)} custom-call(f32[132,8,128]{2,1,0:T(8,128)S(1)} %get-tuple-element.122.next_ref.refs_11_, f32[64,128]{1,0:T(8,128)S(1)} %slice.125.low_ref, f32[64,128]{1,0:T(8,128)S(1)} %collective-permute-done.12.high_ref, f32[128,128]{1,0:T(8,128)S(1)} %broadcast_in_dim.12.damp_ref, ...), custom_call_target="tpu_custom_call" | custom-call | tf_op jit(solution)/shard_map/last_smooth/pallas_call | solution.py:629
  48.2 0.5 collective-permute-done.13
  48.8 2.3 %collective-permute-start.14 = (f32[16,128]{1,0:T(8,128)S(1)}, f32[16,128]{1,0:T(8,128)S(1)}, u32[]{:S(2)}, u32[]{:S(2)}) collective-permute-start(f32[16,128]{1,0:T(8,128)S(1)} %pad_maximum_fusion.6), channel_id=1, source_target_pairs={{0,7},{1,6},{2,5},{3,4},{4,3},{5,2},{6,1},{7,0},{8,15},{9,14},{10,... | collective-permute-start | bytes 24584 | tf_op jit(solution)/shard_map/ppermute | solution.py:99
  51.0 1.7 %collective-permute-done.14 = f32[16,128]{1,0:T(8,128)S(1)} collective-permute-done((f32[16,128]{1,0:T(8,128)S(1)}, f32[16,128]{1,0:T(8,128)S(1)}, u32[]{:S(2)}, u32[]{:S(2)}) %collective-permute-start.14) | collective-permute-done | bytes 8224 | tf_op jit(solution)/shard_map/ppermute | solution.py:99
  52.8 0.4 collective-permute-start.15
  53.1 0.8 %collective-permute-done.15.refs_1_ = f32[8,128]{1,0:T(8,128)S(1)} collective-permute-done((f32[8,128]{1,0:T(8,128)S(1)}, f32[8,128]{1,0:T(8,128)S(1)}, u32[]{:S(2)}, u32[]{:S(2)}) %collective-permute-start.15) | collective-permute-done | bytes 4128 | tf_op jit(solution)/shard_map/ppermute | solution.py:101
  54.0 0.7 %end.1 = (f32[8,8,128]{2,1,0:T(8,128)}, f32[8,128]{1,0:T(8,128)}) custom-call(f32[8,128]{1,0:T(8,128)S(1)} %get-tuple-element.135.refs_0_, f32[8,128]{1,0:T(8,128)S(1)} %collective-permute-done.15.refs_1_, f32[8,128]{1,0:T(8,128)S(1)} %last_smooth.1.refs_2_, f32[8,128]{1,0:T(8,128)S(1)} %get-tuple-element.134.refs_3_, ...), custom_call_target="tpu_custom_call" | custom-call | tf_op jit(solution)/shard_map/end/pallas_call | solution.py:636
  (34 shorter events, 0.1 us)
Async XLA Ops:
  2.9 3.6 %copy-start.1 = (f32[64]{0:T(128)S(1)}, f32[64]{0:T(128)}, u32[]{:S(2)}) copy-start(f32[64]{0:T(128)} %param.17) | copy-start | bytes 772
  2.9 5.1 %collective-permute-start = (f32[40,128]{1,0:T(8,128)S(1)}, f32[40,128]{1,0:T(8,128)S(1)}, u32[]{:S(2)}, u32[]{:S(2)}) collective-permute-start(f32[40,128]{1,0:T(8,128)S(1)} %get-tuple-element.68), channel_id=1, source_target_pairs={{0,18},{2,16},{4,22},{6,20},{8,26},{10,24},{12,30},{14,28},{16,2},... | collective-permute-start | bytes 61448 | tf_op jit(solution)/shard_map/ppermute | solution.py:63
  8.0 3.5 %collective-permute-start.1 = (f32[72,128]{1,0:T(8,128)S(1)}, f32[72,128]{1,0:T(8,128)S(1)}, u32[]{:S(2)}, u32[]{:S(2)}) collective-permute-start(f32[72,128]{1,0:T(8,128)S(1)} %pad_maximum_fusion.4), channel_id=1, source_target_pairs={{0,10},{2,8},{4,14},{6,12},{8,2},{10,0},{12,6},{14,4},{16,26},{18,... | collective-permute-start | bytes 110600 | tf_op jit(solution)/shard_map/ppermute | solution.py:63
  11.6 4.1 %collective-permute-start.2 = (f32[136,128]{1,0:T(8,128)S(1)}, f32[136,128]{1,0:T(8,128)S(1)}, u32[]{:S(2)}, u32[]{:S(2)}) collective-permute-start(f32[136,128]{1,0:T(8,128)S(1)} %pad_maximum_fusion.2), channel_id=1, source_target_pairs={{0,6},{2,4},{4,2},{6,0},{8,14},{10,12},{12,10},{14,8},{16,22},{18,... | collective-permute-start | bytes 208904 | tf_op jit(solution)/shard_map/ppermute | solution.py:63
  15.7 1.4 %collective-permute-start.3 = (f32[264,128]{1,0:T(8,128)S(1)}, f32[264,128]{1,0:T(8,128)S(1)}, u32[]{:S(2)}, u32[]{:S(2)}) collective-permute-start(f32[264,128]{1,0:T(8,128)S(1)} %pad_maximum_fusion.mine_ref), channel_id=1, source_target_pairs={{0,2},{2,0},{4,6},{6,4},{8,10},{10,8},{12,14},{14,12},{16,18},{18,... | collective-permute-start | bytes 405512 | tf_op jit(solution)/shard_map/ppermute | solution.py:63
  17.7 4.9 %collective-permute-start.4 = (f32[144,128]{1,0:T(8,128)S(1)}, f32[144,128]{1,0:T(8,128)S(1)}, u32[]{:S(2)}, u32[]{:S(2)}) collective-permute-start(f32[144,128]{1,0:T(8,128)S(1)} %get-tuple-element.78.mine_ref), channel_id=1, source_target_pairs={{0,1},{1,0},{2,3},{3,2},{4,5},{5,4},{6,7},{7,6},{8,9},{9,8},{10,11... | collective-permute-start | bytes 221192 | tf_op jit(solution)/shard_map/ppermute | solution.py:115
  22.8 4.2 %collective-permute-start.5 = (f32[40,128]{1,0:T(8,128)S(1)}, f32[40,128]{1,0:T(8,128)S(1)}, u32[]{:S(2)}, u32[]{:S(2)}) collective-permute-start(f32[40,128]{1,0:T(8,128)S(1)} %get-tuple-element.87), channel_id=1, source_target_pairs={{0,18},{2,16},{4,22},{6,20},{8,26},{10,24},{12,30},{14,28},{16,2},... | collective-permute-start | bytes 61448 | tf_op jit(solution)/shard_map/ppermute | solution.py:63
  24.4 2.6 %collective-permute-start.6 = (f32[128,128]{1,0:T(8,128)S(1)}, f32[128,128]{1,0:T(8,128)S(1)}, u32[]{:S(2)}, u32[]{:S(2)}) collective-permute-start(f32[128,128]{1,0:T(8,128)S(1)} %slice.120.low_ref.high_ref), channel_id=1, source_target_pairs={{0,2},{2,0},{4,6},{6,4},{8,10},{10,8},{12,14},{14,12},{16,18},{18,... | collective-permute-start | bytes 196616 | tf_op jit(solution)/shard_map/ppermute | solution.py:117
  27.0 3.9 %collective-permute-start.7 = (f32[72,128]{1,0:T(8,128)S(1)}, f32[72,128]{1,0:T(8,128)S(1)}, u32[]{:S(2)}, u32[]{:S(2)}) collective-permute-start(f32[72,128]{1,0:T(8,128)S(1)} %pad_maximum_fusion.5), channel_id=1, source_target_pairs={{0,10},{2,8},{4,14},{6,12},{8,2},{10,0},{12,6},{14,4},{16,26},{18,... | collective-permute-start | bytes 110600 | tf_op jit(solution)/shard_map/ppermute | solution.py:63
  30.9 1.3 %copy-start = (s32[1,1,32]{2,1,0:T(1,128)S(1)}, s32[1,1,32]{2,1,0:T(1,128)}, u32[]{:S(2)}) copy-start(s32[1,1,32]{2,1,0:T(1,128)} %param.12) | copy-start | bytes 388
  30.9 4.2 %collective-permute-start.8 = (f32[136,128]{1,0:T(8,128)S(1)}, f32[136,128]{1,0:T(8,128)S(1)}, u32[]{:S(2)}, u32[]{:S(2)}) collective-permute-start(f32[136,128]{1,0:T(8,128)S(1)} %pad_maximum_fusion.3), channel_id=1, source_target_pairs={{0,6},{2,4},{4,2},{6,0},{8,14},{10,12},{12,10},{14,8},{16,22},{18,... | collective-permute-start | bytes 208904 | tf_op jit(solution)/shard_map/ppermute | solution.py:63
  35.2 1.4 %collective-permute-start.9 = (f32[264,128]{1,0:T(8,128)S(1)}, f32[264,128]{1,0:T(8,128)S(1)}, u32[]{:S(2)}, u32[]{:S(2)}) collective-permute-start(f32[264,128]{1,0:T(8,128)S(1)} %pad_maximum_fusion.1.mine_ref), channel_id=1, source_target_pairs={{0,2},{2,0},{4,6},{6,4},{8,10},{10,8},{12,14},{14,12},{16,18},{18,... | collective-permute-start | bytes 405512 | tf_op jit(solution)/shard_map/ppermute | solution.py:63
  37.2 4.1 %collective-permute-start.10 = (f32[80,128]{1,0:T(8,128)S(1)}, f32[80,128]{1,0:T(8,128)S(1)}, u32[]{:S(2)}, u32[]{:S(2)}) collective-permute-start(f32[80,128]{1,0:T(8,128)S(1)} %get-tuple-element.116.mine_ref), channel_id=1, source_target_pairs={{0,1},{1,0},{2,3},{3,2},{4,5},{5,4},{6,7},{7,6},{8,9},{9,8},{10,11... | collective-permute-start | bytes 122888 | tf_op jit(solution)/shard_map/ppermute | solution.py:126
  41.3 4.2 %collective-permute-start.12 = (f32[64,128]{1,0:T(8,128)S(1)}, f32[64,128]{1,0:T(8,128)S(1)}, u32[]{:S(2)}, u32[]{:S(2)}) collective-permute-start(f32[64,128]{1,0:T(8,128)S(1)} %slice.125.low_ref), channel_id=1, source_target_pairs={{0,2},{2,0},{4,6},{6,4},{8,10},{10,8},{12,14},{14,12},{16,18},{18,... | collective-permute-start | bytes 98312 | tf_op jit(solution)/shard_map/ppermute | solution.py:128
  41.4 4.0 %collective-permute-start.11 = (f32[8,128]{1,0:T(8,128)S(1)}, f32[8,128]{1,0:T(8,128)S(1)}, u32[]{:S(2)}, u32[]{:S(2)}) collective-permute-start(f32[8,128]{1,0:T(8,128)S(1)} %get-tuple-element.120), channel_id=1, source_target_pairs={{0,18},{2,16},{4,22},{6,20},{8,26},{10,24},{12,30},{14,28},{16,2},... | collective-permute-start | bytes 12296 | tf_op jit(solution)/shard_map/ppermute | solution.py:93
  45.4 3.3 %collective-permute-start.13 = (f32[8,128]{1,0:T(8,128)S(1)}, f32[8,128]{1,0:T(8,128)S(1)}, u32[]{:S(2)}, u32[]{:S(2)}) collective-permute-start(f32[8,128]{1,0:T(8,128)S(1)} %add.33), channel_id=1, source_target_pairs={{0,10},{2,8},{4,14},{6,12},{8,2},{10,0},{12,6},{14,4},{16,26},{18,... | collective-permute-start | bytes 12296 | tf_op jit(solution)/shard_map/ppermute | solution.py:93
  48.8 4.0 %collective-permute-start.14 = (f32[16,128]{1,0:T(8,128)S(1)}, f32[16,128]{1,0:T(8,128)S(1)}, u32[]{:S(2)}, u32[]{:S(2)}) collective-permute-start(f32[16,128]{1,0:T(8,128)S(1)} %pad_maximum_fusion.6), channel_id=1, source_target_pairs={{0,7},{1,6},{2,5},{3,4},{4,3},{5,2},{6,1},{7,0},{8,15},{9,14},{10,... | collective-permute-start | bytes 24584 | tf_op jit(solution)/shard_map/ppermute | solution.py:99
  52.8 1.2 %collective-permute-start.15 = (f32[8,128]{1,0:T(8,128)S(1)}, f32[8,128]{1,0:T(8,128)S(1)}, u32[]{:S(2)}, u32[]{:S(2)}) collective-permute-start(f32[8,128]{1,0:T(8,128)S(1)} %get-tuple-element.135.refs_0_), channel_id=1, source_target_pairs={{0,2},{2,0},{4,6},{6,4},{8,10},{10,8},{12,14},{14,12},{16,18},{18,... | collective-permute-start | bytes 12296 | tf_op jit(solution)/shard_map/ppermute | solution.py:101

commit v7 on v6

--- a/solution.py
+++ b/solution.py
@@ -87,18 +87,18 @@
 def last_sums(value, given, step_of):
     count, slabs = lax.axis_size("ray"), lax.axis_size("vox")
     if slabs != 2 or count & (count - 1) or count < 16:
-        mine = step_of(given)
-        return lax.psum(value, "ray"), mine, vox_others(mine)
+        mine, rest = step_of(given)
+        return (lax.psum(value, "ray"), mine, vox_others(mine)), rest
     for step in hops(count)[:-2]:
         value = value + lax.ppermute(value, "ray", pairs_of(count, step))
         if step == count // 4 | 1:
             given = step_of(given)
         value, given = lax.optimization_barrier((value, given))
-    mine = given
+    mine, rest = given
     both = jnp.concatenate([value, mine], axis=0)
     both = lax.ppermute(both, ("ray", "vox"), [(i, i ^ 7) for i in range(2 * count)])
     value = value + both[:8]
-    return value, lax.ppermute(value, "ray", pairs_of(count, 1)), mine, both[8:]
+    return (value, lax.ppermute(value, "ray", pairs_of(count, 1)), mine, both[8:]), rest
 
 
 def halo_of(low_edge, high_edge):
@@ -490,7 +490,7 @@
 
 
 def last_smooth_body(halves, next_ref, low_ref, high_ref, damp_ref, smooth_ref, norm_ref, left_ref, rest_ref,
-                     square_ref, near_ref):
+                     left0_ref, norm0_ref, square_ref, weights_ref, near_ref):
     sub, lane = sub_iota(), lane_iota()
     has_low, has_high = flags()
     if halves:
@@ -513,28 +513,28 @@
 
     square = lax.fori_loop(0, PAIRS, left, jnp.zeros((LON_DEV, LAT), F32), unroll=UNROLL)
     square_ref[...] = jnp.broadcast_to(total(square), (8, LAT))
-
-
-def end_body(share, parts, *refs):
-    sums = refs[0][...]
-    for ref in refs[1:parts]:
-        sums = sums + ref[...]
-    (left0_ref, norm0_ref, left1_ref, rest_ref, norm1_ref, rays_ref, field_ref, next_ref,
-     density_ref, out_ref) = refs[parts:]
-    left2_sq = sums
-    out_ref[...] = rays_ref[...] * lax.rsqrt(left2_sq)
-    left0_sq, norm0, left1_sq, right1 = left0_ref[...], norm0_ref[...], left1_ref[...], norm1_ref[...]
+    left0_sq, norm0, left1_sq = left0_ref[...], norm0_ref[...], left_ref[...]
     left0, left1 = jnp.sqrt(left0_sq), jnp.sqrt(left1_sq)
     right0 = norm0 / left0
     diag1 = jnp.sqrt(right0 * right0 + left1_sq)
     cosine, sine = right0 / diag1, left1 / diag1
-    coupling = sine * right1
-    diag_bar = -cosine * right1
+    coupling = sine * norm
+    diag_bar = -cosine * norm
     step1, resid = cosine * left0, sine * left0
-    diag2 = jnp.sqrt(diag_bar * diag_bar + left2_sq)
-    step2 = diag_bar / diag2 * resid
-    on_next = step2 / diag2 / (left1 * right1)
-    on_first = (step1 / diag1 - step2 / diag2 * coupling / diag1 - on_next * rest_ref[...]) / norm0
+    weights_ref[0] = diag_bar * resid / (left1 * norm)
+    weights_ref[1] = diag_bar * diag_bar
+    weights_ref[2] = step1 / diag1 / norm0
+    weights_ref[3] = (left1 * norm * coupling / diag1 + rest_ref[...]) / norm0
+
+
+def end_body(share, parts, *refs):
+    left2_sq = refs[0][...]
+    for ref in refs[1:parts]:
+        left2_sq = left2_sq + ref[...]
+    weights_ref, rays_ref, field_ref, next_ref, density_ref, out_ref = refs[parts:]
+    out_ref[...] = rays_ref[...] * lax.rsqrt(left2_sq)
+    on_next = weights_ref[0] / (weights_ref[1] + left2_sq)
+    on_first = weights_ref[2] - weights_ref[3] * on_next
     first = lax.axis_index("ray") * share + PAD
     for j in range(share):
         density_ref[j] = on_first * field_ref[first + j] + on_next * next_ref[first + j]
@@ -627,16 +627,17 @@
 
     def last_step(beside):
         return local_call(
-            functools.partial(last_smooth_body, halves), "last_smooth", [VM] * 8, [row], [pltpu.VMEM((2, PAIRS, LAT), F32)],
-        )(following, *beside, damp, smooth, norm1, left1, rest)[0]
-
-    shares = last_sums(ray_square, beside, last_step)
+            functools.partial(last_smooth_body, halves), "last_smooth", [VM] * 10, [row, ((4, 8, LAT), F32)],
+            [pltpu.VMEM((2, PAIRS, LAT), F32)],
+        )(following, *beside, damp, smooth, norm1, left1, rest, left0, norm0)
+
+    shares, weights = last_sums(ray_square, beside, last_step)
 
     share = PAIRS // rays_n
     density, rays_out = local_call(
-        functools.partial(end_body, share, len(shares)), "end", [VM] * (len(shares) + 8),
+        functools.partial(end_body, share, len(shares)), "end", [VM] * (len(shares) + 4),
         [((share, LON_DEV, LAT), F32), (held, F32)],
-    )(*shares, left0, norm0, left1, rest, norm1, last_rays, field, following)
+    )(*shares, weights, last_rays, field, following)
     return (density.reshape(ALT // rays_n, EPOCHS, LON_DEV, LAT), rays_out.reshape(-1))
 
 

time: 54.8 us -> 54.7 us (level)
  no operation moved by 1% of the time
where the time goes in v7:
time: 54.7 us; the launch traced here: 54.6 us
  starting transfers between devices  25.3 us (46%)
  waiting for transfers between devices  19.6 us (36%)
  Pallas kernels  7.88 us (14%)
  between operations  1.45 us (3%)
    ppermute x8, starting transfers between devices, gather_rays(): other = lax.ppermute(packet, 'ray', pairs_of(count, step))  12.8 us
    ppermute x8, waiting for transfers between devices, gather_rays(): other = lax.ppermute(packet, 'ray', pairs_of(count, step))  10.1 us
    ppermute x2, starting transfers between devices, last_sums(): value = value + lax.ppermute(value, 'ray', pairs_of(count, step))  4.39 us
    ppermute x1, waiting for transfers between devices, next_halo(): other = lax.ppermute(sums, 'vox', [(0, 1), (1, 0)])  2.48 us
    ppermute x1, waiting for transfers between devices, first_halo(): other = lax.ppermute(sums, 'vox', [(0, 1), (1, 0)])  2.37 us
    ppermute x1, starting transfers between devices, last_sums(): lax.ppermute(both, ('ray', 'vox'), [(i, i ^ 7) for i in range(2 * count)])  2.3 us
    ppermute x1, starting transfers between devices, first_halo(): other = lax.ppermute(sums, 'vox', [(0, 1), (1, 0)])  2.28 us
    ppermute x2, waiting for transfers between devices, last_sums(): value = value + lax.ppermute(value, 'ray', pairs_of(count, step))  2.1 us
  transfers between devices with their start and end apart: 16, of which 14 were waited for; matrix products, arithmetic and copies ran while one was open for 0% of the time, Pallas kernels for 8%

profile of v7, /device:TPU:0, one launch (start us, length us, event | category | flops | bytes accessed | tf_op | source)
XLA Modules:
  0.0 54.6 jit_solution(13576817861538811228)
XLA Ops:
  1.3 1.6 %start.1 = (f32[40,128]{1,0:T(8,128)S(1)}, f32[8,128]{1,0:T(8,128)S(1)}, f32[8,128]{1,0:T(8,128)S(1)}, f32[32,8,128]{2,1,0:T(8,128)S(1)}, s32[32,128]{1,0:T(8,128)S(1)}, /*index=5*/bf16[32,128,128]{2,1,0:T(8,128)(2,1)S(1)}) custom-call(s32[1,1]{1,0:T(1,128)S(6)} %copy.11.count_ref, s32[32]{0:T(128)} %bitcast.13, s32[32]{0:T(128)} %bitcast.8, f32[32]{0:T(128)} %bitcast.14, ...), custom_call_target="tpu_custom_call" | custom-call | tf_op jit(solution)/shard_map/start/pallas_call | solution.py:569
  2.9 0.0 copy-start.1
  2.9 3.5 %collective-permute-start = (f32[40,128]{1,0:T(8,128)S(1)}, f32[40,128]{1,0:T(8,128)S(1)}, u32[]{:S(2)}, u32[]{:S(2)}) collective-permute-start(f32[40,128]{1,0:T(8,128)S(1)} %get-tuple-element.71), channel_id=1, source_target_pairs={{0,18},{2,16},{4,22},{6,20},{8,26},{10,24},{12,30},{14,28},{16,2},... | collective-permute-start | bytes 61448 | tf_op jit(solution)/shard_map/ppermute | solution.py:63
  6.4 0.1 broadcast_in_dim.10
  6.5 0.1 broadcast_in_dim.11
  6.6 1.3 %collective-permute-done = f32[40,128]{1,0:T(8,128)S(1)} collective-permute-done((f32[40,128]{1,0:T(8,128)S(1)}, f32[40,128]{1,0:T(8,128)S(1)}, u32[]{:S(2)}, u32[]{:S(2)}) %collective-permute-start) | collective-permute-done | bytes 20512 | tf_op jit(solution)/shard_map/ppermute | solution.py:63
  8.0 0.1 broadcast_in_dim.12.damp_ref
  8.0 1.9 %collective-permute-start.1 = (f32[72,128]{1,0:T(8,128)S(1)}, f32[72,128]{1,0:T(8,128)S(1)}, u32[]{:S(2)}, u32[]{:S(2)}) collective-permute-start(f32[72,128]{1,0:T(8,128)S(1)} %pad_maximum_fusion.4), channel_id=1, source_target_pairs={{0,10},{2,8},{4,14},{6,12},{8,2},{10,0},{12,6},{14,4},{16,26},{18,... | collective-permute-start | bytes 110600 | tf_op jit(solution)/shard_map/ppermute | solution.py:63
  9.9 0.3 turn.1.turned_ref
  10.3 1.3 %collective-permute-done.1 = f32[72,128]{1,0:T(8,128)S(1)} collective-permute-done((f32[72,128]{1,0:T(8,128)S(1)}, f32[72,128]{1,0:T(8,128)S(1)}, u32[]{:S(2)}, u32[]{:S(2)}) %collective-permute-start.1) | collective-permute-done | bytes 36896 | tf_op jit(solution)/shard_map/ppermute | solution.py:63
  11.6 1.8 %collective-permute-start.2 = (f32[136,128]{1,0:T(8,128)S(1)}, f32[136,128]{1,0:T(8,128)S(1)}, u32[]{:S(2)}, u32[]{:S(2)}) collective-permute-start(f32[136,128]{1,0:T(8,128)S(1)} %pad_maximum_fusion.2), channel_id=1, source_target_pairs={{0,6},{2,4},{4,2},{6,0},{8,14},{10,12},{12,10},{14,8},{16,22},{18,... | collective-permute-start | bytes 208904 | tf_op jit(solution)/shard_map/ppermute | solution.py:63
  13.4 2.3 %collective-permute-done.2 = f32[136,128]{1,0:T(8,128)S(1)} collective-permute-done((f32[136,128]{1,0:T(8,128)S(1)}, f32[136,128]{1,0:T(8,128)S(1)}, u32[]{:S(2)}, u32[]{:S(2)}) %collective-permute-start.2) | collective-permute-done | bytes 69664 | tf_op jit(solution)/shard_map/ppermute | solution.py:63
  15.7 0.3 collective-permute-start.3
  16.1 0.3 first_half.1
  16.4 0.8 %collective-permute-done.3.other_ref = f32[264,128]{1,0:T(8,128)S(1)} collective-permute-done((f32[264,128]{1,0:T(8,128)S(1)}, f32[264,128]{1,0:T(8,128)S(1)}, u32[]{:S(2)}, u32[]{:S(2)}) %collective-permute-start.3) | collective-permute-done | bytes 135200 | tf_op jit(solution)/shard_map/ppermute | solution.py:63
  17.1 0.6 %first.1 = (f32[132,8,128]{2,1,0:T(8,128)S(1)}, f32[32,128]{1,0:T(8,128)S(1)}, f32[144,128]{1,0:T(8,128)S(1)}, f32[8,128]{1,0:T(8,128)S(1)}, s32[2,128]{1,0:T(2,128)S(1)}) custom-call(f32[264,128]{1,0:T(8,128)S(1)} %collective-permute-done.3.other_ref, f32[128,8,128]{2,1,0:T(8,128)S(1)} %get-tuple-element.77.half_ref, ...), custom_call_target="tpu_custom_call" | custom-call | tf_op jit(solution)/shard_map/first/pallas_call | solution.py:587
  17.7 2.3 %collective-permute-start.4 = (f32[144,128]{1,0:T(8,128)S(1)}, f32[144,128]{1,0:T(8,128)S(1)}, u32[]{:S(2)}, u32[]{:S(2)}) collective-permute-start(f32[144,128]{1,0:T(8,128)S(1)} %get-tuple-element.81.mine_ref), channel_id=1, source_target_pairs={{0,1},{1,0},{2,3},{3,2},{4,5},{5,4},{6,7},{7,6},{8,9},{9,8},{10,11... | collective-permute-start | bytes 221192 | tf_op jit(solution)/shard_map/ppermute | solution.py:115
  20.0 0.2 onehot.1
  20.2 2.4 %collective-permute-done.4.other_ref = f32[144,128]{1,0:T(8,128)S(1)} collective-permute-done((f32[144,128]{1,0:T(8,128)S(1)}, f32[144,128]{1,0:T(8,128)S(1)}, u32[]{:S(2)}, u32[]{:S(2)}) %collective-permute-start.4) | collective-permute-done | bytes 73760 | tf_op jit(solution)/shard_map/ppermute | solution.py:115
  22.6 0.3 second.1
  22.8 1.6 %collective-permute-start.5 = (f32[40,128]{1,0:T(8,128)S(1)}, f32[40,128]{1,0:T(8,128)S(1)}, u32[]{:S(2)}, u32[]{:S(2)}) collective-permute-start(f32[40,128]{1,0:T(8,128)S(1)} %get-tuple-element.90), channel_id=1, source_target_pairs={{0,18},{2,16},{4,22},{6,20},{8,26},{10,24},{12,30},{14,28},{16,2},... | collective-permute-start | bytes 61448 | tf_op jit(solution)/shard_map/ppermute | solution.py:63
  24.4 1.5 %collective-permute-start.6 = (f32[128,128]{1,0:T(8,128)S(1)}, f32[128,128]{1,0:T(8,128)S(1)}, u32[]{:S(2)}, u32[]{:S(2)}) collective-permute-start(f32[128,128]{1,0:T(8,128)S(1)} %slice.120.low_ref.high_ref), channel_id=1, source_target_pairs={{0,2},{2,0},{4,6},{6,4},{8,10},{10,8},{12,14},{14,12},{16,18},{18,... | collective-permute-start | bytes 196616 | tf_op jit(solution)/shard_map/ppermute | solution.py:117
  26.0 1.0 %collective-permute-done.5 = f32[40,128]{1,0:T(8,128)S(1)} collective-permute-done((f32[40,128]{1,0:T(8,128)S(1)}, f32[40,128]{1,0:T(8,128)S(1)}, u32[]{:S(2)}, u32[]{:S(2)}) %collective-permute-start.5) | collective-permute-done | bytes 20512 | tf_op jit(solution)/shard_map/ppermute | solution.py:63
  27.0 2.1 %collective-permute-start.7 = (f32[72,128]{1,0:T(8,128)S(1)}, f32[72,128]{1,0:T(8,128)S(1)}, u32[]{:S(2)}, u32[]{:S(2)}) collective-permute-start(f32[72,128]{1,0:T(8,128)S(1)} %pad_maximum_fusion.5), channel_id=1, source_target_pairs={{0,10},{2,8},{4,14},{6,12},{8,2},{10,0},{12,6},{14,4},{16,26},{18,... | collective-permute-start | bytes 110600 | tf_op jit(solution)/shard_map/ppermute | solution.py:63
  29.1 0.9 %smooth.1 = (f32[128,8,128]{2,1,0:T(8,128)S(1)}, f32[132,8,128]{2,1,0:T(8,128)S(1)}, f32[2,128,128]{2,1,0:T(8,128)S(1)}, f32[8,128]{1,0:T(8,128)S(1)}) custom-call(f32[132,8,128]{2,1,0:T(8,128)S(1)} %get-tuple-element.92.field_ref.refs_6_, f32[128,128]{1,0:T(8,128)S(1)} %slice.120.low_ref.high_ref, f32[128,128]{1,0:T(8,128)S(1)} %collective-permute-done.6.low2_ref.high2_ref, ...), custom_call_target="tpu_custom_call" | custom-call | tf_op jit(solution)/shard_map/smooth/pallas_call | solution.py:601
  30.0 0.9 %collective-permute-done.7 = f32[72,128]{1,0:T(8,128)S(1)} collective-permute-done((f32[72,128]{1,0:T(8,128)S(1)}, f32[72,128]{1,0:T(8,128)S(1)}, u32[]{:S(2)}, u32[]{:S(2)}) %collective-permute-start.7) | collective-permute-done | bytes 36896 | tf_op jit(solution)/shard_map/ppermute | solution.py:63
  30.9 0.0 copy-start
  30.9 1.3 %collective-permute-start.8 = (f32[136,128]{1,0:T(8,128)S(1)}, f32[136,128]{1,0:T(8,128)S(1)}, u32[]{:S(2)}, u32[]{:S(2)}) collective-permute-start(f32[136,128]{1,0:T(8,128)S(1)} %pad_maximum_fusion.3), channel_id=1, source_target_pairs={{0,6},{2,4},{4,2},{6,0},{8,14},{10,12},{12,10},{14,8},{16,22},{18,... | collective-permute-start | bytes 208904 | tf_op jit(solution)/shard_map/ppermute | solution.py:63
  32.2 1.3 %again.1 = (f32[128,8,128]{2,1,0:T(8,128)S(1)}, f32[32,128]{1,0:T(8,128)S(1)}) custom-call(s32[32]{0:T(128)S(1)} %bitcast.9, f32[132,8,128]{2,1,0:T(8,128)S(1)} %get-tuple-element.106.scaled_ref, f32[2,128,128]{2,1,0:T(8,128)S(1)} %get-tuple-element.107.far_ref), custom_call_target="tpu_custom_call" | custom-call | tf_op jit(solution)/shard_map/again/pallas_call | solution.py:608
  33.5 1.7 %collective-permute-done.8 = f32[136,128]{1,0:T(8,128)S(1)} collective-permute-done((f32[136,128]{1,0:T(8,128)S(1)}, f32[136,128]{1,0:T(8,128)S(1)}, u32[]{:S(2)}, u32[]{:S(2)}) %collective-permute-start.8) | collective-permute-done | bytes 69664 | tf_op jit(solution)/shard_map/ppermute | solution.py:63
  35.2 0.2 collective-permute-start.9
  35.4 0.3 third_half.1
  35.7 0.9 %collective-permute-done.9.other_ref = f32[264,128]{1,0:T(8,128)S(1)} collective-permute-done((f32[264,128]{1,0:T(8,128)S(1)}, f32[264,128]{1,0:T(8,128)S(1)}, u32[]{:S(2)}, u32[]{:S(2)}) %collective-permute-start.9) | collective-permute-done | bytes 135200 | tf_op jit(solution)/shard_map/ppermute | solution.py:63
  36.6 0.6 %third.1 = (f32[132,8,128]{2,1,0:T(8,128)S(1)}, f32[80,128]{1,0:T(8,128)S(1)}, f32[8,128]{1,0:T(8,128)S(1)}) custom-call(f32[264,128]{1,0:T(8,128)S(1)} %collective-permute-done.9.other_ref, f32[128,8,128]{2,1,0:T(8,128)S(1)} %get-tuple-element.114.half_ref, f32[32,128]{1,0:T(8,128)S(1)} %get-tuple-element.115.half_lines_ref, ...), custom_call_target="tpu_custom_call" | custom-call | tf_op jit(solution)/shard_map/third/pallas_call | solution.py:619
  37.2 1.6 %collective-permute-start.10 = (f32[80,128]{1,0:T(8,128)S(1)}, f32[80,128]{1,0:T(8,128)S(1)}, u32[]{:S(2)}, u32[]{:S(2)}) collective-permute-start(f32[80,128]{1,0:T(8,128)S(1)} %get-tuple-element.119.mine_ref), channel_id=1, source_target_pairs={{0,1},{1,0},{2,3},{3,2},{4,5},{5,4},{6,7},{7,6},{8,9},{9,8},{10,11... | collective-permute-start | bytes 122888 | tf_op jit(solution)/shard_map/ppermute | solution.py:126
  38.8 2.5 %collective-permute-done.10.other_ref = f32[80,128]{1,0:T(8,128)S(1)} collective-permute-done((f32[80,128]{1,0:T(8,128)S(1)}, f32[80,128]{1,0:T(8,128)S(1)}, u32[]{:S(2)}, u32[]{:S(2)}) %collective-permute-start.10) | collective-permute-done | bytes 40992 | tf_op jit(solution)/shard_map/ppermute | solution.py:126
  41.3 0.0 collective-permute-start.12
  41.3 0.1 fourth.1
  41.4 2.4 %collective-permute-start.11 = (f32[8,128]{1,0:T(8,128)S(1)}, f32[8,128]{1,0:T(8,128)S(1)}, u32[]{:S(2)}, u32[]{:S(2)}) collective-permute-start(f32[8,128]{1,0:T(8,128)S(1)} %get-tuple-element.123), channel_id=1, source_target_pairs={{0,18},{2,16},{4,22},{6,20},{8,26},{10,24},{12,30},{14,28},{16,2},... | collective-permute-start | bytes 12296 | tf_op jit(solution)/shard_map/ppermute | solution.py:93
  43.9 1.6 %collective-permute-done.11 = f32[8,128]{1,0:T(8,128)S(1)} collective-permute-done((f32[8,128]{1,0:T(8,128)S(1)}, f32[8,128]{1,0:T(8,128)S(1)}, u32[]{:S(2)}, u32[]{:S(2)}) %collective-permute-start.11) | collective-permute-done | bytes 4128 | tf_op jit(solution)/shard_map/ppermute | solution.py:93
  45.4 2.0 %collective-permute-start.13 = (f32[8,128]{1,0:T(8,128)S(1)}, f32[8,128]{1,0:T(8,128)S(1)}, u32[]{:S(2)}, u32[]{:S(2)}) collective-permute-start(f32[8,128]{1,0:T(8,128)S(1)} %add.33), channel_id=1, source_target_pairs={{0,10},{2,8},{4,14},{6,12},{8,2},{10,0},{12,6},{14,4},{16,26},{18,... | collective-permute-start | bytes 12296 | tf_op jit(solution)/shard_map/ppermute | solution.py:93
  47.4 0.8 %last_smooth.1 = (f32[8,128]{1,0:T(8,128)S(1)}, f32[4,8,128]{2,1,0:T(8,128)S(1)}) custom-call(f32[132,8,128]{2,1,0:T(8,128)S(1)} %get-tuple-element.125.next_ref.refs_7_, f32[64,128]{1,0:T(8,128)S(1)} %slice.125.low_ref, f32[64,128]{1,0:T(8,128)S(1)} %collective-permute-done.12.high_ref, f32[128,128]{1,0:T(8,128)S(1)} %broadcast_in_dim.12.damp_ref, ...), custom_call_target="tpu_custom_call" | custom-call | tf_op jit(solution)/shard_map/last_smooth/pallas_call | solution.py:629
  48.2 0.5 collective-permute-done.13
  48.8 2.3 %collective-permute-start.14 = (f32[16,128]{1,0:T(8,128)S(1)}, f32[16,128]{1,0:T(8,128)S(1)}, u32[]{:S(2)}, u32[]{:S(2)}) collective-permute-start(f32[16,128]{1,0:T(8,128)S(1)} %pad_maximum_fusion.6), channel_id=1, source_target_pairs={{0,7},{1,6},{2,5},{3,4},{4,3},{5,2},{6,1},{7,0},{8,15},{9,14},{10,... | collective-permute-start | bytes 24584 | tf_op jit(solution)/shard_map/ppermute | solution.py:99
  51.0 1.7 %collective-permute-done.14 = f32[16,128]{1,0:T(8,128)S(1)} collective-permute-done((f32[16,128]{1,0:T(8,128)S(1)}, f32[16,128]{1,0:T(8,128)S(1)}, u32[]{:S(2)}, u32[]{:S(2)}) %collective-permute-start.14) | collective-permute-done | bytes 8224 | tf_op jit(solution)/shard_map/ppermute | solution.py:99
  52.8 0.4 collective-permute-start.15
  53.1 0.8 %collective-permute-done.15.refs_1_ = f32[8,128]{1,0:T(8,128)S(1)} collective-permute-done((f32[8,128]{1,0:T(8,128)S(1)}, f32[8,128]{1,0:T(8,128)S(1)}, u32[]{:S(2)}, u32[]{:S(2)}) %collective-permute-start.15) | collective-permute-done | bytes 4128 | tf_op jit(solution)/shard_map/ppermute | solution.py:101
  54.0 0.6 %end.1 = (f32[8,8,128]{2,1,0:T(8,128)}, f32[8,128]{1,0:T(8,128)}) custom-call(f32[8,128]{1,0:T(8,128)S(1)} %get-tuple-element.141.refs_0_, f32[8,128]{1,0:T(8,128)S(1)} %collective-permute-done.15.refs_1_, f32[8,128]{1,0:T(8,128)S(1)} %get-tuple-element.135.refs_2_, f32[8,128]{1,0:T(8,128)S(1)} %get-tuple-element.140.refs_3_, ...), custom_call_target="tpu_custom_call" | custom-call | tf_op jit(solution)/shard_map/end/pallas_call | solution.py:637
  (34 shorter events, 0.1 us)
Async XLA Ops:
  2.9 3.6 %copy-start.1 = (f32[64]{0:T(128)S(1)}, f32[64]{0:T(128)}, u32[]{:S(2)}) copy-start(f32[64]{0:T(128)} %param.17) | copy-start | bytes 772
  2.9 5.1 %collective-permute-start = (f32[40,128]{1,0:T(8,128)S(1)}, f32[40,128]{1,0:T(8,128)S(1)}, u32[]{:S(2)}, u32[]{:S(2)}) collective-permute-start(f32[40,128]{1,0:T(8,128)S(1)} %get-tuple-element.71), channel_id=1, source_target_pairs={{0,18},{2,16},{4,22},{6,20},{8,26},{10,24},{12,30},{14,28},{16,2},... | collective-permute-start | bytes 61448 | tf_op jit(solution)/shard_map/ppermute | solution.py:63
  8.0 3.5 %collective-permute-start.1 = (f32[72,128]{1,0:T(8,128)S(1)}, f32[72,128]{1,0:T(8,128)S(1)}, u32[]{:S(2)}, u32[]{:S(2)}) collective-permute-start(f32[72,128]{1,0:T(8,128)S(1)} %pad_maximum_fusion.4), channel_id=1, source_target_pairs={{0,10},{2,8},{4,14},{6,12},{8,2},{10,0},{12,6},{14,4},{16,26},{18,... | collective-permute-start | bytes 110600 | tf_op jit(solution)/shard_map/ppermute | solution.py:63
  11.6 4.1 %collective-permute-start.2 = (f32[136,128]{1,0:T(8,128)S(1)}, f32[136,128]{1,0:T(8,128)S(1)}, u32[]{:S(2)}, u32[]{:S(2)}) collective-permute-start(f32[136,128]{1,0:T(8,128)S(1)} %pad_maximum_fusion.2), channel_id=1, source_target_pairs={{0,6},{2,4},{4,2},{6,0},{8,14},{10,12},{12,10},{14,8},{16,22},{18,... | collective-permute-start | bytes 208904 | tf_op jit(solution)/shard_map/ppermute | solution.py:63
  15.7 1.4 %collective-permute-start.3 = (f32[264,128]{1,0:T(8,128)S(1)}, f32[264,128]{1,0:T(8,128)S(1)}, u32[]{:S(2)}, u32[]{:S(2)}) collective-permute-start(f32[264,128]{1,0:T(8,128)S(1)} %pad_maximum_fusion.mine_ref), channel_id=1, source_target_pairs={{0,2},{2,0},{4,6},{6,4},{8,10},{10,8},{12,14},{14,12},{16,18},{18,... | collective-permute-start | bytes 405512 | tf_op jit(solution)/shard_map/ppermute | solution.py:63
  17.7 4.9 %collective-permute-start.4 = (f32[144,128]{1,0:T(8,128)S(1)}, f32[144,128]{1,0:T(8,128)S(1)}, u32[]{:S(2)}, u32[]{:S(2)}) collective-permute-start(f32[144,128]{1,0:T(8,128)S(1)} %get-tuple-element.81.mine_ref), channel_id=1, source_target_pairs={{0,1},{1,0},{2,3},{3,2},{4,5},{5,4},{6,7},{7,6},{8,9},{9,8},{10,11... | collective-permute-start | bytes 221192 | tf_op jit(solution)/shard_map/ppermute | solution.py:115
  22.8 4.2 %collective-permute-start.5 = (f32[40,128]{1,0:T(8,128)S(1)}, f32[40,128]{1,0:T(8,128)S(1)}, u32[]{:S(2)}, u32[]{:S(2)}) collective-permute-start(f32[40,128]{1,0:T(8,128)S(1)} %get-tuple-element.90), channel_id=1, source_target_pairs={{0,18},{2,16},{4,22},{6,20},{8,26},{10,24},{12,30},{14,28},{16,2},... | collective-permute-start | bytes 61448 | tf_op jit(solution)/shard_map/ppermute | solution.py:63
  24.4 2.6 %collective-permute-start.6 = (f32[128,128]{1,0:T(8,128)S(1)}, f32[128,128]{1,0:T(8,128)S(1)}, u32[]{:S(2)}, u32[]{:S(2)}) collective-permute-start(f32[128,128]{1,0:T(8,128)S(1)} %slice.120.low_ref.high_ref), channel_id=1, source_target_pairs={{0,2},{2,0},{4,6},{6,4},{8,10},{10,8},{12,14},{14,12},{16,18},{18,... | collective-permute-start | bytes 196616 | tf_op jit(solution)/shard_map/ppermute | solution.py:117
  27.0 3.9 %collective-permute-start.7 = (f32[72,128]{1,0:T(8,128)S(1)}, f32[72,128]{1,0:T(8,128)S(1)}, u32[]{:S(2)}, u32[]{:S(2)}) collective-permute-start(f32[72,128]{1,0:T(8,128)S(1)} %pad_maximum_fusion.5), channel_id=1, source_target_pairs={{0,10},{2,8},{4,14},{6,12},{8,2},{10,0},{12,6},{14,4},{16,26},{18,... | collective-permute-start | bytes 110600 | tf_op jit(solution)/shard_map/ppermute | solution.py:63
  30.9 1.3 %copy-start = (s32[1,1,32]{2,1,0:T(1,128)S(1)}, s32[1,1,32]{2,1,0:T(1,128)}, u32[]{:S(2)}) copy-start(s32[1,1,32]{2,1,0:T(1,128)} %param.12) | copy-start | bytes 388
  30.9 4.2 %collective-permute-start.8 = (f32[136,128]{1,0:T(8,128)S(1)}, f32[136,128]{1,0:T(8,128)S(1)}, u32[]{:S(2)}, u32[]{:S(2)}) collective-permute-start(f32[136,128]{1,0:T(8,128)S(1)} %pad_maximum_fusion.3), channel_id=1, source_target_pairs={{0,6},{2,4},{4,2},{6,0},{8,14},{10,12},{12,10},{14,8},{16,22},{18,... | collective-permute-start | bytes 208904 | tf_op jit(solution)/shard_map/ppermute | solution.py:63
  35.2 1.4 %collective-permute-start.9 = (f32[264,128]{1,0:T(8,128)S(1)}, f32[264,128]{1,0:T(8,128)S(1)}, u32[]{:S(2)}, u32[]{:S(2)}) collective-permute-start(f32[264,128]{1,0:T(8,128)S(1)} %pad_maximum_fusion.1.mine_ref), channel_id=1, source_target_pairs={{0,2},{2,0},{4,6},{6,4},{8,10},{10,8},{12,14},{14,12},{16,18},{18,... | collective-permute-start | bytes 405512 | tf_op jit(solution)/shard_map/ppermute | solution.py:63
  37.2 4.1 %collective-permute-start.10 = (f32[80,128]{1,0:T(8,128)S(1)}, f32[80,128]{1,0:T(8,128)S(1)}, u32[]{:S(2)}, u32[]{:S(2)}) collective-permute-start(f32[80,128]{1,0:T(8,128)S(1)} %get-tuple-element.119.mine_ref), channel_id=1, source_target_pairs={{0,1},{1,0},{2,3},{3,2},{4,5},{5,4},{6,7},{7,6},{8,9},{9,8},{10,11... | collective-permute-start | bytes 122888 | tf_op jit(solution)/shard_map/ppermute | solution.py:126
  41.3 4.2 %collective-permute-start.12 = (f32[64,128]{1,0:T(8,128)S(1)}, f32[64,128]{1,0:T(8,128)S(1)}, u32[]{:S(2)}, u32[]{:S(2)}) collective-permute-start(f32[64,128]{1,0:T(8,128)S(1)} %slice.125.low_ref), channel_id=1, source_target_pairs={{0,2},{2,0},{4,6},{6,4},{8,10},{10,8},{12,14},{14,12},{16,18},{18,... | collective-permute-start | bytes 98312 | tf_op jit(solution)/shard_map/ppermute | solution.py:128
  41.4 4.0 %collective-permute-start.11 = (f32[8,128]{1,0:T(8,128)S(1)}, f32[8,128]{1,0:T(8,128)S(1)}, u32[]{:S(2)}, u32[]{:S(2)}) collective-permute-start(f32[8,128]{1,0:T(8,128)S(1)} %get-tuple-element.123), channel_id=1, source_target_pairs={{0,18},{2,16},{4,22},{6,20},{8,26},{10,24},{12,30},{14,28},{16,2},... | collective-permute-start | bytes 12296 | tf_op jit(solution)/shard_map/ppermute | solution.py:93
  45.4 3.3 %collective-permute-start.13 = (f32[8,128]{1,0:T(8,128)S(1)}, f32[8,128]{1,0:T(8,128)S(1)}, u32[]{:S(2)}, u32[]{:S(2)}) collective-permute-start(f32[8,128]{1,0:T(8,128)S(1)} %add.33), channel_id=1, source_target_pairs={{0,10},{2,8},{4,14},{6,12},{8,2},{10,0},{12,6},{14,4},{16,26},{18,... | collective-permute-start | bytes 12296 | tf_op jit(solution)/shard_map/ppermute | solution.py:93
  48.8 4.0 %collective-permute-start.14 = (f32[16,128]{1,0:T(8,128)S(1)}, f32[16,128]{1,0:T(8,128)S(1)}, u32[]{:S(2)}, u32[]{:S(2)}) collective-permute-start(f32[16,128]{1,0:T(8,128)S(1)} %pad_maximum_fusion.6), channel_id=1, source_target_pairs={{0,7},{1,6},{2,5},{3,4},{4,3},{5,2},{6,1},{7,0},{8,15},{9,14},{10,... | collective-permute-start | bytes 24584 | tf_op jit(solution)/shard_map/ppermute | solution.py:99
  52.8 1.2 %collective-permute-start.15 = (f32[8,128]{1,0:T(8,128)S(1)}, f32[8,128]{1,0:T(8,128)S(1)}, u32[]{:S(2)}, u32[]{:S(2)}) collective-permute-start(f32[8,128]{1,0:T(8,128)S(1)} %get-tuple-element.141.refs_0_), channel_id=1, source_target_pairs={{0,2},{2,0},{4,6},{6,4},{8,10},{10,8},{12,14},{14,12},{16,18},{18,... | collective-permute-start | bytes 12296 | tf_op jit(solution)/shard_map/ppermute | solution.py:101

commit v8 on v7

--- a/solution.py
+++ b/solution.py
@@ -610,7 +610,7 @@
         )(col_index, scaled, beside)
         return smooth, square, again, again_lines
 
-    near, far, given = gather_rays(mine, 8, (lambda _: columns, smooth_step, again_step))
+    near, far, given = gather_rays(mine, 8, (lambda _: (), lambda _: columns, lambda given: again_step(smooth_step(given))))
     smooth, square, again, again_lines = given
 
     half, half_lines = local_call(

time: 54.7 us -> 54.7 us (level)
  starting transfers between devices: 25.3 us -> 24.1 us
  local copies, waits for them, and re-layouts: 0.35 us -> 1 us
    ppermute x1, starting transfers between devices: 1.55 us -> 0.01 us  [first_halo(): partner = lax.ppermute(column, 'ray', pairs_of(lax.axis_size('ray'), 1))]
    ppermute x8, waiting for transfers between devices: 10.1 us -> 10.8 us  [gather_rays(): other = lax.ppermute(packet, 'ray', pairs_of(count, step))]
    unnamed x4, local copies, waits for them, and re-layouts: 0.01 us -> 0.66 us
where the time goes in v8:
time: 54.7 us; the launch traced here: 54.6 us
  starting transfers between devices  24.1 us (44%)
  waiting for transfers between devices  20 us (37%)
  Pallas kernels  7.88 us (14%)
  between operations  1.45 us (3%)
  local copies, waits for them, and re-layouts  1 us (2%)
    ppermute x8, starting transfers between devices, gather_rays(): other = lax.ppermute(packet, 'ray', pairs_of(count, step))  13 us
    ppermute x8, waiting for transfers between devices, gather_rays(): other = lax.ppermute(packet, 'ray', pairs_of(count, step))  10.8 us
    ppermute x2, starting transfers between devices, last_sums(): value = value + lax.ppermute(value, 'ray', pairs_of(count, step))  4.64 us
    ppermute x1, waiting for transfers between devices, next_halo(): other = lax.ppermute(sums, 'vox', [(0, 1), (1, 0)])  2.48 us
    ppermute x1, waiting for transfers between devices, first_halo(): other = lax.ppermute(sums, 'vox', [(0, 1), (1, 0)])  2.37 us
    ppermute x1, starting transfers between devices, last_sums(): lax.ppermute(both, ('ray', 'vox'), [(i, i ^ 7) for i in range(2 * count)])  2.3 us
    ppermute x1, starting transfers between devices, first_halo(): other = lax.ppermute(sums, 'vox', [(0, 1), (1, 0)])  2.28 us
    ppermute x2, waiting for transfers between devices, last_sums(): value = value + lax.ppermute(value, 'ray', pairs_of(count, step))  1.85 us
  transfers between devices with their start and end apart: 16, of which 14 were waited for; matrix products, arithmetic and copies ran while one was open for 0% of the time, Pallas kernels for 8%

profile of v8, /device:TPU:0, one launch (start us, length us, event | category | flops | bytes accessed | tf_op | source)
XLA Modules:
  0.0 54.6 jit_solution(3158496112337079744)
XLA Ops:
  1.3 1.6 %start.1 = (f32[40,128]{1,0:T(8,128)S(1)}, f32[8,128]{1,0:T(8,128)S(1)}, f32[8,128]{1,0:T(8,128)S(1)}, f32[32,8,128]{2,1,0:T(8,128)S(1)}, s32[32,128]{1,0:T(8,128)S(1)}, /*index=5*/bf16[32,128,128]{2,1,0:T(8,128)(2,1)S(1)}) custom-call(s32[1,1]{1,0:T(1,128)S(6)} %copy.11.count_ref, s32[32]{0:T(128)} %bitcast.13, s32[32]{0:T(128)} %bitcast.8, f32[32]{0:T(128)} %bitcast.14, ...), custom_call_target="tpu_custom_call" | custom-call | tf_op jit(solution)/shard_map/start/pallas_call | solution.py:569
  2.9 0.0 copy-start.1
  2.9 3.5 %collective-permute-start = (f32[40,128]{1,0:T(8,128)S(1)}, f32[40,128]{1,0:T(8,128)S(1)}, u32[]{:S(2)}, u32[]{:S(2)}) collective-permute-start(f32[40,128]{1,0:T(8,128)S(1)} %get-tuple-element.66), channel_id=1, source_target_pairs={{0,18},{2,16},{4,22},{6,20},{8,26},{10,24},{12,30},{14,28},{16,2},... | collective-permute-start | bytes 61448 | tf_op jit(solution)/shard_map/ppermute | solution.py:63
  6.4 0.1 broadcast_in_dim.10
  6.5 0.1 broadcast_in_dim.11
  6.6 1.3 %collective-permute-done = f32[40,128]{1,0:T(8,128)S(1)} collective-permute-done((f32[40,128]{1,0:T(8,128)S(1)}, f32[40,128]{1,0:T(8,128)S(1)}, u32[]{:S(2)}, u32[]{:S(2)}) %collective-permute-start) | collective-permute-done | bytes 20512 | tf_op jit(solution)/shard_map/ppermute | solution.py:63
  8.0 0.1 broadcast_in_dim.12.damp_ref
  8.0 1.9 %collective-permute-start.1 = (f32[72,128]{1,0:T(8,128)S(1)}, f32[72,128]{1,0:T(8,128)S(1)}, u32[]{:S(2)}, u32[]{:S(2)}) collective-permute-start(f32[72,128]{1,0:T(8,128)S(1)} %pad_maximum_fusion.4), channel_id=1, source_target_pairs={{0,10},{2,8},{4,14},{6,12},{8,2},{10,0},{12,6},{14,4},{16,26},{18,... | collective-permute-start | bytes 110600 | tf_op jit(solution)/shard_map/ppermute | solution.py:63
  9.9 0.3 turn.1.turned_ref
  10.3 1.3 %collective-permute-done.1 = f32[72,128]{1,0:T(8,128)S(1)} collective-permute-done((f32[72,128]{1,0:T(8,128)S(1)}, f32[72,128]{1,0:T(8,128)S(1)}, u32[]{:S(2)}, u32[]{:S(2)}) %collective-permute-start.1) | collective-permute-done | bytes 36896 | tf_op jit(solution)/shard_map/ppermute | solution.py:63
  11.6 1.8 %collective-permute-start.2 = (f32[136,128]{1,0:T(8,128)S(1)}, f32[136,128]{1,0:T(8,128)S(1)}, u32[]{:S(2)}, u32[]{:S(2)}) collective-permute-start(f32[136,128]{1,0:T(8,128)S(1)} %pad_maximum_fusion.2), channel_id=1, source_target_pairs={{0,6},{2,4},{4,2},{6,0},{8,14},{10,12},{12,10},{14,8},{16,22},{18,... | collective-permute-start | bytes 208904 | tf_op jit(solution)/shard_map/ppermute | solution.py:63
  13.4 2.3 %collective-permute-done.2 = f32[136,128]{1,0:T(8,128)S(1)} collective-permute-done((f32[136,128]{1,0:T(8,128)S(1)}, f32[136,128]{1,0:T(8,128)S(1)}, u32[]{:S(2)}, u32[]{:S(2)}) %collective-permute-start.2) | collective-permute-done | bytes 69664 | tf_op jit(solution)/shard_map/ppermute | solution.py:63
  15.7 0.3 collective-permute-start.3
  16.1 0.3 first_half.1
  16.4 0.8 %collective-permute-done.3.other_ref = f32[264,128]{1,0:T(8,128)S(1)} collective-permute-done((f32[264,128]{1,0:T(8,128)S(1)}, f32[264,128]{1,0:T(8,128)S(1)}, u32[]{:S(2)}, u32[]{:S(2)}) %collective-permute-start.3) | collective-permute-done | bytes 135200 | tf_op jit(solution)/shard_map/ppermute | solution.py:63
  17.1 0.6 %first.1 = (f32[132,8,128]{2,1,0:T(8,128)S(1)}, f32[32,128]{1,0:T(8,128)S(1)}, f32[144,128]{1,0:T(8,128)S(1)}, f32[8,128]{1,0:T(8,128)S(1)}, s32[2,128]{1,0:T(2,128)S(1)}) custom-call(f32[264,128]{1,0:T(8,128)S(1)} %collective-permute-done.3.other_ref, f32[128,8,128]{2,1,0:T(8,128)S(1)} %get-tuple-element.72.half_ref, ...), custom_call_target="tpu_custom_call" | custom-call | tf_op jit(solution)/shard_map/first/pallas_call | solution.py:587
  17.7 2.3 %collective-permute-start.4 = (f32[144,128]{1,0:T(8,128)S(1)}, f32[144,128]{1,0:T(8,128)S(1)}, u32[]{:S(2)}, u32[]{:S(2)}) collective-permute-start(f32[144,128]{1,0:T(8,128)S(1)} %get-tuple-element.76.mine_ref), channel_id=1, source_target_pairs={{0,1},{1,0},{2,3},{3,2},{4,5},{5,4},{6,7},{7,6},{8,9},{9,8},{10,11... | collective-permute-start | bytes 221192 | tf_op jit(solution)/shard_map/ppermute | solution.py:115
  20.0 0.2 onehot.1
  20.2 2.4 %collective-permute-done.4.other_ref = f32[144,128]{1,0:T(8,128)S(1)} collective-permute-done((f32[144,128]{1,0:T(8,128)S(1)}, f32[144,128]{1,0:T(8,128)S(1)}, u32[]{:S(2)}, u32[]{:S(2)}) %collective-permute-start.4) | collective-permute-done | bytes 73760 | tf_op jit(solution)/shard_map/ppermute | solution.py:115
  22.6 0.3 second.1
  22.8 1.6 %collective-permute-start.5 = (f32[40,128]{1,0:T(8,128)S(1)}, f32[40,128]{1,0:T(8,128)S(1)}, u32[]{:S(2)}, u32[]{:S(2)}) collective-permute-start(f32[40,128]{1,0:T(8,128)S(1)} %get-tuple-element.85), channel_id=1, source_target_pairs={{0,18},{2,16},{4,22},{6,20},{8,26},{10,24},{12,30},{14,28},{16,2},... | collective-permute-start | bytes 61448 | tf_op jit(solution)/shard_map/ppermute | solution.py:63
  24.4 2.6 %collective-permute-done.5 = f32[40,128]{1,0:T(8,128)S(1)} collective-permute-done((f32[40,128]{1,0:T(8,128)S(1)}, f32[40,128]{1,0:T(8,128)S(1)}, u32[]{:S(2)}, u32[]{:S(2)}) %collective-permute-start.5) | collective-permute-done | bytes 20512 | tf_op jit(solution)/shard_map/ppermute | solution.py:63
  27.0 2.1 %collective-permute-start.6 = (f32[72,128]{1,0:T(8,128)S(1)}, f32[72,128]{1,0:T(8,128)S(1)}, u32[]{:S(2)}, u32[]{:S(2)}) collective-permute-start(f32[72,128]{1,0:T(8,128)S(1)} %pad_maximum_fusion.5), channel_id=1, source_target_pairs={{0,10},{2,8},{4,14},{6,12},{8,2},{10,0},{12,6},{14,4},{16,26},{18,... | collective-permute-start | bytes 110600 | tf_op jit(solution)/shard_map/ppermute | solution.py:63
  29.1 1.8 %collective-permute-done.6 = f32[72,128]{1,0:T(8,128)S(1)} collective-permute-done((f32[72,128]{1,0:T(8,128)S(1)}, f32[72,128]{1,0:T(8,128)S(1)}, u32[]{:S(2)}, u32[]{:S(2)}) %collective-permute-start.6) | collective-permute-done | bytes 36896 | tf_op jit(solution)/shard_map/ppermute | solution.py:63
  30.9 1.3 %collective-permute-start.8 = (f32[136,128]{1,0:T(8,128)S(1)}, f32[136,128]{1,0:T(8,128)S(1)}, u32[]{:S(2)}, u32[]{:S(2)}) collective-permute-start(f32[136,128]{1,0:T(8,128)S(1)} %pad_maximum_fusion.3), channel_id=1, source_target_pairs={{0,6},{2,4},{4,2},{6,0},{8,14},{10,12},{12,10},{14,8},{16,22},{18,... | collective-permute-start | bytes 208904 | tf_op jit(solution)/shard_map/ppermute | solution.py:63
  32.2 0.9 %smooth.1 = (f32[128,8,128]{2,1,0:T(8,128)S(1)}, f32[132,8,128]{2,1,0:T(8,128)S(1)}, f32[2,128,128]{2,1,0:T(8,128)S(1)}, f32[8,128]{1,0:T(8,128)S(1)}) custom-call(f32[132,8,128]{2,1,0:T(8,128)S(1)} %get-tuple-element.87.field_ref.refs_6_, f32[128,128]{1,0:T(8,128)S(1)} %slice.124.low_ref.high_ref, f32[128,128]{1,0:T(8,128)S(1)} %collective-permute-done.7.low2_ref.high2_ref, ...), custom_call_target="tpu_custom_call" | custom-call | tf_op jit(solution)/shard_map/smooth/pallas_call | solution.py:601
  33.1 0.0 copy-start
  33.1 0.6 %copy-done = s32[1,1,32]{2,1,0:T(1,128)S(1)} copy-done((s32[1,1,32]{2,1,0:T(1,128)S(1)}, s32[1,1,32]{2,1,0:T(1,128)}, u32[]{:S(2)}) %copy-start) | copy-done | bytes 152
  33.8 1.3 %again.1 = (f32[128,8,128]{2,1,0:T(8,128)S(1)}, f32[32,128]{1,0:T(8,128)S(1)}) custom-call(s32[32]{0:T(128)S(1)} %bitcast.9, f32[132,8,128]{2,1,0:T(8,128)S(1)} %get-tuple-element.96.scaled_ref, f32[2,128,128]{2,1,0:T(8,128)S(1)} %get-tuple-element.97.far_ref), custom_call_target="tpu_custom_call" | custom-call | tf_op jit(solution)/shard_map/again/pallas_call | solution.py:608
  35.0 0.1 collective-permute-done.8
  35.2 0.4 collective-permute-start.9
  35.6 0.3 third_half.1
  35.9 0.7 %collective-permute-done.9.other_ref = f32[264,128]{1,0:T(8,128)S(1)} collective-permute-done((f32[264,128]{1,0:T(8,128)S(1)}, f32[264,128]{1,0:T(8,128)S(1)}, u32[]{:S(2)}, u32[]{:S(2)}) %collective-permute-start.9) | collective-permute-done | bytes 135200 | tf_op jit(solution)/shard_map/ppermute | solution.py:63
  36.6 0.6 %third.1 = (f32[132,8,128]{2,1,0:T(8,128)S(1)}, f32[80,128]{1,0:T(8,128)S(1)}, f32[8,128]{1,0:T(8,128)S(1)}) custom-call(f32[264,128]{1,0:T(8,128)S(1)} %collective-permute-done.9.other_ref, f32[128,8,128]{2,1,0:T(8,128)S(1)} %get-tuple-element.104.half_ref, f32[32,128]{1,0:T(8,128)S(1)} %get-tuple-element.105.half_lines_ref, ...), custom_call_target="tpu_custom_call" | custom-call | tf_op jit(solution)/shard_map/third/pallas_call | solution.py:619
  37.2 1.6 %collective-permute-start.10 = (f32[80,128]{1,0:T(8,128)S(1)}, f32[80,128]{1,0:T(8,128)S(1)}, u32[]{:S(2)}, u32[]{:S(2)}) collective-permute-start(f32[80,128]{1,0:T(8,128)S(1)} %get-tuple-element.109.mine_ref), channel_id=1, source_target_pairs={{0,1},{1,0},{2,3},{3,2},{4,5},{5,4},{6,7},{7,6},{8,9},{9,8},{10,11... | collective-permute-start | bytes 122888 | tf_op jit(solution)/shard_map/ppermute | solution.py:126
  38.8 2.5 %collective-permute-done.10.other_ref = f32[80,128]{1,0:T(8,128)S(1)} collective-permute-done((f32[80,128]{1,0:T(8,128)S(1)}, f32[80,128]{1,0:T(8,128)S(1)}, u32[]{:S(2)}, u32[]{:S(2)}) %collective-permute-start.10) | collective-permute-done | bytes 40992 | tf_op jit(solution)/shard_map/ppermute | solution.py:126
  41.3 0.1 fourth.1
  41.4 2.9 %collective-permute-start.11 = (f32[8,128]{1,0:T(8,128)S(1)}, f32[8,128]{1,0:T(8,128)S(1)}, u32[]{:S(2)}, u32[]{:S(2)}) collective-permute-start(f32[8,128]{1,0:T(8,128)S(1)} %get-tuple-element.113), channel_id=1, source_target_pairs={{0,18},{2,16},{4,22},{6,20},{8,26},{10,24},{12,30},{14,28},{16,2},... | collective-permute-start | bytes 12296 | tf_op jit(solution)/shard_map/ppermute | solution.py:93
  44.3 1.3 %collective-permute-done.11 = f32[8,128]{1,0:T(8,128)S(1)} collective-permute-done((f32[8,128]{1,0:T(8,128)S(1)}, f32[8,128]{1,0:T(8,128)S(1)}, u32[]{:S(2)}, u32[]{:S(2)}) %collective-permute-start.11) | collective-permute-done | bytes 4128 | tf_op jit(solution)/shard_map/ppermute | solution.py:93
  45.6 0.0 collective-permute-done.12.high_ref
  45.6 1.8 %collective-permute-start.13 = (f32[8,128]{1,0:T(8,128)S(1)}, f32[8,128]{1,0:T(8,128)S(1)}, u32[]{:S(2)}, u32[]{:S(2)}) collective-permute-start(f32[8,128]{1,0:T(8,128)S(1)} %add.33), channel_id=1, source_target_pairs={{0,10},{2,8},{4,14},{6,12},{8,2},{10,0},{12,6},{14,4},{16,26},{18,... | collective-permute-start | bytes 12296 | tf_op jit(solution)/shard_map/ppermute | solution.py:93
  47.4 0.8 %last_smooth.1 = (f32[8,128]{1,0:T(8,128)S(1)}, f32[4,8,128]{2,1,0:T(8,128)S(1)}) custom-call(f32[132,8,128]{2,1,0:T(8,128)S(1)} %get-tuple-element.115.next_ref.refs_7_, f32[64,128]{1,0:T(8,128)S(1)} %slice.127.low_ref, f32[64,128]{1,0:T(8,128)S(1)} %collective-permute-done.12.high_ref, f32[128,128]{1,0:T(8,128)S(1)} %broadcast_in_dim.12.damp_ref, ...), custom_call_target="tpu_custom_call" | custom-call | tf_op jit(solution)/shard_map/last_smooth/pallas_call | solution.py:629
  48.2 0.5 collective-permute-done.13
  48.7 2.3 %collective-permute-start.14 = (f32[16,128]{1,0:T(8,128)S(1)}, f32[16,128]{1,0:T(8,128)S(1)}, u32[]{:S(2)}, u32[]{:S(2)}) collective-permute-start(f32[16,128]{1,0:T(8,128)S(1)} %pad_maximum_fusion.6), channel_id=1, source_target_pairs={{0,7},{1,6},{2,5},{3,4},{4,3},{5,2},{6,1},{7,0},{8,15},{9,14},{10,... | collective-permute-start | bytes 24584 | tf_op jit(solution)/shard_map/ppermute | solution.py:99
  51.0 1.7 %collective-permute-done.14 = f32[16,128]{1,0:T(8,128)S(1)} collective-permute-done((f32[16,128]{1,0:T(8,128)S(1)}, f32[16,128]{1,0:T(8,128)S(1)}, u32[]{:S(2)}, u32[]{:S(2)}) %collective-permute-start.14) | collective-permute-done | bytes 8224 | tf_op jit(solution)/shard_map/ppermute | solution.py:99
  52.8 0.4 collective-permute-start.15
  53.1 0.8 %collective-permute-done.15.refs_1_ = f32[8,128]{1,0:T(8,128)S(1)} collective-permute-done((f32[8,128]{1,0:T(8,128)S(1)}, f32[8,128]{1,0:T(8,128)S(1)}, u32[]{:S(2)}, u32[]{:S(2)}) %collective-permute-start.15) | collective-permute-done | bytes 4128 | tf_op jit(solution)/shard_map/ppermute | solution.py:101
  53.9 0.6 %end.1 = (f32[8,8,128]{2,1,0:T(8,128)}, f32[8,128]{1,0:T(8,128)}) custom-call(f32[8,128]{1,0:T(8,128)S(1)} %get-tuple-element.131.refs_0_, f32[8,128]{1,0:T(8,128)S(1)} %collective-permute-done.15.refs_1_, f32[8,128]{1,0:T(8,128)S(1)} %get-tuple-element.125.refs_2_, f32[8,128]{1,0:T(8,128)S(1)} %get-tuple-element.130.refs_3_, ...), custom_call_target="tpu_custom_call" | custom-call | tf_op jit(solution)/shard_map/end/pallas_call | solution.py:637
  (34 shorter events, 0.1 us)
Async XLA Ops:
  2.9 3.6 %copy-start.1 = (f32[64]{0:T(128)S(1)}, f32[64]{0:T(128)}, u32[]{:S(2)}) copy-start(f32[64]{0:T(128)} %param.17) | copy-start | bytes 772
  2.9 5.1 %collective-permute-start = (f32[40,128]{1,0:T(8,128)S(1)}, f32[40,128]{1,0:T(8,128)S(1)}, u32[]{:S(2)}, u32[]{:S(2)}) collective-permute-start(f32[40,128]{1,0:T(8,128)S(1)} %get-tuple-element.66), channel_id=1, source_target_pairs={{0,18},{2,16},{4,22},{6,20},{8,26},{10,24},{12,30},{14,28},{16,2},... | collective-permute-start | bytes 61448 | tf_op jit(solution)/shard_map/ppermute | solution.py:63
  8.0 3.5 %collective-permute-start.1 = (f32[72,128]{1,0:T(8,128)S(1)}, f32[72,128]{1,0:T(8,128)S(1)}, u32[]{:S(2)}, u32[]{:S(2)}) collective-permute-start(f32[72,128]{1,0:T(8,128)S(1)} %pad_maximum_fusion.4), channel_id=1, source_target_pairs={{0,10},{2,8},{4,14},{6,12},{8,2},{10,0},{12,6},{14,4},{16,26},{18,... | collective-permute-start | bytes 110600 | tf_op jit(solution)/shard_map/ppermute | solution.py:63
  11.6 4.1 %collective-permute-start.2 = (f32[136,128]{1,0:T(8,128)S(1)}, f32[136,128]{1,0:T(8,128)S(1)}, u32[]{:S(2)}, u32[]{:S(2)}) collective-permute-start(f32[136,128]{1,0:T(8,128)S(1)} %pad_maximum_fusion.2), channel_id=1, source_target_pairs={{0,6},{2,4},{4,2},{6,0},{8,14},{10,12},{12,10},{14,8},{16,22},{18,... | collective-permute-start | bytes 208904 | tf_op jit(solution)/shard_map/ppermute | solution.py:63
  15.7 1.4 %collective-permute-start.3 = (f32[264,128]{1,0:T(8,128)S(1)}, f32[264,128]{1,0:T(8,128)S(1)}, u32[]{:S(2)}, u32[]{:S(2)}) collective-permute-start(f32[264,128]{1,0:T(8,128)S(1)} %pad_maximum_fusion.mine_ref), channel_id=1, source_target_pairs={{0,2},{2,0},{4,6},{6,4},{8,10},{10,8},{12,14},{14,12},{16,18},{18,... | collective-permute-start | bytes 405512 | tf_op jit(solution)/shard_map/ppermute | solution.py:63
  17.7 4.9 %collective-permute-start.4 = (f32[144,128]{1,0:T(8,128)S(1)}, f32[144,128]{1,0:T(8,128)S(1)}, u32[]{:S(2)}, u32[]{:S(2)}) collective-permute-start(f32[144,128]{1,0:T(8,128)S(1)} %get-tuple-element.76.mine_ref), channel_id=1, source_target_pairs={{0,1},{1,0},{2,3},{3,2},{4,5},{5,4},{6,7},{7,6},{8,9},{9,8},{10,11... | collective-permute-start | bytes 221192 | tf_op jit(solution)/shard_map/ppermute | solution.py:115
  22.8 4.2 %collective-permute-start.5 = (f32[40,128]{1,0:T(8,128)S(1)}, f32[40,128]{1,0:T(8,128)S(1)}, u32[]{:S(2)}, u32[]{:S(2)}) collective-permute-start(f32[40,128]{1,0:T(8,128)S(1)} %get-tuple-element.85), channel_id=1, source_target_pairs={{0,18},{2,16},{4,22},{6,20},{8,26},{10,24},{12,30},{14,28},{16,2},... | collective-permute-start | bytes 61448 | tf_op jit(solution)/shard_map/ppermute | solution.py:63
  27.0 3.9 %collective-permute-start.6 = (f32[72,128]{1,0:T(8,128)S(1)}, f32[72,128]{1,0:T(8,128)S(1)}, u32[]{:S(2)}, u32[]{:S(2)}) collective-permute-start(f32[72,128]{1,0:T(8,128)S(1)} %pad_maximum_fusion.5), channel_id=1, source_target_pairs={{0,10},{2,8},{4,14},{6,12},{8,2},{10,0},{12,6},{14,4},{16,26},{18,... | collective-permute-start | bytes 110600 | tf_op jit(solution)/shard_map/ppermute | solution.py:63
  29.1 1.8 %collective-permute-start.7 = (f32[128,128]{1,0:T(8,128)S(1)}, f32[128,128]{1,0:T(8,128)S(1)}, u32[]{:S(2)}, u32[]{:S(2)}) collective-permute-start(f32[128,128]{1,0:T(8,128)S(1)} %slice.124.low_ref.high_ref), channel_id=1, source_target_pairs={{0,2},{2,0},{4,6},{6,4},{8,10},{10,8},{12,14},{14,12},{16,18},{18,... | collective-permute-start | bytes 196616 | tf_op jit(solution)/shard_map/ppermute | solution.py:117
  30.9 4.2 %collective-permute-start.8 = (f32[136,128]{1,0:T(8,128)S(1)}, f32[136,128]{1,0:T(8,128)S(1)}, u32[]{:S(2)}, u32[]{:S(2)}) collective-permute-start(f32[136,128]{1,0:T(8,128)S(1)} %pad_maximum_fusion.3), channel_id=1, source_target_pairs={{0,6},{2,4},{4,2},{6,0},{8,14},{10,12},{12,10},{14,8},{16,22},{18,... | collective-permute-start | bytes 208904 | tf_op jit(solution)/shard_map/ppermute | solution.py:63
  33.1 0.7 %copy-start = (s32[1,1,32]{2,1,0:T(1,128)S(1)}, s32[1,1,32]{2,1,0:T(1,128)}, u32[]{:S(2)}) copy-start(s32[1,1,32]{2,1,0:T(1,128)} %param.12) | copy-start | bytes 388
  35.2 1.4 %collective-permute-start.9 = (f32[264,128]{1,0:T(8,128)S(1)}, f32[264,128]{1,0:T(8,128)S(1)}, u32[]{:S(2)}, u32[]{:S(2)}) collective-permute-start(f32[264,128]{1,0:T(8,128)S(1)} %pad_maximum_fusion.1.mine_ref), channel_id=1, source_target_pairs={{0,2},{2,0},{4,6},{6,4},{8,10},{10,8},{12,14},{14,12},{16,18},{18,... | collective-permute-start | bytes 405512 | tf_op jit(solution)/shard_map/ppermute | solution.py:63
  37.2 4.1 %collective-permute-start.10 = (f32[80,128]{1,0:T(8,128)S(1)}, f32[80,128]{1,0:T(8,128)S(1)}, u32[]{:S(2)}, u32[]{:S(2)}) collective-permute-start(f32[80,128]{1,0:T(8,128)S(1)} %get-tuple-element.109.mine_ref), channel_id=1, source_target_pairs={{0,1},{1,0},{2,3},{3,2},{4,5},{5,4},{6,7},{7,6},{8,9},{9,8},{10,11... | collective-permute-start | bytes 122888 | tf_op jit(solution)/shard_map/ppermute | solution.py:126
  41.3 4.4 %collective-permute-start.12 = (f32[64,128]{1,0:T(8,128)S(1)}, f32[64,128]{1,0:T(8,128)S(1)}, u32[]{:S(2)}, u32[]{:S(2)}) collective-permute-start(f32[64,128]{1,0:T(8,128)S(1)} %slice.127.low_ref), channel_id=1, source_target_pairs={{0,2},{2,0},{4,6},{6,4},{8,10},{10,8},{12,14},{14,12},{16,18},{18,... | collective-permute-start | bytes 98312 | tf_op jit(solution)/shard_map/ppermute | solution.py:128
  41.4 4.2 %collective-permute-start.11 = (f32[8,128]{1,0:T(8,128)S(1)}, f32[8,128]{1,0:T(8,128)S(1)}, u32[]{:S(2)}, u32[]{:S(2)}) collective-permute-start(f32[8,128]{1,0:T(8,128)S(1)} %get-tuple-element.113), channel_id=1, source_target_pairs={{0,18},{2,16},{4,22},{6,20},{8,26},{10,24},{12,30},{14,28},{16,2},... | collective-permute-start | bytes 12296 | tf_op jit(solution)/shard_map/ppermute | solution.py:93
  45.6 3.1 %collective-permute-start.13 = (f32[8,128]{1,0:T(8,128)S(1)}, f32[8,128]{1,0:T(8,128)S(1)}, u32[]{:S(2)}, u32[]{:S(2)}) collective-permute-start(f32[8,128]{1,0:T(8,128)S(1)} %add.33), channel_id=1, source_target_pairs={{0,10},{2,8},{4,14},{6,12},{8,2},{10,0},{12,6},{14,4},{16,26},{18,... | collective-permute-start | bytes 12296 | tf_op jit(solution)/shard_map/ppermute | solution.py:93
  48.7 4.0 %collective-permute-start.14 = (f32[16,128]{1,0:T(8,128)S(1)}, f32[16,128]{1,0:T(8,128)S(1)}, u32[]{:S(2)}, u32[]{:S(2)}) collective-permute-start(f32[16,128]{1,0:T(8,128)S(1)} %pad_maximum_fusion.6), channel_id=1, source_target_pairs={{0,7},{1,6},{2,5},{3,4},{4,3},{5,2},{6,1},{7,0},{8,15},{9,14},{10,... | collective-permute-start | bytes 24584 | tf_op jit(solution)/shard_map/ppermute | solution.py:99
  52.8 1.2 %collective-permute-start.15 = (f32[8,128]{1,0:T(8,128)S(1)}, f32[8,128]{1,0:T(8,128)S(1)}, u32[]{:S(2)}, u32[]{:S(2)}) collective-permute-start(f32[8,128]{1,0:T(8,128)S(1)} %get-tuple-element.131.refs_0_), channel_id=1, source_target_pairs={{0,2},{2,0},{4,6},{6,4},{8,10},{10,8},{12,14},{14,12},{16,18},{18,... | collective-permute-start | bytes 12296 | tf_op jit(solution)/shard_map/ppermute | solution.py:101

commit v9 on v8

--- a/solution.py
+++ b/solution.py
@@ -412,7 +412,9 @@
             onehot_ref[first : first + CHUNK, :] = onehot_of(pieces, sub_iota((CHUNK, LAT)) + first)
 
 
-def again_body(slots, col_ref, scaled_ref, far_ref, again_ref, lines_ref):
+def again_body(slots, col_in, scaled_ref, far_ref, again_ref, lines_ref, col_ref, sem):
+    copy = pltpu.make_async_copy(col_in, col_ref, sem)
+    copy.start()
     sub, lane = sub_iota(), lane_iota()
 
     def right(pair, carry):
@@ -420,6 +422,7 @@
         return carry
 
     lax.fori_loop(0, PAIRS, right, 0, unroll=UNROLL)
+    copy.wait()
     for k in range(slots):
         col = col_ref[k]
         lines_ref[pl.ds(k, 1), :] = again_ref[col // LON_DEV, pl.ds(col % LON_DEV, 1), :]
@@ -606,8 +609,9 @@
     def again_step(given):
         smooth, scaled, beside, square = given
         again, again_lines = local_call(
-            functools.partial(again_body, slots), "again", [SM] + [VM] * 2, [slab, ((slots, LAT), F32)],
-        )(col_index, scaled, beside)
+            functools.partial(again_body, slots), "again", [hbm] + [VM] * 2, [slab, ((slots, LAT), F32)],
+            [pltpu.SMEM((slots,), jnp.int32), pltpu.SemaphoreType.DMA],
+        )(pltpu.with_memory_space_constraint(col_index, pltpu.MemorySpace.HBM), scaled, beside)
         return smooth, square, again, again_lines
 
     near, far, given = gather_rays(mine, 8, (lambda _: (), lambda _: columns, lambda given: again_step(smooth_step(given))))

time: 54.7 us -> 54.7 us (level)
  waiting for transfers between devices: 20 us -> 21.5 us
  local copies, waits for them, and re-layouts: 1 us -> 0.35 us
    ppermute x8, waiting for transfers between devices: 10.8 us -> 12 us  [gather_rays(): other = lax.ppermute(packet, 'ray', pairs_of(count, step))]
    unnamed x4 -> x2, local copies, waits for them, and re-layouts: 0.66 us -> 0.01 us
  transfers between devices with their start and end apart: 16 -> 16, of which waited for: 14 -> 14; matrix products, arithmetic and copies ran while one was open for 0% -> 0% of each run, Pallas kernels for 8% -> 7%
where the time goes in v9:
time: 54.7 us; the launch traced here: 54.6 us
  starting transfers between devices  23.7 us (43%)
  waiting for transfers between devices  21.5 us (39%)
  Pallas kernels  7.46 us (14%)
  between operations  1.45 us (3%)
    ppermute x8, starting transfers between devices, gather_rays(): other = lax.ppermute(packet, 'ray', pairs_of(count, step))  12.8 us
    ppermute x8, waiting for transfers between devices, gather_rays(): other = lax.ppermute(packet, 'ray', pairs_of(count, step))  12 us
    ppermute x2, starting transfers between devices, last_sums(): value = value + lax.ppermute(value, 'ray', pairs_of(count, step))  4.39 us
    ppermute x1, waiting for transfers between devices, next_halo(): other = lax.ppermute(sums, 'vox', [(0, 1), (1, 0)])  2.48 us
    ppermute x1, waiting for transfers between devices, first_halo(): other = lax.ppermute(sums, 'vox', [(0, 1), (1, 0)])  2.37 us
    ppermute x1, starting transfers between devices, last_sums(): lax.ppermute(both, ('ray', 'vox'), [(i, i ^ 7) for i in range(2 * count)])  2.3 us
    ppermute x1, starting transfers between devices, first_halo(): other = lax.ppermute(sums, 'vox', [(0, 1), (1, 0)])  2.28 us
    ppermute x2, waiting for transfers between devices, last_sums(): value = value + lax.ppermute(value, 'ray', pairs_of(count, step))  2.1 us
  transfers between devices with their start and end apart: 16, of which 14 were waited for; matrix products, arithmetic and copies ran while one was open for 0% of the time, Pallas kernels for 7%

profile of v9, /device:TPU:0, one launch (start us, length us, event | category | flops | bytes accessed | tf_op | source)
XLA Modules:
  0.0 54.6 jit_solution(17728482513990423649)
XLA Ops:
  1.3 1.6 %start.1 = (f32[40,128]{1,0:T(8,128)S(1)}, f32[8,128]{1,0:T(8,128)S(1)}, f32[8,128]{1,0:T(8,128)S(1)}, f32[32,8,128]{2,1,0:T(8,128)S(1)}, s32[32,128]{1,0:T(8,128)S(1)}, /*index=5*/bf16[32,128,128]{2,1,0:T(8,128)(2,1)S(1)}) custom-call(s32[1,1]{1,0:T(1,128)S(6)} %copy.11.count_ref, s32[32]{0:T(128)} %bitcast.13, s32[32]{0:T(128)} %bitcast.11, f32[32]{0:T(128)} %bitcast.14, ...), custom_call_target="tpu_custom_call" | custom-call | tf_op jit(solution)/shard_map/start/pallas_call | solution.py:572
  2.9 0.0 copy-start
  2.9 3.5 %collective-permute-start = (f32[40,128]{1,0:T(8,128)S(1)}, f32[40,128]{1,0:T(8,128)S(1)}, u32[]{:S(2)}, u32[]{:S(2)}) collective-permute-start(f32[40,128]{1,0:T(8,128)S(1)} %get-tuple-element.66), channel_id=1, source_target_pairs={{0,18},{2,16},{4,22},{6,20},{8,26},{10,24},{12,30},{14,28},{16,2},... | collective-permute-start | bytes 61448 | tf_op jit(solution)/shard_map/ppermute | solution.py:63
  6.4 0.1 broadcast_in_dim.10
  6.5 0.1 broadcast_in_dim.11
  6.6 1.3 %collective-permute-done = f32[40,128]{1,0:T(8,128)S(1)} collective-permute-done((f32[40,128]{1,0:T(8,128)S(1)}, f32[40,128]{1,0:T(8,128)S(1)}, u32[]{:S(2)}, u32[]{:S(2)}) %collective-permute-start) | collective-permute-done | bytes 20512 | tf_op jit(solution)/shard_map/ppermute | solution.py:63
  8.0 0.1 broadcast_in_dim.12.damp_ref
  8.0 1.9 %collective-permute-start.1 = (f32[72,128]{1,0:T(8,128)S(1)}, f32[72,128]{1,0:T(8,128)S(1)}, u32[]{:S(2)}, u32[]{:S(2)}) collective-permute-start(f32[72,128]{1,0:T(8,128)S(1)} %pad_maximum_fusion.4), channel_id=1, source_target_pairs={{0,10},{2,8},{4,14},{6,12},{8,2},{10,0},{12,6},{14,4},{16,26},{18,... | collective-permute-start | bytes 110600 | tf_op jit(solution)/shard_map/ppermute | solution.py:63
  9.9 0.3 turn.1.turned_ref
  10.3 1.3 %collective-permute-done.1 = f32[72,128]{1,0:T(8,128)S(1)} collective-permute-done((f32[72,128]{1,0:T(8,128)S(1)}, f32[72,128]{1,0:T(8,128)S(1)}, u32[]{:S(2)}, u32[]{:S(2)}) %collective-permute-start.1) | collective-permute-done | bytes 36896 | tf_op jit(solution)/shard_map/ppermute | solution.py:63
  11.6 1.8 %collective-permute-start.2 = (f32[136,128]{1,0:T(8,128)S(1)}, f32[136,128]{1,0:T(8,128)S(1)}, u32[]{:S(2)}, u32[]{:S(2)}) collective-permute-start(f32[136,128]{1,0:T(8,128)S(1)} %pad_maximum_fusion.2), channel_id=1, source_target_pairs={{0,6},{2,4},{4,2},{6,0},{8,14},{10,12},{12,10},{14,8},{16,22},{18,... | collective-permute-start | bytes 208904 | tf_op jit(solution)/shard_map/ppermute | solution.py:63
  13.4 2.3 %collective-permute-done.2 = f32[136,128]{1,0:T(8,128)S(1)} collective-permute-done((f32[136,128]{1,0:T(8,128)S(1)}, f32[136,128]{1,0:T(8,128)S(1)}, u32[]{:S(2)}, u32[]{:S(2)}) %collective-permute-start.2) | collective-permute-done | bytes 69664 | tf_op jit(solution)/shard_map/ppermute | solution.py:63
  15.7 0.3 collective-permute-start.3
  16.1 0.3 first_half.1
  16.4 0.8 %collective-permute-done.3.other_ref = f32[264,128]{1,0:T(8,128)S(1)} collective-permute-done((f32[264,128]{1,0:T(8,128)S(1)}, f32[264,128]{1,0:T(8,128)S(1)}, u32[]{:S(2)}, u32[]{:S(2)}) %collective-permute-start.3) | collective-permute-done | bytes 135200 | tf_op jit(solution)/shard_map/ppermute | solution.py:63
  17.1 0.6 %first.1 = (f32[132,8,128]{2,1,0:T(8,128)S(1)}, f32[32,128]{1,0:T(8,128)S(1)}, f32[144,128]{1,0:T(8,128)S(1)}, f32[8,128]{1,0:T(8,128)S(1)}, s32[2,128]{1,0:T(2,128)S(1)}) custom-call(f32[264,128]{1,0:T(8,128)S(1)} %collective-permute-done.3.other_ref, f32[128,8,128]{2,1,0:T(8,128)S(1)} %get-tuple-element.72.half_ref, ...), custom_call_target="tpu_custom_call" | custom-call | tf_op jit(solution)/shard_map/first/pallas_call | solution.py:590
  17.7 2.3 %collective-permute-start.4 = (f32[144,128]{1,0:T(8,128)S(1)}, f32[144,128]{1,0:T(8,128)S(1)}, u32[]{:S(2)}, u32[]{:S(2)}) collective-permute-start(f32[144,128]{1,0:T(8,128)S(1)} %get-tuple-element.76.mine_ref), channel_id=1, source_target_pairs={{0,1},{1,0},{2,3},{3,2},{4,5},{5,4},{6,7},{7,6},{8,9},{9,8},{10,11... | collective-permute-start | bytes 221192 | tf_op jit(solution)/shard_map/ppermute | solution.py:115
  20.0 0.2 onehot.1
  20.2 2.4 %collective-permute-done.4.other_ref = f32[144,128]{1,0:T(8,128)S(1)} collective-permute-done((f32[144,128]{1,0:T(8,128)S(1)}, f32[144,128]{1,0:T(8,128)S(1)}, u32[]{:S(2)}, u32[]{:S(2)}) %collective-permute-start.4) | collective-permute-done | bytes 73760 | tf_op jit(solution)/shard_map/ppermute | solution.py:115
  22.6 0.3 second.1
  22.8 1.6 %collective-permute-start.5 = (f32[40,128]{1,0:T(8,128)S(1)}, f32[40,128]{1,0:T(8,128)S(1)}, u32[]{:S(2)}, u32[]{:S(2)}) collective-permute-start(f32[40,128]{1,0:T(8,128)S(1)} %get-tuple-element.85), channel_id=1, source_target_pairs={{0,18},{2,16},{4,22},{6,20},{8,26},{10,24},{12,30},{14,28},{16,2},... | collective-permute-start | bytes 61448 | tf_op jit(solution)/shard_map/ppermute | solution.py:63
  24.4 2.6 %collective-permute-done.5 = f32[40,128]{1,0:T(8,128)S(1)} collective-permute-done((f32[40,128]{1,0:T(8,128)S(1)}, f32[40,128]{1,0:T(8,128)S(1)}, u32[]{:S(2)}, u32[]{:S(2)}) %collective-permute-start.5) | collective-permute-done | bytes 20512 | tf_op jit(solution)/shard_map/ppermute | solution.py:63
  27.0 2.1 %collective-permute-start.6 = (f32[72,128]{1,0:T(8,128)S(1)}, f32[72,128]{1,0:T(8,128)S(1)}, u32[]{:S(2)}, u32[]{:S(2)}) collective-permute-start(f32[72,128]{1,0:T(8,128)S(1)} %pad_maximum_fusion.5), channel_id=1, source_target_pairs={{0,10},{2,8},{4,14},{6,12},{8,2},{10,0},{12,6},{14,4},{16,26},{18,... | collective-permute-start | bytes 110600 | tf_op jit(solution)/shard_map/ppermute | solution.py:63
  29.1 0.0 collective-permute-start.7
  29.1 1.8 %collective-permute-done.6 = f32[72,128]{1,0:T(8,128)S(1)} collective-permute-done((f32[72,128]{1,0:T(8,128)S(1)}, f32[72,128]{1,0:T(8,128)S(1)}, u32[]{:S(2)}, u32[]{:S(2)}) %collective-permute-start.6) | collective-permute-done | bytes 36896 | tf_op jit(solution)/shard_map/ppermute | solution.py:63
  30.9 0.0 collective-permute-done.7.low2_ref.high2_ref
  30.9 1.3 %collective-permute-start.8 = (f32[136,128]{1,0:T(8,128)S(1)}, f32[136,128]{1,0:T(8,128)S(1)}, u32[]{:S(2)}, u32[]{:S(2)}) collective-permute-start(f32[136,128]{1,0:T(8,128)S(1)} %pad_maximum_fusion.3), channel_id=1, source_target_pairs={{0,6},{2,4},{4,2},{6,0},{8,14},{10,12},{12,10},{14,8},{16,22},{18,... | collective-permute-start | bytes 208904 | tf_op jit(solution)/shard_map/ppermute | solution.py:63
  32.2 0.9 %smooth.1 = (f32[128,8,128]{2,1,0:T(8,128)S(1)}, f32[132,8,128]{2,1,0:T(8,128)S(1)}, f32[2,128,128]{2,1,0:T(8,128)S(1)}, f32[8,128]{1,0:T(8,128)S(1)}) custom-call(f32[132,8,128]{2,1,0:T(8,128)S(1)} %get-tuple-element.87.field_ref.refs_6_, f32[128,128]{1,0:T(8,128)S(1)} %slice.124.low_ref.high_ref, f32[128,128]{1,0:T(8,128)S(1)} %collective-permute-done.7.low2_ref.high2_ref, ...), custom_call_target="tpu_custom_call" | custom-call | tf_op jit(solution)/shard_map/smooth/pallas_call | solution.py:604
  33.1 0.9 %again.1 = (f32[128,8,128]{2,1,0:T(8,128)S(1)}, f32[32,128]{1,0:T(8,128)S(1)}) custom-call(s32[32]{0:T(128)} %bitcast.12, f32[132,8,128]{2,1,0:T(8,128)S(1)} %get-tuple-element.96.scaled_ref, f32[2,128,128]{2,1,0:T(8,128)S(1)} %get-tuple-element.97.far_ref), custom_call_target="tpu_custom_call" | custom-call | tf_op jit(solution)/shard_map/again/pallas_call | solution.py:611
  34.0 1.2 %collective-permute-done.8 = f32[136,128]{1,0:T(8,128)S(1)} collective-permute-done((f32[136,128]{1,0:T(8,128)S(1)}, f32[136,128]{1,0:T(8,128)S(1)}, u32[]{:S(2)}, u32[]{:S(2)}) %collective-permute-start.8) | collective-permute-done | bytes 69664 | tf_op jit(solution)/shard_map/ppermute | solution.py:63
  35.2 0.2 collective-permute-start.9
  35.4 0.3 third_half.1
  35.7 0.9 %collective-permute-done.9.other_ref = f32[264,128]{1,0:T(8,128)S(1)} collective-permute-done((f32[264,128]{1,0:T(8,128)S(1)}, f32[264,128]{1,0:T(8,128)S(1)}, u32[]{:S(2)}, u32[]{:S(2)}) %collective-permute-start.9) | collective-permute-done | bytes 135200 | tf_op jit(solution)/shard_map/ppermute | solution.py:63
  36.6 0.6 %third.1 = (f32[132,8,128]{2,1,0:T(8,128)S(1)}, f32[80,128]{1,0:T(8,128)S(1)}, f32[8,128]{1,0:T(8,128)S(1)}) custom-call(f32[264,128]{1,0:T(8,128)S(1)} %collective-permute-done.9.other_ref, f32[128,8,128]{2,1,0:T(8,128)S(1)} %get-tuple-element.104.half_ref, f32[32,128]{1,0:T(8,128)S(1)} %get-tuple-element.105.half_lines_ref, ...), custom_call_target="tpu_custom_call" | custom-call | tf_op jit(solution)/shard_map/third/pallas_call | solution.py:623
  37.2 1.6 %collective-permute-start.10 = (f32[80,128]{1,0:T(8,128)S(1)}, f32[80,128]{1,0:T(8,128)S(1)}, u32[]{:S(2)}, u32[]{:S(2)}) collective-permute-start(f32[80,128]{1,0:T(8,128)S(1)} %get-tuple-element.109.mine_ref), channel_id=1, source_target_pairs={{0,1},{1,0},{2,3},{3,2},{4,5},{5,4},{6,7},{7,6},{8,9},{9,8},{10,11... | collective-permute-start | bytes 122888 | tf_op jit(solution)/shard_map/ppermute | solution.py:126
  38.8 2.5 %collective-permute-done.10.other_ref = f32[80,128]{1,0:T(8,128)S(1)} collective-permute-done((f32[80,128]{1,0:T(8,128)S(1)}, f32[80,128]{1,0:T(8,128)S(1)}, u32[]{:S(2)}, u32[]{:S(2)}) %collective-permute-start.10) | collective-permute-done | bytes 40992 | tf_op jit(solution)/shard_map/ppermute | solution.py:126
  41.3 0.1 fourth.1
  41.4 2.4 %collective-permute-start.11 = (f32[8,128]{1,0:T(8,128)S(1)}, f32[8,128]{1,0:T(8,128)S(1)}, u32[]{:S(2)}, u32[]{:S(2)}) collective-permute-start(f32[8,128]{1,0:T(8,128)S(1)} %get-tuple-element.113), channel_id=1, source_target_pairs={{0,18},{2,16},{4,22},{6,20},{8,26},{10,24},{12,30},{14,28},{16,2},... | collective-permute-start | bytes 12296 | tf_op jit(solution)/shard_map/ppermute | solution.py:93
  43.9 1.6 %collective-permute-done.11 = f32[8,128]{1,0:T(8,128)S(1)} collective-permute-done((f32[8,128]{1,0:T(8,128)S(1)}, f32[8,128]{1,0:T(8,128)S(1)}, u32[]{:S(2)}, u32[]{:S(2)}) %collective-permute-start.11) | collective-permute-done | bytes 4128 | tf_op jit(solution)/shard_map/ppermute | solution.py:93
  45.4 0.0 collective-permute-done.12.high_ref
  45.4 2.0 %collective-permute-start.13 = (f32[8,128]{1,0:T(8,128)S(1)}, f32[8,128]{1,0:T(8,128)S(1)}, u32[]{:S(2)}, u32[]{:S(2)}) collective-permute-start(f32[8,128]{1,0:T(8,128)S(1)} %add.33), channel_id=1, source_target_pairs={{0,10},{2,8},{4,14},{6,12},{8,2},{10,0},{12,6},{14,4},{16,26},{18,... | collective-permute-start | bytes 12296 | tf_op jit(solution)/shard_map/ppermute | solution.py:93
  47.4 0.8 %last_smooth.1 = (f32[8,128]{1,0:T(8,128)S(1)}, f32[4,8,128]{2,1,0:T(8,128)S(1)}) custom-call(f32[132,8,128]{2,1,0:T(8,128)S(1)} %get-tuple-element.115.next_ref.refs_7_, f32[64,128]{1,0:T(8,128)S(1)} %slice.127.low_ref, f32[64,128]{1,0:T(8,128)S(1)} %collective-permute-done.12.high_ref, f32[128,128]{1,0:T(8,128)S(1)} %broadcast_in_dim.12.damp_ref, ...), custom_call_target="tpu_custom_call" | custom-call | tf_op jit(solution)/shard_map/last_smooth/pallas_call | solution.py:633
  48.2 0.5 collective-permute-done.13
  48.7 2.3 %collective-permute-start.14 = (f32[16,128]{1,0:T(8,128)S(1)}, f32[16,128]{1,0:T(8,128)S(1)}, u32[]{:S(2)}, u32[]{:S(2)}) collective-permute-start(f32[16,128]{1,0:T(8,128)S(1)} %pad_maximum_fusion.6), channel_id=1, source_target_pairs={{0,7},{1,6},{2,5},{3,4},{4,3},{5,2},{6,1},{7,0},{8,15},{9,14},{10,... | collective-permute-start | bytes 24584 | tf_op jit(solution)/shard_map/ppermute | solution.py:99
  51.0 1.7 %collective-permute-done.14 = f32[16,128]{1,0:T(8,128)S(1)} collective-permute-done((f32[16,128]{1,0:T(8,128)S(1)}, f32[16,128]{1,0:T(8,128)S(1)}, u32[]{:S(2)}, u32[]{:S(2)}) %collective-permute-start.14) | collective-permute-done | bytes 8224 | tf_op jit(solution)/shard_map/ppermute | solution.py:99
  52.8 0.4 collective-permute-start.15
  53.1 0.8 %collective-permute-done.15.refs_1_ = f32[8,128]{1,0:T(8,128)S(1)} collective-permute-done((f32[8,128]{1,0:T(8,128)S(1)}, f32[8,128]{1,0:T(8,128)S(1)}, u32[]{:S(2)}, u32[]{:S(2)}) %collective-permute-start.15) | collective-permute-done | bytes 4128 | tf_op jit(solution)/shard_map/ppermute | solution.py:101
  53.9 0.6 %end.1 = (f32[8,8,128]{2,1,0:T(8,128)}, f32[8,128]{1,0:T(8,128)}) custom-call(f32[8,128]{1,0:T(8,128)S(1)} %get-tuple-element.131.refs_0_, f32[8,128]{1,0:T(8,128)S(1)} %collective-permute-done.15.refs_1_, f32[8,128]{1,0:T(8,128)S(1)} %get-tuple-element.125.refs_2_, f32[8,128]{1,0:T(8,128)S(1)} %get-tuple-element.130.refs_3_, ...), custom_call_target="tpu_custom_call" | custom-call | tf_op jit(solution)/shard_map/end/pallas_call | solution.py:641
  (32 shorter events, 0.1 us)
Async XLA Ops:
  2.9 3.6 %copy-start = (f32[64]{0:T(128)S(1)}, f32[64]{0:T(128)}, u32[]{:S(2)}) copy-start(f32[64]{0:T(128)} %param.17) | copy-start | bytes 772
  2.9 5.1 %collective-permute-start = (f32[40,128]{1,0:T(8,128)S(1)}, f32[40,128]{1,0:T(8,128)S(1)}, u32[]{:S(2)}, u32[]{:S(2)}) collective-permute-start(f32[40,128]{1,0:T(8,128)S(1)} %get-tuple-element.66), channel_id=1, source_target_pairs={{0,18},{2,16},{4,22},{6,20},{8,26},{10,24},{12,30},{14,28},{16,2},... | collective-permute-start | bytes 61448 | tf_op jit(solution)/shard_map/ppermute | solution.py:63
  8.0 3.5 %collective-permute-start.1 = (f32[72,128]{1,0:T(8,128)S(1)}, f32[72,128]{1,0:T(8,128)S(1)}, u32[]{:S(2)}, u32[]{:S(2)}) collective-permute-start(f32[72,128]{1,0:T(8,128)S(1)} %pad_maximum_fusion.4), channel_id=1, source_target_pairs={{0,10},{2,8},{4,14},{6,12},{8,2},{10,0},{12,6},{14,4},{16,26},{18,... | collective-permute-start | bytes 110600 | tf_op jit(solution)/shard_map/ppermute | solution.py:63
  11.6 4.1 %collective-permute-start.2 = (f32[136,128]{1,0:T(8,128)S(1)}, f32[136,128]{1,0:T(8,128)S(1)}, u32[]{:S(2)}, u32[]{:S(2)}) collective-permute-start(f32[136,128]{1,0:T(8,128)S(1)} %pad_maximum_fusion.2), channel_id=1, source_target_pairs={{0,6},{2,4},{4,2},{6,0},{8,14},{10,12},{12,10},{14,8},{16,22},{18,... | collective-permute-start | bytes 208904 | tf_op jit(solution)/shard_map/ppermute | solution.py:63
  15.7 1.4 %collective-permute-start.3 = (f32[264,128]{1,0:T(8,128)S(1)}, f32[264,128]{1,0:T(8,128)S(1)}, u32[]{:S(2)}, u32[]{:S(2)}) collective-permute-start(f32[264,128]{1,0:T(8,128)S(1)} %pad_maximum_fusion.mine_ref), channel_id=1, source_target_pairs={{0,2},{2,0},{4,6},{6,4},{8,10},{10,8},{12,14},{14,12},{16,18},{18,... | collective-permute-start | bytes 405512 | tf_op jit(solution)/shard_map/ppermute | solution.py:63
  17.7 4.9 %collective-permute-start.4 = (f32[144,128]{1,0:T(8,128)S(1)}, f32[144,128]{1,0:T(8,128)S(1)}, u32[]{:S(2)}, u32[]{:S(2)}) collective-permute-start(f32[144,128]{1,0:T(8,128)S(1)} %get-tuple-element.76.mine_ref), channel_id=1, source_target_pairs={{0,1},{1,0},{2,3},{3,2},{4,5},{5,4},{6,7},{7,6},{8,9},{9,8},{10,11... | collective-permute-start | bytes 221192 | tf_op jit(solution)/shard_map/ppermute | solution.py:115
  22.8 4.2 %collective-permute-start.5 = (f32[40,128]{1,0:T(8,128)S(1)}, f32[40,128]{1,0:T(8,128)S(1)}, u32[]{:S(2)}, u32[]{:S(2)}) collective-permute-start(f32[40,128]{1,0:T(8,128)S(1)} %get-tuple-element.85), channel_id=1, source_target_pairs={{0,18},{2,16},{4,22},{6,20},{8,26},{10,24},{12,30},{14,28},{16,2},... | collective-permute-start | bytes 61448 | tf_op jit(solution)/shard_map/ppermute | solution.py:63
  27.0 3.9 %collective-permute-start.6 = (f32[72,128]{1,0:T(8,128)S(1)}, f32[72,128]{1,0:T(8,128)S(1)}, u32[]{:S(2)}, u32[]{:S(2)}) collective-permute-start(f32[72,128]{1,0:T(8,128)S(1)} %pad_maximum_fusion.5), channel_id=1, source_target_pairs={{0,10},{2,8},{4,14},{6,12},{8,2},{10,0},{12,6},{14,4},{16,26},{18,... | collective-permute-start | bytes 110600 | tf_op jit(solution)/shard_map/ppermute | solution.py:63
  29.1 1.8 %collective-permute-start.7 = (f32[128,128]{1,0:T(8,128)S(1)}, f32[128,128]{1,0:T(8,128)S(1)}, u32[]{:S(2)}, u32[]{:S(2)}) collective-permute-start(f32[128,128]{1,0:T(8,128)S(1)} %slice.124.low_ref.high_ref), channel_id=1, source_target_pairs={{0,2},{2,0},{4,6},{6,4},{8,10},{10,8},{12,14},{14,12},{16,18},{18,... | collective-permute-start | bytes 196616 | tf_op jit(solution)/shard_map/ppermute | solution.py:117
  30.9 4.2 %collective-permute-start.8 = (f32[136,128]{1,0:T(8,128)S(1)}, f32[136,128]{1,0:T(8,128)S(1)}, u32[]{:S(2)}, u32[]{:S(2)}) collective-permute-start(f32[136,128]{1,0:T(8,128)S(1)} %pad_maximum_fusion.3), channel_id=1, source_target_pairs={{0,6},{2,4},{4,2},{6,0},{8,14},{10,12},{12,10},{14,8},{16,22},{18,... | collective-permute-start | bytes 208904 | tf_op jit(solution)/shard_map/ppermute | solution.py:63
  35.2 1.4 %collective-permute-start.9 = (f32[264,128]{1,0:T(8,128)S(1)}, f32[264,128]{1,0:T(8,128)S(1)}, u32[]{:S(2)}, u32[]{:S(2)}) collective-permute-start(f32[264,128]{1,0:T(8,128)S(1)} %pad_maximum_fusion.1.mine_ref), channel_id=1, source_target_pairs={{0,2},{2,0},{4,6},{6,4},{8,10},{10,8},{12,14},{14,12},{16,18},{18,... | collective-permute-start | bytes 405512 | tf_op jit(solution)/shard_map/ppermute | solution.py:63
  37.2 4.1 %collective-permute-start.10 = (f32[80,128]{1,0:T(8,128)S(1)}, f32[80,128]{1,0:T(8,128)S(1)}, u32[]{:S(2)}, u32[]{:S(2)}) collective-permute-start(f32[80,128]{1,0:T(8,128)S(1)} %get-tuple-element.109.mine_ref), channel_id=1, source_target_pairs={{0,1},{1,0},{2,3},{3,2},{4,5},{5,4},{6,7},{7,6},{8,9},{9,8},{10,11... | collective-permute-start | bytes 122888 | tf_op jit(solution)/shard_map/ppermute | solution.py:126
  41.3 4.2 %collective-permute-start.12 = (f32[64,128]{1,0:T(8,128)S(1)}, f32[64,128]{1,0:T(8,128)S(1)}, u32[]{:S(2)}, u32[]{:S(2)}) collective-permute-start(f32[64,128]{1,0:T(8,128)S(1)} %slice.127.low_ref), channel_id=1, source_target_pairs={{0,2},{2,0},{4,6},{6,4},{8,10},{10,8},{12,14},{14,12},{16,18},{18,... | collective-permute-start | bytes 98312 | tf_op jit(solution)/shard_map/ppermute | solution.py:128
  41.4 4.0 %collective-permute-start.11 = (f32[8,128]{1,0:T(8,128)S(1)}, f32[8,128]{1,0:T(8,128)S(1)}, u32[]{:S(2)}, u32[]{:S(2)}) collective-permute-start(f32[8,128]{1,0:T(8,128)S(1)} %get-tuple-element.113), channel_id=1, source_target_pairs={{0,18},{2,16},{4,22},{6,20},{8,26},{10,24},{12,30},{14,28},{16,2},... | collective-permute-start | bytes 12296 | tf_op jit(solution)/shard_map/ppermute | solution.py:93
  45.4 3.3 %collective-permute-start.13 = (f32[8,128]{1,0:T(8,128)S(1)}, f32[8,128]{1,0:T(8,128)S(1)}, u32[]{:S(2)}, u32[]{:S(2)}) collective-permute-start(f32[8,128]{1,0:T(8,128)S(1)} %add.33), channel_id=1, source_target_pairs={{0,10},{2,8},{4,14},{6,12},{8,2},{10,0},{12,6},{14,4},{16,26},{18,... | collective-permute-start | bytes 12296 | tf_op jit(solution)/shard_map/ppermute | solution.py:93
  48.7 4.0 %collective-permute-start.14 = (f32[16,128]{1,0:T(8,128)S(1)}, f32[16,128]{1,0:T(8,128)S(1)}, u32[]{:S(2)}, u32[]{:S(2)}) collective-permute-start(f32[16,128]{1,0:T(8,128)S(1)} %pad_maximum_fusion.6), channel_id=1, source_target_pairs={{0,7},{1,6},{2,5},{3,4},{4,3},{5,2},{6,1},{7,0},{8,15},{9,14},{10,... | collective-permute-start | bytes 24584 | tf_op jit(solution)/shard_map/ppermute | solution.py:99
  52.8 1.2 %collective-permute-start.15 = (f32[8,128]{1,0:T(8,128)S(1)}, f32[8,128]{1,0:T(8,128)S(1)}, u32[]{:S(2)}, u32[]{:S(2)}) collective-permute-start(f32[8,128]{1,0:T(8,128)S(1)} %get-tuple-element.131.refs_0_), channel_id=1, source_target_pairs={{0,2},{2,0},{4,6},{6,4},{8,10},{10,8},{12,14},{14,12},{16,18},{18,... | collective-permute-start | bytes 12296 | tf_op jit(solution)/shard_map/ppermute | solution.py:101
